TPU v7x, 32 devices: a whole 2x2x4 slice. The times are simulated.
32 devices in a mesh: dp: 8 (over y, x, core), fsdp: 4 (over z).
Axes of the slice: x: 2, y: 2, z: 4, core: 2. Of those that a mesh axis runs over, the one named last changes fastest.
Arguments:
- tokens: bfloat16 [32768, 768], P(('dp', 'fsdp')), may hold values from -6 to 6
- cotangent: bfloat16 [32768, 768], P(('dp', 'fsdp')), may hold values from -6 to 6
- doc_lengths: int32 [64, 4], P(('dp', 'fsdp')), may hold values from 1 to 288, 512 in all within a row
- query_ids: int32 [256, 1], P(('dp', 'fsdp')), may hold values from 0 to 63
- qkv_weight: bfloat16 [768, 2304], P(('dp', 'fsdp')), may hold values from -0.21875 to 0.21875
- query_bias: bfloat16 [768], P(('dp', 'fsdp')), may hold values from -3 to 3
- value_bias: bfloat16 [768], P(('dp', 'fsdp')), may hold values from -3 to 3
- attn_weight: bfloat16 [768, 768], P(('dp', 'fsdp')), may hold values from -0.875 to 0.875
- attn_bias: bfloat16 [768], P(('dp', 'fsdp')), may hold values from -2 to 2
- first_gain: bfloat16 [768], P(('dp', 'fsdp')), may hold values from 0.5 to 1.5
- first_shift: bfloat16 [768], P(('dp', 'fsdp')), may hold values from -2 to 2
- inner_weight: bfloat16 [768, 3072], P(('dp', 'fsdp')), may hold values from -0.21875 to 0.21875
- inner_bias: bfloat16 [3072], P(('dp', 'fsdp')), may hold values from -3 to 3
- outer_weight: bfloat16 [3072, 768], P(('dp', 'fsdp')), may hold values from -0.21875 to 0.21875
- outer_bias: bfloat16 [768], P(('dp', 'fsdp')), may hold values from -2 to 2
- second_gain: bfloat16 [768], P(('dp', 'fsdp')), may hold values from 0.5 to 1.5
- second_shift: bfloat16 [768], P(('dp', 'fsdp')), may hold values from -2 to 2
- span_weight: bfloat16 [768, 128], P(('dp', 'fsdp')), may hold values from -0.21875 to 0.21875
- answer_vector: bfloat16 [128], P(('dp', 'fsdp')), may hold values from -1 to 1
Outputs:
- log_likelihood: float32 [], replicated
- layer_output: bfloat16 [32768, 768], P(('dp', 'fsdp'))
- input_grad: float32 [32768, 768], P(('dp', 'fsdp'))
- qkv_weight_grad: float32 [768, 2304], P(('dp', 'fsdp'))
- query_bias_grad: float32 [768], P(('dp', 'fsdp'))
- value_bias_grad: float32 [768], P(('dp', 'fsdp'))
- attn_weight_grad: float32 [768, 768], P(('dp', 'fsdp'))
- attn_bias_grad: float32 [768], P(('dp', 'fsdp'))
- first_gain_grad: float32 [768], P(('dp', 'fsdp'))
- first_shift_grad: float32 [768], P(('dp', 'fsdp'))
- inner_weight_grad: float32 [768, 3072], P(('dp', 'fsdp'))
- inner_bias_grad: float32 [3072], P(('dp', 'fsdp'))
- outer_weight_grad: float32 [3072, 768], P(('dp', 'fsdp'))
- outer_bias_grad: float32 [768], P(('dp', 'fsdp'))
- second_gain_grad: float32 [768], P(('dp', 'fsdp'))
- second_shift_grad: float32 [768], P(('dp', 'fsdp'))
- span_weight_grad: float32 [768, 128], P(('dp', 'fsdp'))
- answer_vector_grad: float32 [128], P(('dp', 'fsdp'))
Inputs may be any that keep to these rules, and one draw needn't show every extreme that they name: `doc_lengths`: the 4 lengths of a pack sum to 512, and in every pack one of them is 288. `query_ids`: every query has one segment or more.
All inputs are finite; a program needn't handle non-finite values.
Results may differ from a plain program's by a relative error of at most 0.014.
Values may be sent and summed in bfloat16 or wider, within the bound.
No kernel may reach another device: no remote copies, remote signals or barrier semaphores. Data moves between devices by JAX's collectives and lax.ppermute only.
A program may use at most 192 MiB of HBM per device.

v0:
```python
import functools, math
import jax, jax.numpy as jnp
from jax import lax
from jax.experimental import pallas as pl
from jax.experimental.pallas import tpu as pltpu
from jax.sharding import PartitionSpec as P
PACK=512; SEGS_PACK=4; HEADS=12; HEAD_DIM=64; LANES=128; SUBLANES=8
MASKED=-1e30
VMEM_MOST=60*1024*1024
F32=jnp.float32; BF16=jnp.bfloat16
def swap(block, axis, mask):
    size = lax.axis_size(axis)
    return lax.ppermute(block, axis, [(i, i ^ mask) for i in range(size)])


def bit_orders(dp):
    bits = [1 << t for t in range(dp.bit_length() - 1)]
    first, others = bits[:1], bits[1:]
    return first + others, first + others[1:] + others[:1]


def offsets(order):
    found = [0]
    for bit in reversed(order):
        found = found + [f | bit for f in found]
    return found


def gather_near(shard):
    if shard.shape[0] % SUBLANES:
        return [lax.all_gather(shard, "fsdp", axis=0, tiled=True)]
    return [shard] + [swap(shard, "fsdp", k) for k in range(1, lax.axis_size("fsdp"))]


class Gathering:
    def __init__(self, pieces, orders, split):
        self.orders = orders
        self.near = len(pieces)
        self.left = len(orders[0]) - 1
        cut = [[p[:, :split] for p in pieces], [p[:, split:] for p in pieces]]
        self.blocks = [jnp.stack(c) for c in cut]
        self.came = None

    def send(self):
        self.came = [swap(b, "dp", o[self.left]) for b, o in zip(self.blocks, self.orders)]

    def join(self):
        self.blocks = [jnp.concatenate([b, c], axis=0) for b, c in zip(self.blocks, self.came)]
        self.left -= 1

    def advance(self, left):
        while self.left > left:
            self.send()
            self.join()

    def parts(self):
        return [self.blocks[0], self.came[0], self.blocks[1], self.came[1]]


def part(block, dim, which):
    return lax.dynamic_index_in_dim(block, which, dim, keepdims=False)


def add_low(a, b):
    return (a.astype(F32) + b.astype(F32)).astype(BF16)


class Reduction:
    def __init__(self, keep, give, order):
        self.order = list(order)
        self.bits = sorted(order, reverse=True)
        self.keep, self.give = keep, give
        self.came = None

    def send(self):
        self.came = swap(self.give, "dp", self.order[0])

    def add(self):
        total = add_low(self.keep, self.came)
        self.bits.remove(self.order.pop(0))
        if not self.order:
            self.keep = total
            return
        total = total.reshape((2,) * len(self.bits) + total.shape[-2:])
        dim = self.bits.index(self.order[0])
        own = (lax.axis_index("dp") // self.order[0]) % 2
        flat = lambda x: x.reshape((-1,) + x.shape[-2:])
        self.keep, self.give = flat(part(total, dim, own)), flat(part(total, dim, 1 - own))

    def advance(self, left):
        while len(self.order) > left:
            self.send()
            self.add()


def start_near(blocks):
    fsdp = lax.axis_size("fsdp")
    split = [b.reshape(fsdp, -1, b.shape[-1]) for b in blocks]
    own = lax.axis_index("fsdp")
    take = lambda k: jnp.concatenate([part(b, 0, own ^ k) for b in split], axis=1)
    return take(0), [swap(take(k), "fsdp", k) for k in range(1, fsdp)]


def add_near(own, came):
    total = own.astype(F32)
    for block in came:
        total = total + block.astype(F32)
    return total


def tie(*groups):
    return lax.optimization_barrier(groups)


def once(shape):
    return pl.BlockSpec(shape,lambda i:(0,)*len(shape),pipeline_mode=pl.Buffered(1))

def dot_nn(a,b): return jnp.dot(a,b,preferred_element_type=F32)
def dot_nt(a,b): return lax.dot_general(a,b,(((1,),(1,)),((),())),preferred_element_type=F32)
def dot_tn(a,b): return lax.dot_general(a,b,(((0,),(0,)),((),())),preferred_element_type=F32)

def segment_tiles(lens_ref, g):
    row=lax.broadcasted_iota(jnp.int32,(PACK,LANES),0)
    lane=lax.broadcasted_iota(jnp.int32,(PACK,LANES),1)
    seg=jnp.zeros((PACK,LANES),jnp.int32); bound=jnp.int32(0)
    for j in range(SEGS_PACK):
        bound=bound+lens_ref[g,j]
        seg=seg+(row>=bound).astype(jnp.int32)
    place=lane-48
    inside=jnp.logical_and(place>=0,place<SEGS_PACK)
    same=place==seg
    apart=jnp.where(jnp.logical_and(inside,jnp.logical_not(same)),MASKED,0.0)
    own=jnp.where(same,1.0,0.0)
    return lane,apart,own

def head_lanes(lane,h):
    return jnp.logical_and(lane<48,lane%16==h)

def assemble(me_ref, orders, fsdp, parts, full_ref, sems):
    copies, start = [], 0
    for color, order in enumerate(orders):
        cols = parts[2 * color].shape[2]
        for half in range(2):
            src = parts[2 * color + half]
            near = offsets(order)[half * src.shape[0] // fsdp :]
            for n in range(src.shape[0]):
                block = (near[n // fsdp] ^ me_ref[0]) * fsdp
                block += (n % fsdp) ^ me_ref[1] if fsdp > 1 else 0
                place = pl.ds(pl.multiple_of(block * src.shape[1], SUBLANES), src.shape[1])
                copies.append(
                    pltpu.make_async_copy(
                        src.at[n], full_ref.at[place, pl.ds(start, cols)], sems.at[len(copies)]
                    )
                )
        start += cols
    for copy in copies:
        copy.start()
    for copy in copies:
        copy.wait()


def whole_div(x, n):
    return jnp.floor((x.astype(F32) + 0.5) * (1.0 / n)).astype(jnp.int32)


def unpack_small(block, share, rows_in, answers):
    width = block.shape[0]
    count = -(-(rows_in * share + answers) // LANES)
    row = lax.broadcasted_iota(jnp.int32, (width, LANES), 0)
    lane = lax.broadcasted_iota(jnp.int32, (width, LANES), 1)
    turned = jnp.concatenate(
        [dot_tn(block, (row == lane * share + k).astype(BF16)) for k in range(count)], axis=0
    ).astype(BF16)
    entry = lax.broadcasted_iota(jnp.int32, (count * LANES, width), 0)
    place = lax.broadcasted_iota(jnp.int32, (count * LANES, width), 1)
    owner = whole_div(lax.broadcasted_iota(jnp.int32, (LANES, width), 1), share)
    owns = (lax.broadcasted_iota(jnp.int32, (LANES, width), 0) == owner).astype(BF16)
    spread = dot_nn(turned, owns)
    fits = entry - whole_div(entry, share) * share == place - whole_div(place, share) * share
    spread = jnp.where(fits, spread, 0.0).astype(BF16)
    vector = lax.broadcasted_iota(jnp.int32, (16, count * LANES), 0)
    source = whole_div(lax.broadcasted_iota(jnp.int32, (16, count * LANES), 1), share)
    vectors = dot_nn((vector == source).astype(BF16), spread)
    line = lax.broadcasted_iota(jnp.int32, (LANES, LANES), 1)
    owns = (lax.broadcasted_iota(jnp.int32, (LANES, LANES), 0) == whole_div(line, answers)).astype(BF16)
    spread = dot_nn(turned, owns)
    entry = lax.broadcasted_iota(jnp.int32, spread.shape, 0) - rows_in * share
    place = lax.broadcasted_iota(jnp.int32, spread.shape, 1)
    fits = entry == place - whole_div(place, answers) * answers
    return vectors, jnp.sum(jnp.where(fits, spread, 0.0), axis=0, keepdims=True)


def attention_kernel(orders,fsdp,small,lens_ref,me_ref,tok_ref,p0,p1,p2,p3,w_ref,vec_ref,mix_ref,ctx_ref,lse_ref,acc_ref,sems):
    pack=pl.program_id(0)
    width=tok_ref.shape[1]; wide=3*width
    @pl.when(pack==0)
    def _():
        assemble(me_ref,orders,fsdp,(p0,p1,p2,p3),w_ref,sems)
        vectors,answer=unpack_small(w_ref[:,wide:],*small)
        vec_ref[...]=vectors
        vec_ref[15:16,:LANES]=answer
    query_row=vec_ref[6:7,:]; value_row=vec_ref[7:8,:]
    lane,apart,own=segment_tiles(lens_ref,pack)
    apart=apart.astype(BF16); own=own.astype(BF16)
    tok=tok_ref[...]
    mix_ref[:,:width]=((dot_nn(tok,w_ref[:,:width])+query_row).astype(BF16).astype(F32)*(1/math.sqrt(HEAD_DIM))).astype(BF16)
    mix_ref[:,width:2*width]=dot_nn(tok,w_ref[:,width:2*width]).astype(BF16)
    mix_ref[:,2*width:]=(dot_nn(tok,w_ref[:,2*width:wide])+value_row).astype(BF16)
    acc_ref[...]=jnp.zeros_like(acc_ref)
    ones=jnp.ones((PACK,LANES),BF16)
    def pair(p,carry):
        at=lambda base: pl.ds(pl.multiple_of(base+p*LANES,LANES),LANES)
        q2=mix_ref[:,at(0)]; k2=mix_ref[:,at(width)]; v2=mix_ref[:,at(2*width)]
        kx=jnp.concatenate([k2,own],axis=1)
        vx=jnp.concatenate([v2,ones],axis=1)
        outs=[]
        for half in range(2):
            qm=jnp.where(lane//HEAD_DIM==half,q2,jnp.zeros_like(q2))
            s=dot_nt(jnp.concatenate([qm,apart],axis=1),kx)
            m=jnp.max(s,axis=1,keepdims=True)
            w=jnp.exp(s-m).astype(BF16)
            o=dot_nn(w,vx)
            total=o[:,LANES:]
            outs.append(o[:,:LANES]/total)
            acc_ref[...]=jnp.where(head_lanes(lane,2*p+half),m+jnp.log(total),acc_ref[...])
        ctx_ref[:,at(0)]=jnp.where(lane<HEAD_DIM,outs[0],outs[1]).astype(BF16)
        return carry
    lax.fori_loop(0,HEADS//2,pair,0)
    lse_ref[...]=acc_ref[...]

def attention(lens,me,tok,parts,orders,fsdp,small):
    rows,width=tok.shape; share=parts[0].shape[1]; full=parts[0].shape[2]+parts[2].shape[2]
    hbm=pl.BlockSpec(memory_space=pl.ANY)
    sm=pl.BlockSpec(memory_space=pltpu.SMEM)
    wide=3*width
    sizes=((wide,BF16),(width,BF16),(LANES,F32))
    outs=[jax.ShapeDtypeStruct((rows,n),t) for n,t in sizes]
    heads=[jax.ShapeDtypeStruct((width,full),BF16),jax.ShapeDtypeStruct((16,width),F32)]
    fixed=[once((width,full)),once((16,width))]
    cost=pl.CostEstimate(flops=2*rows*width*wide+8*rows*PACK*width,bytes_accessed=rows*wide*4,transcendentals=HEADS*PACK*rows)
    spec=lambda n: pl.BlockSpec((PACK,n),lambda g:(g,0))
    return pl.pallas_call(functools.partial(attention_kernel,orders,fsdp,small),grid=(rows//PACK,),
        in_specs=[sm,sm,spec(width)]+[hbm]*4,out_specs=fixed+[spec(n) for n,_ in sizes],out_shape=heads+outs,
        scratch_shapes=[pltpu.VMEM((PACK,LANES),F32),pltpu.SemaphoreType.DMA((4*parts[0].shape[0],))],
        compiler_params=pltpu.CompilerParams(vmem_limit_bytes=VMEM_MOST),name='attention',cost_estimate=cost)(lens,me,tok,*parts)

def split_three(x,lane):
    hi=x.astype(BF16).astype(F32)
    rest=x-hi
    mid=rest.astype(BF16).astype(F32)
    return jnp.where(lane<16,hi,jnp.where(lane<32,mid,jnp.where(lane<48,rest-mid,0.0)))

def attention_grad_kernel(pairs,lens_ref,mix_ref,ctx_ref,dctx_ref,lse_ref,out_ref):
    g=pl.program_id(0)
    width=ctx_ref.shape[1]
    part=(pairs[1]-pairs[0])*LANES
    lane,apart,own=segment_tiles(lens_ref,g)
    prod=dctx_ref[...].astype(F32)*ctx_ref[...].astype(F32)
    hi=prod.astype(BF16); lo=(prod-hi.astype(F32)).astype(BF16)
    wr=lax.broadcasted_iota(jnp.int32,(width,LANES),0); wl=lax.broadcasted_iota(jnp.int32,(width,LANES),1)
    pick=jnp.where(jnp.logical_and(wl<48,wl%16==wr//HEAD_DIM),1.0,0.0).astype(BF16)
    dots=dot_nn(hi,pick)+dot_nn(lo,pick)
    qe=(apart-split_three(lse_ref[...],lane)).astype(BF16)
    de=(-split_three(dots,lane)).astype(BF16)
    def pair(p,carry):
        at=lambda base: pl.ds(pl.multiple_of(base+p*LANES,LANES),LANES)
        q2=mix_ref[:,at(0)]; k2=mix_ref[:,at(width)]; v2=mix_ref[:,at(2*width)]; d2=dctx_ref[:,at(0)]
        kt=k2.T
        dk=jnp.zeros((PACK,LANES),F32); dv=jnp.zeros((PACK,LANES),F32); dqs=[]
        for half in range(2):
            here=lane//HEAD_DIM==half
            qm=jnp.where(here,q2,jnp.zeros_like(q2)); dm=jnp.where(here,d2,jnp.zeros_like(d2))
            mark=jnp.where(head_lanes(lane,2*p+half),1.0,0.0)
            kx=jnp.concatenate([k2,(own+mark).astype(BF16)],axis=1)
            vx=jnp.concatenate([v2,mark.astype(BF16)],axis=1)
            st=dot_nt(kx,jnp.concatenate([qm,qe],axis=1))
            pt=jnp.exp(st)
            dpt=dot_nt(vx,jnp.concatenate([dm,de],axis=1))
            ds=(pt*dpt).astype(BF16)
            dv=dv+dot_nn(pt.astype(BF16),dm)
            dk=dk+dot_nn(ds,qm)
            dqs.append(dot_nn(kt[half*HEAD_DIM:(half+1)*HEAD_DIM],ds))
        dq=jnp.concatenate(dqs,axis=0).T*(1/math.sqrt(HEAD_DIM))
        to=lambda base: pl.ds(pl.multiple_of(base+(p-pairs[0])*LANES,LANES),LANES)
        out_ref[:,to(0)]=dq.astype(BF16)
        out_ref[:,to(part)]=dk.astype(BF16)
        out_ref[:,to(2*part)]=dv.astype(BF16)
        return carry
    lax.fori_loop(pairs[0],pairs[1],pair,0)

def attention_grad(pairs,lens,mix,ctx,dctx,lse):
    rows,width=ctx.shape; wide=mix.shape[1]; part=3*(pairs[1]-pairs[0])*LANES
    b=lambda n: pl.BlockSpec((PACK,n),lambda g:(g,0))
    share=(pairs[1]-pairs[0])/(HEADS//2)
    return pl.pallas_call(functools.partial(attention_grad_kernel,pairs),grid=(rows//PACK,),
        in_specs=[pl.BlockSpec(memory_space=pltpu.SMEM),b(wide),b(width),b(width),b(LANES)],
        out_specs=b(part),out_shape=jax.ShapeDtypeStruct((rows,part),BF16),
        compiler_params=pltpu.CompilerParams(vmem_limit_bytes=VMEM_MOST),name='attention_grad',
        cost_estimate=pl.CostEstimate(flops=int(share*20*rows*PACK*width),bytes_accessed=rows*wide*4,transcendentals=int(share*HEADS*rows*PACK)))(lens,mix,ctx,dctx,lse)
EPS=1e-6
TILE=256
def half_tail(a, e):
    t=1.0/(1.0+0.3275911*a)
    p=t*(0.5*0.254829592+t*(0.5*-0.284496736+t*(0.5*1.421413741+t*(0.5*-1.453152027+t*(0.5*1.061405429)))))
    return p*e

def gelu_pair(x):
    z=jnp.abs(x)*(1/math.sqrt(2))
    e=jnp.exp(-z*z)
    h=half_tail(z,e)
    phi=jnp.where(x>0,1.0-h,h)
    return x*phi, phi+x*(e*(1/math.sqrt(2*math.pi)))

def normed(h):
    c=h-jnp.mean(h,axis=1,keepdims=True)
    f=lax.rsqrt(jnp.mean(c*c,axis=1,keepdims=True)+EPS)
    return c*f,f

def norm_back(e,n,f):
    return f*(e-jnp.mean(e,axis=1,keepdims=True)-n*jnp.mean(e*n,axis=1,keepdims=True))

def row_segments(lens_ref,first_row,rows):
    row=first_row+lax.broadcasted_iota(jnp.int32,(rows,LANES),0)
    lane=lax.broadcasted_iota(jnp.int32,(rows,LANES),1)
    packs=lens_ref.shape[0]
    seg=jnp.zeros((rows,LANES),jnp.int32)
    for g in range(packs):
        end=jnp.int32(g*PACK)
        for j in range(SEGS_PACK):
            end=end+lens_ref[g,j]
            seg=seg+(row>=end).astype(jnp.int32)
    return seg==lane

def feed_forward_kernel(lens_ref,ctx_ref,tok_ref,w_ref,vec_ref,n1_ref,r1_ref,low_ref,act_ref,dg_ref,n2_ref,r2_ref,res_ref,span_ref,score_ref,doc_ref,all_ref):
    i=pl.program_id(0)
    width=ctx_ref.shape[1]; rows=ctx_ref.shape[0]; reps=act_ref.shape[1]//width
    vec=lambda k: vec_ref[k:k+1,:]
    base=2*reps*width
    att=dot_nn(ctx_ref[...],w_ref[:,base:base+width])+vec(0)
    n1,f1=normed(tok_ref[...].astype(F32)+att)
    n1_ref[...]=n1; r1_ref[...]=jnp.broadcast_to(f1,(rows,LANES))
    first=n1*vec(1)+vec(2)
    low=first.astype(BF16); low_ref[...]=low
    out=first+vec(3)
    for q in range(reps):
        c=slice(q*width,(q+1)*width)
        x=dot_nn(low,w_ref[:,c])+vec(8+q)
        a,d=gelu_pair(x)
        a=a.astype(BF16)
        act_ref[:,c]=a; dg_ref[:,c]=d.astype(BF16)
        out=out+dot_nn(a,w_ref[:,(reps+q)*width:(reps+q+1)*width])
    n2,f2=normed(out)
    n2_ref[...]=n2; r2_ref[...]=jnp.broadcast_to(f2,(rows,LANES))
    res=(n2*vec(4)+vec(5)).astype(BF16)
    res_ref[...]=res
    span=dot_nn(res,w_ref[:,base+width:base+width+LANES])
    span_ref[...]=span
    score=jnp.broadcast_to(jnp.sum(span*vec_ref[15:16,:LANES],axis=1,keepdims=True),(rows,LANES))
    score_ref[...]=score
    all_ref[pl.ds(pl.multiple_of(i*rows,rows),rows),:]=score
    @pl.when(i==pl.num_programs(0)-1)
    def _():
        member=row_segments(lens_ref,0,all_ref.shape[0])
        s=jnp.where(member,all_ref[...],MASKED)
        top=jnp.max(s,axis=0,keepdims=True)
        total=jnp.sum(jnp.where(member,jnp.exp(s-top),0.0),axis=0,keepdims=True)
        real=lax.broadcasted_iota(jnp.int32,(1,LANES),1)<lens_ref.shape[0]*SEGS_PACK
        doc_ref[...]=jnp.where(real,top+jnp.log(jnp.where(real,total,1.0)),MASKED)

def feed_forward(lens,ctx,tok,w,vec,reps):
    rows,width=ctx.shape; ff=reps*width
    b=lambda n: pl.BlockSpec((TILE,n),lambda i:(i,0))
    s=lambda n,t: jax.ShapeDtypeStruct((rows,n),t)
    return pl.pallas_call(feed_forward_kernel,grid=(rows//TILE,),
        in_specs=[pl.BlockSpec(memory_space=pltpu.SMEM),b(width),b(width),once(w.shape),once(vec.shape)],
        out_specs=[b(width),b(LANES),b(width),b(ff),b(ff),b(width),b(LANES),b(width),b(LANES),b(LANES),once((1,LANES))],
        out_shape=[s(width,F32),s(LANES,F32),s(width,BF16),s(ff,BF16),s(ff,BF16),s(width,F32),s(LANES,F32),s(width,BF16),s(LANES,F32),s(LANES,F32),jax.ShapeDtypeStruct((1,LANES),F32)],
        scratch_shapes=[pltpu.VMEM((rows,LANES),F32)],
        compiler_params=pltpu.CompilerParams(vmem_limit_bytes=VMEM_MOST),name='feed_forward')(lens,ctx,tok,w,vec)

def feed_forward_grad_kernel(lens_ref,own_ids_ref,doc_ref,scores_ref,ids_ref,cot_ref,n2_ref,r2_ref,res_ref,span_ref,score_ref,dg_ref,n1_ref,r1_ref,w_ref,vec_ref,
                   olow_ref,ilow_ref,alow_ref,fsum_ref,dctx_ref,small_ref,spanw_ref,weight_ref,acc_ref):
    i=pl.program_id(0); last=pl.num_programs(0)-1
    rows,width=cot_ref.shape; reps=dg_ref.shape[1]//width
    vec=lambda k: vec_ref[k:k+1,:]
    base=2*reps*width
    @pl.when(i==0)
    def _():
        lane=lax.broadcasted_iota(jnp.int32,(1,LANES),1)
        marg=jnp.zeros((1,LANES),F32)
        for s in range(own_ids_ref.shape[0]):
            hit=ids_ref[...]==own_ids_ref[s].astype(F32)
            x=jnp.where(hit,scores_ref[...],MASKED)
            top=jnp.max(jnp.max(x,axis=1,keepdims=True),axis=0,keepdims=True)
            total=jnp.where(hit,jnp.exp(x-top),0.0)
            total=jnp.sum(jnp.sum(total,axis=1,keepdims=True),axis=0,keepdims=True)
            marg=jnp.where(lane==s,top+jnp.log(total),marg)
        weight_ref[...]=jnp.exp(doc_ref[...]-marg)
        small_ref[...]=jnp.zeros_like(small_ref)
        acc_ref[...]=jnp.zeros_like(acc_ref)
    member=row_segments(lens_ref,i*rows,rows)
    part=jnp.where(member,jnp.exp(jnp.where(member,score_ref[...]-doc_ref[...],0.0))*weight_ref[...],0.0)
    tw=jnp.sum(part,axis=1,keepdims=True)
    ans=vec_ref[15:16,:LANES]
    small_ref[15:16,:LANES]+=jnp.sum(tw*span_ref[...],axis=0,keepdims=True)
    sg=(tw*ans).astype(BF16)
    acc_ref[...]+=dot_tn(res_ref[...],sg)
    @pl.when(i==last)
    def _():
        spanw_ref[...]=acc_ref[...].astype(BF16)
    rg=cot_ref[...].astype(F32)+dot_nt(sg,w_ref[:,base+width:base+width+LANES])
    n2=n2_ref[...]
    def colsum(k,v):
        small_ref[k:k+1,:]+=jnp.sum(v,axis=0,keepdims=True)
    colsum(0,rg*n2); colsum(1,rg)
    ssum=norm_back(rg*vec(4),n2,r2_ref[:,:1])
    olow=ssum.astype(BF16); olow_ref[...]=olow
    colsum(2,olow.astype(F32))
    fg=ssum
    for q in range(reps):
        c=slice(q*width,(q+1)*width)
        il=(dot_nt(olow,w_ref[:,(reps+q)*width:(reps+q+1)*width])*dg_ref[:,c].astype(F32)).astype(BF16)
        ilow_ref[:,c]=il
        colsum(8+q,il.astype(F32))
        fg=fg+dot_nt(il,w_ref[:,c])
    n1=n1_ref[...]
    colsum(3,fg*n1); colsum(4,fg)
    fsum=norm_back(fg*vec(1),n1,r1_ref[:,:1])
    fsum_ref[...]=fsum
    alow=fsum.astype(BF16); alow_ref[...]=alow
    colsum(5,alow.astype(F32))
    dctx_ref[...]=dot_nt(alow,w_ref[:,base:base+width]).astype(BF16)

def feed_forward_grad(lens,own_ids,doc,scores,ids,cot,n2,r2,res,span,score,dg,n1,r1,w,vec):
    rows,width=cot.shape; ff=dg.shape[1]
    b=lambda n: pl.BlockSpec((TILE,n),lambda i:(i,0))
    s=lambda n,t: jax.ShapeDtypeStruct((rows,n),t)
    sm=pl.BlockSpec(memory_space=pltpu.SMEM)
    return pl.pallas_call(feed_forward_grad_kernel,grid=(rows//TILE,),
        in_specs=[sm,sm,once(doc.shape),once(scores.shape),once(ids.shape),b(width),b(width),b(LANES),b(width),b(LANES),b(LANES),b(ff),b(width),b(LANES),once(w.shape),once(vec.shape)],
        out_specs=[b(width),b(ff),b(width),b(width),b(width),once(vec.shape),once((width,LANES))],
        out_shape=[s(width,BF16),s(ff,BF16),s(width,BF16),s(width,F32),s(width,BF16),jax.ShapeDtypeStruct(vec.shape,F32),jax.ShapeDtypeStruct((width,LANES),BF16)],
        scratch_shapes=[pltpu.VMEM((1,LANES),F32),pltpu.VMEM((width,LANES),F32)],
        compiler_params=pltpu.CompilerParams(vmem_limit_bytes=VMEM_MOST),name='feed_forward_grad')(lens,own_ids,doc,scores,ids,cot,n2,r2,res,span,score,dg,n1,r1,w,vec)

def put_blocks(me_ref,keep_ref,give_ref,value,at):
    blocks,rows,_=keep_ref.shape
    second=me_ref[0]%2
    for t in range(blocks):
        low=value[2*t*rows:(2*t+1)*rows].astype(BF16)
        high=value[(2*t+1)*rows:(2*t+2)*rows].astype(BF16)
        @pl.when(second==0)
        def _():
            keep_ref[t,:,at]=low; give_ref[t,:,at]=high
        @pl.when(second==1)
        def _():
            keep_ref[t,:,at]=high; give_ref[t,:,at]=low

def early_kernel(reps,me_ref,low_ref,ilow_ref,act_ref,olow_ref,ctx_ref,alow_ref,keep_ref,give_ref):
    j=pl.program_id(0); last=pl.num_programs(0)-1
    put=lambda value: put_blocks(me_ref,keep_ref,give_ref,value,slice(None))
    @pl.when(j<reps)
    def _(): put(dot_tn(low_ref[...],ilow_ref[...]))
    @pl.when(jnp.logical_and(j>=reps,j<last))
    def _(): put(dot_tn(act_ref[...],olow_ref[...]))
    @pl.when(j==last)
    def _(): put(dot_tn(ctx_ref[...],alow_ref[...]))

def split_outs(dp,width,n):
    block=(dp//2,width//dp,width)
    return [pl.BlockSpec(block,lambda j:(0,0,j))]*2,[jax.ShapeDtypeStruct(block[:2]+(n*width,),BF16)]*2

def early_grads(me,low,ilow,act,olow,ctx,alow,outer_blocks,dp):
    rows,width=low.shape; reps=act.shape[1]//width
    full=once((rows,width)); n=reps+outer_blocks+1
    specs,shapes=split_outs(dp,width,n)
    return pl.pallas_call(functools.partial(early_kernel,reps),grid=(n,),
        in_specs=[pl.BlockSpec(memory_space=pltpu.SMEM),full,pl.BlockSpec((rows,width),lambda j:(0,jnp.minimum(j,reps-1))),pl.BlockSpec((rows,width),lambda j:(0,jnp.clip(j-reps,0,outer_blocks-1))),full,full,full],
        out_specs=specs,out_shape=shapes,
        compiler_params=pltpu.CompilerParams(vmem_limit_bytes=VMEM_MOST),name='early_weight_grads',
        cost_estimate=pl.CostEstimate(flops=2*rows*width*width*n,bytes_accessed=rows*width*n*4,transcendentals=0))(me,low,ilow,act,olow,ctx,alow)

def outer_kernel(me_ref,act_ref,olow_ref,keep_ref,give_ref):
    put_blocks(me_ref,keep_ref,give_ref,dot_tn(act_ref[...],olow_ref[...]),slice(None))

def outer_grads(me,act,olow,first,dp):
    rows,width=olow.shape; n=act.shape[1]//width-first
    specs,shapes=split_outs(dp,width,n)
    return pl.pallas_call(outer_kernel,grid=(n,),
        in_specs=[pl.BlockSpec(memory_space=pltpu.SMEM),pl.BlockSpec((rows,width),lambda j:(0,j+first)),once((rows,width))],
        out_specs=specs,out_shape=shapes,
        compiler_params=pltpu.CompilerParams(vmem_limit_bytes=VMEM_MOST),name='outer_weight_grad',
        cost_estimate=pl.CostEstimate(flops=2*rows*width*width*n,bytes_accessed=rows*width*n*4,transcendentals=0))(me,act,olow)

def late_kernel(me_ref,tok_ref,mg_ref,span_ref,keep_ref,give_ref,sum_ref):
    j=pl.program_id(0)
    width=tok_ref.shape[1]
    mg=mg_ref[...]
    sum_ref[...]=jnp.broadcast_to(jnp.sum(mg.astype(F32),axis=0,keepdims=True),sum_ref.shape)
    put_blocks(me_ref,keep_ref,give_ref,dot_tn(tok_ref[...],mg),pl.ds(pl.multiple_of(j*width,LANES),width))
    @pl.when(j==pl.num_programs(0)-1)
    def _():
        full=keep_ref.shape[2]
        put_blocks(me_ref,keep_ref,give_ref,span_ref[...].astype(F32),slice(full-span_ref.shape[1],full))

def late_grads(me,tok,mg,span,dp):
    rows,width=tok.shape; wide=mg.shape[1]
    out=(dp//2,width//dp,wide+span.shape[1])
    return pl.pallas_call(late_kernel,grid=(wide//width,),
        in_specs=[pl.BlockSpec(memory_space=pltpu.SMEM),once((rows,width)),pl.BlockSpec((rows,width),lambda j:(0,j)),once(span.shape)],
        out_specs=[once(out),once(out),pl.BlockSpec((8,width),lambda j:(0,j))],
        out_shape=[jax.ShapeDtypeStruct(out,BF16)]*2+[jax.ShapeDtypeStruct((8,wide),F32)],
        compiler_params=pltpu.CompilerParams(vmem_limit_bytes=VMEM_MOST),name='late_weight_grads',
        cost_estimate=pl.CostEstimate(flops=2*rows*width*wide,bytes_accessed=rows*wide*4,transcendentals=0))(me,tok,mg,span)

def input_kernel(sizes,w_ref,fs_ref,*refs):
    *mgs,out_ref=refs
    width=fs_ref.shape[1]
    total=fs_ref[...]
    start=0
    for mg_ref,n in zip(mgs,sizes):
        for k in range(3):
            total=total+dot_nt(mg_ref[:,k*n:(k+1)*n],w_ref[:,k*width+start:k*width+start+n])
        start+=n
    out_ref[...]=total

def input_grads(w,fs,mgs):
    rows,width=fs.shape
    b=lambda n: pl.BlockSpec((TILE,n),lambda i:(i,0))
    return pl.pallas_call(functools.partial(input_kernel,[m.shape[1]//3 for m in mgs]),grid=(rows//TILE,),
        in_specs=[once(w.shape),b(width)]+[b(m.shape[1]) for m in mgs],out_specs=b(width),out_shape=jax.ShapeDtypeStruct((rows,width),F32),
        compiler_params=pltpu.CompilerParams(vmem_limit_bytes=VMEM_MOST),name='input_grad',
        cost_estimate=pl.CostEstimate(flops=6*rows*width*width,bytes_accessed=rows*width*16,transcendentals=0))(w,fs,*mgs)
AXES = ("dp", "fsdp")
LATE_BLOCKS = 3


def pack_lanes(parts):
    flat = jnp.concatenate(parts, axis=-1)
    wide = -(-flat.shape[-1] // LANES) * LANES
    flat = jnp.pad(flat, [(0, 0)] * (flat.ndim - 1) + [(0, wide - flat.shape[-1])])
    return flat.reshape(flat.shape[:-1] + (wide // LANES, LANES))


def unpack_lanes(packed, sizes):
    flat = packed.reshape(packed.shape[:-2] + (-1,))
    starts = [sum(sizes[:i]) for i in range(len(sizes))]
    return [flat[..., a : a + n] for a, n in zip(starts, sizes)]


def to_all(block, devices):
    return lax.all_to_all(jnp.broadcast_to(block[None], (devices,) + block.shape), AXES, 0, 0)


def shards(
    tokens,
    cotangent,
    doc_lengths,
    query_ids,
    qkv_weight,
    query_bias,
    value_bias,
    attn_weight,
    attn_bias,
    first_gain,
    first_shift,
    inner_weight,
    inner_bias,
    outer_weight,
    outer_bias,
    second_gain,
    second_shift,
    span_weight,
    answer_vector,
):
    rows, width = tokens.shape
    packs_here = rows // PACK
    devices = lax.axis_size("dp") * lax.axis_size("fsdp")
    share = qkv_weight.shape[0]
    ff = inner_weight.shape[1]
    reps = ff // width
    segs_here = packs_here * SEGS_PACK
    span = span_weight.shape[1]

    row_params = (attn_bias, first_gain, first_shift, outer_bias, second_gain, second_shift)
    smalls = row_params + (query_bias, value_bias, inner_bias, answer_vector)
    answers = answer_vector.shape[0]
    rows_in = len(row_params) + 2 + reps
    packed = pack_lanes(smalls)
    packed = jnp.pad(packed, ((0, share - packed.shape[0]), (0, 0)))
    id_row = jnp.pad(
        query_ids[:, 0].astype(F32)[None], ((0, 0), (0, LANES - segs_here)), constant_values=-1.0
    )

    orders = bit_orders(lax.axis_size("dp"))
    fsdp = lax.axis_size("fsdp")
    me = jnp.stack([lax.axis_index("dp"), lax.axis_index("fsdp")]).astype(jnp.int32)
    mix = jnp.concatenate([qkv_weight, packed], axis=1)
    mix_near = gather_near(mix)
    near = len(mix_near)
    mix_walk = Gathering(mix_near, orders, qkv_weight.shape[1] // 2)
    mix_walk.advance(0)
    mix_walk.send()
    mix_parts = mix_walk.parts()
    inner_turned = (
        inner_weight.reshape(share, devices, reps, share).transpose(0, 2, 1, 3).reshape(share, ff)
    )
    outer_blocks = [outer_weight[q * share : (q + 1) * share] for q in range(reps)]
    rest = jnp.concatenate([inner_turned] + outer_blocks + [attn_weight, span_weight], axis=1)
    rest_full = lax.all_gather(rest, AXES, axis=0, tiled=True)

    mix_full, vectors, mixed, context, logsum = attention(
        doc_lengths, me, tokens, mix_parts, orders, near, (share, rows_in, answers)
    )
    (
        normed_one,
        factor_one,
        first_low,
        active,
        gelu_slope,
        normed_two,
        factor_two,
        result,
        span_rows,
        token_score,
        doc_score,
    ) = feed_forward(
        doc_lengths, context, tokens, rest_full, vectors, reps
    )
    exchanged = to_all(jnp.concatenate([doc_score, id_row], axis=0), devices)
    scores_all, ids_all = exchanged[:, 0], exchanged[:, 1]

    outer_low, inner_low, attended_low, first_sum_grad, context_grad, small_sums, span_grad = (
        feed_forward_grad(
            doc_lengths,
            query_ids.reshape(-1),
            doc_score,
            scores_all,
            ids_all,
            cotangent,
            normed_two,
            factor_two,
            result,
            span_rows,
            token_score,
            gelu_slope,
            normed_one,
            factor_one,
            rest_full,
            vectors,
        )
    )
    early_blocks = reps - LATE_BLOCKS
    dp = lax.axis_size("dp")
    keep, give = early_grads(
        me, first_low, inner_low, active, outer_low, context, attended_low, early_blocks, dp
    )
    came = swap(give, "dp", orders[0][0])
    outer_low, keep = tie(outer_low, keep)
    outer_walk = Reduction(*outer_grads(me, active, outer_low, early_blocks, dp), orders[1])
    came, outer_walk.keep = tie(came, outer_walk.keep)
    outer_walk.send()
    early = add_low(keep, came)
    cores = [[d for d in range(dp) if d % 2 == c] for c in range(2)]
    early_dp = lax.psum_scatter(
        early.reshape(-1, early.shape[-1]),
        "dp",
        scatter_dimension=0,
        axis_index_groups=cores,
        tiled=True,
    )
    context_grad, early = tie(context_grad, early)
    mixed_grad = attention_grad((0, HEADS // 2), doc_lengths, mixed, context, context_grad, logsum)
    mixed_grad, outer_walk.came = tie(mixed_grad, outer_walk.came)
    *late, bias_sums = late_grads(me, tokens, mixed_grad, span_grad, dp)
    late, outer_walk.came = tie(late, outer_walk.came)
    late_walk = Reduction(*late, orders[0])
    late_walk.send()
    outer_walk.add()
    outer_walk.advance(2)
    outer_walk.send()
    n_rows = small_sums.shape[0]
    by_owner = small_sums.reshape(n_rows, devices, share).transpose(1, 0, 2)
    biases = bias_sums[0].reshape(3, devices, share).transpose(1, 0, 2)
    small_grads = pack_lanes(
        [
            by_owner.reshape(devices, n_rows * share),
            biases.reshape(devices, 3 * share),
            small_sums[15, :span].reshape(devices, span // devices),
        ]
    )
    small_grads, late_walk.came, outer_walk.give = tie(
        small_grads, late_walk.came, outer_walk.give
    )
    late_walk.add()
    late_walk.advance(2)
    late_walk.send()
    small_grads, early_dp, late_walk.keep, outer_walk.keep = tie(
        small_grads, early_dp, late_walk.keep, outer_walk.keep
    )
    received = lax.all_to_all(small_grads, AXES, 0, 0)
    early_sum, early_takes = start_near([early_dp])
    scores_all, first_sum_grad, early_sum = tie(scores_all, first_sum_grad, early_sum)
    input_grad = input_grads(mix_full, first_sum_grad, [mixed_grad])
    input_grad, early_takes, late_walk.came, outer_walk.came = tie(
        input_grad, early_takes, late_walk.came, outer_walk.came
    )
    outer_walk.add()
    outer_walk.send()
    late_walk.add()
    late_walk.send()
    received, late_walk.came, outer_walk.came = tie(
        received, late_walk.came, outer_walk.came
    )
    outer_walk.add()
    late_walk.add()
    late_sum, takes = start_near([late_walk.keep, outer_walk.keep])
    received, early_takes, late_sum = tie(received, early_takes, late_sum)
    early_sum = add_near(early_sum, early_takes)
    mine = jnp.sum(received, axis=0)
    own_rows, own_biases, answer_own = unpack_lanes(
        mine, [n_rows * share, 3 * share, span // devices]
    )
    row_of = lambda k: own_rows[k * share : (k + 1) * share]
    queries = lax.broadcasted_iota(F32, (packs_here * devices, 1), 0)
    member_query = ids_all[:, :segs_here].reshape(1, -1) == queries
    marginal = jax.nn.logsumexp(
        jnp.where(member_query, scores_all[:, :segs_here].reshape(1, -1), MASKED), axis=1
    )
    inner_own = (
        early_sum[:, :ff].reshape(share, reps, devices, share).transpose(0, 2, 1, 3)
    ).reshape(share, ff)
    inner_own, takes = tie(inner_own, takes)
    late_sum = add_near(late_sum, takes)
    outer_own = jnp.concatenate(
        [early_sum[:, ff + q * width : ff + (q + 1) * width] for q in range(early_blocks)]
        + [late_sum[:, 3 * width + span + q * width :][:, :width] for q in range(LATE_BLOCKS)],
        axis=0,
    )
    return (
        jnp.sum(marginal),
        result,
        input_grad,
        late_sum[:, : 3 * width],
        own_biases[:share],
        own_biases[2 * share :],
        early_sum[:, -width:],
        row_of(5),
        row_of(3),
        row_of(4),
        inner_own,
        own_rows[8 * share : (8 + reps) * share],
        outer_own,
        row_of(2),
        row_of(0),
        row_of(1),
        late_sum[:, 3 * width : 3 * width + span],
        answer_own,
    )


def solution(mesh):
    rows = P(AXES, None)
    flat = P(AXES)
    in_specs = (rows,) * 4 + (rows, flat, flat, rows, flat, flat, flat, rows, flat, rows)
    in_specs += (flat, flat, flat, rows, flat)
    out_specs = (P(), rows, rows, rows, flat, flat, rows, flat, flat, flat, rows, flat, rows)
    out_specs += (flat, flat, flat, rows, flat)
    return jax.shard_map(shards, mesh=mesh, in_specs=in_specs, out_specs=out_specs, check_vma=False)
```

profile of v0, /device:TPU:0, one launch (start us, length us, event | category | flops | bytes accessed | tf_op | source)
XLA Modules:
  0.0 326.7 jit_solution(9131495187260856395)
XLA Ops:
  7.3 2.1 reshape.111
  12.7 3.1 collective-permute-start
  15.7 2.6 collective-permute-start.1
  18.4 7.8 %collective-permute-done.2 = bf16[24,2432]{1,0:T(8,128)(2,1)S(1)} collective-permute-done((bf16[24,2432]{1,0:T(8,128)(2,1)S(1)}, bf16[24,2432]{1,0:T(8,128)(2,1)S(1)}, u32[]{:S(2)}, u32[]{:S(2)}) %collective-permute-start.2) | collective-permute-done | bytes 116768 | tf_op jit(solution)/shard_map/ppermute | solution.py:13
  26.2 1.7 collective-permute-done.1
  28.0 1.6 collective-permute-start.6
  29.7 1.6 collective-permute-start.3
  31.4 2.9 collective-permute-done.6
  34.3 1.6 collective-permute-start.7
  36.0 1.8 collective-permute-done.3
  38.1 12.0 %collective-permute-done.7 = bf16[8,24,1280]{2,1,0:T(8,128)(2,1)S(1)} collective-permute-done((bf16[8,24,1280]{2,1,0:T(8,128)(2,1)S(1)}, bf16[8,24,1280]{2,1,0:T(8,128)(2,1)S(1)}, u32[]{:S(2)}, u32[]{:S(2)}) %collective-permute-start.7) | collective-permute-done | bytes 491552 | tf_op jit(solution)/shard_map/ppermute | solution.py:13
  51.5 2.7 collective-permute-done.5.p1
  55.2 25.7 %attention.1 = (bf16[768,2432]{1,0:T(8,128)(2,1)}, f32[16,768]{1,0:T(8,128)}, bf16[1024,2304]{1,0:T(8,128)(2,1)}, bf16[1024,768]{1,0:T(8,128)(2,1)}, f32[1024,128]{1,0:T(8,128)}) custom-call(s32[2,4]{1,0:T(2,128)} %lens_ref.7, s32[2]{0:T(128)} %pad_add_fusion.me_ref, bf16[1024,768]{1,0:T(8,128)(2,1)} %tok_ref.5, bf16[16,24,1152]{2,1,0:T(8,128)(2,1)} %copy-done.18, ...), custom_call_target="tpu_custom_call" | custom-call | flops 6845104128 | bytes 9437184 | tf_op jit(solution)/shard_map/attention/pallas_call | solution.py:242
  80.9 27.5 %all-gather.2.cloned.1.call-done.w_ref = bf16[768,7040]{1,0:T(8,128)(2,1)} async-done(((bf16[24,7040]{1,0:T(8,128)(2,1)}), bf16[768,7040]{1,0:T(8,128)(2,1)}) %all-gather.2.cloned.1.call-update) | async-done | bytes 10813456 | tf_op jit(solution)/shard_map/all_gather | solution.py:610
  108.3 31.5 %feed_forward.1 = (f32[1024,768]{1,0:T(8,128)}, f32[1024,128]{1,0:T(8,128)}, bf16[1024,768]{1,0:T(8,128)(2,1)}, bf16[1024,3072]{1,0:T(8,128)(2,1)}, bf16[1024,30...) custom-call(s32[2,4]{1,0:T(2,128)} %lens_ref.7, ...), custom_call_target="tpu_custom_call" | custom-call | tf_op jit(solution)/shard_map/feed_forward/pallas_call | solution.py:374
  140.5 10.4 %all_to_all.10 = f32[32,2,128]{2,1,0:T(2,128)S(1)} all-to-all(f32[32,2,128]{2,1,0:T(2,128)S(1)} %broadcast_in_dim.25), channel_id=1, replica_groups=mesh['dp'=8,'fsdp'=4] {'dp','fsdp'}, dimensions={0} | all-to-all | bytes 65536 | tf_op jit(solution)/shard_map/all_to_all | solution.py:552
  151.5 25.8 %feed_forward_grad.1 = (bf16[1024,768]{1,0:T(8,128)(2,1)}, bf16[1024,3072]{1,0:T(8,128)(2,1)}, bf16[1024,768]{1,0:T(8,128)(2,1)}, f32[1024,768]{1,0:T(8,128)}, b...) custom-call(s32[2,4]{1,0:T(2,128)} %lens_ref.7, s32[8]{0:T(128)} %bitcast.128, ...), custom_call_target="tpu_custom_call" | custom-call | tf_op jit(solution)/shard_map/feed_forward_grad/pallas_call | solution.py:439
  177.3 14.8 %early_weight_grads.1 = (bf16[4,96,4608]{2,1,0:T(8,128)(2,1)}, bf16[4,96,4608]{2,1,0:T(8,128)(2,1)}) custom-call(s32[2]{0:T(128)} %pad_add_fusion.me_ref, bf16[1024,768]{1,0:T(8,128)(2,1)} %get-tuple-element.101.low_ref, bf16[1024,3072]{1,0:T(8,128)(2,1)} %get-tuple-element.102.ilow_ref, bf16[1024,3072]{1,0:T(8,128)(2,1)} %get-tuple-element.103.act_ref, ...), custom_call_target="tpu_custom_call" | custom-call | flops 7247757312 | bytes 18874368 | tf_op jit(solution)/shard_map/early_weight_grads/pallas_call | solution.py:477
  192.1 8.1 %outer_weight_grad.1 = (bf16[4,96,2304]{2,1,0:T(8,128)(2,1)}, bf16[4,96,2304]{2,1,0:T(8,128)(2,1)}) custom-call(s32[2]{0:T(128)} %pad_add_fusion.me_ref, bf16[1024,3072]{1,0:T(8,128)(2,1)} %get-tuple-element.103.act_ref, bf16[1024,768]{1,0:T(8,128)(2,1)} %get-tuple-element.108.olow_ref), custom_call_target="tpu_custom_call" | custom-call | flops 3623878656 | bytes 9437184 | tf_op jit(solution)/shard_map/outer_weight_grad/pallas_call | solution.py:489
  200.2 4.6 %add_convert_fusion = bf16[4,96,4608]{2,1,0:T(8,128)(2,1)} fusion(bf16[4,96,4608]{2,1,0:T(8,128)(2,1)} %collective-permute-done.9, bf16[4,96,4608]{2,1,0:T(8,128)(2,1)S(1)} %copy-done), kind=kLoop, calls=%fused_computation | loop fusion | flops 7077888 | bytes 10616832 | tf_op jit(solution)/shard_map/convert_element_type | solution.py:65
  206.8 26.7 %attention_grad.1.mg_ref.refs_0_ = bf16[1024,2304]{1,0:T(8,128)(2,1)} custom-call(s32[2,4]{1,0:T(2,128)} %lens_ref.7, bf16[1024,2304]{1,0:T(8,128)(2,1)} %get-tuple-element.98.mix_ref, bf16[1024,768]{1,0:T(8,128)(2,1)} %get-tuple-element.85.ctx_ref, bf16[1024,768]{1,0:T(8,128)(2,1)} %get-tuple-element.111.dctx_ref, f32[1024,128]{1,0:T(8,128)} %get-tuple-element.112.lse_ref), custom_call_target="tpu_custom_call" | custom-call | flops 8053063680 | bytes 9437184 | tf_op jit(solution)/shard_map/attention_grad/pallas_call | solution.py:295
  233.5 9.6 %late_weight_grads.1 = (bf16[4,96,2432]{2,1,0:T(8,128)(2,1)}, bf16[4,96,2432]{2,1,0:T(8,128)(2,1)}, f32[8,2304]{1,0:T(8,128)}) custom-call(s32[2]{0:T(128)} %pad_add_fusion.me_ref, bf16[1024,768]{1,0:T(8,128)(2,1)} %tok_ref.5, bf16[1024,2304]{1,0:T(8,128)(2,1)} %attention_grad.1.mg_ref.refs_0_, bf16[768,128]{1,0:T(8,128)(2,1)} %get-tuple-element.115.span_ref), custom_call_target="tpu_custom_call" | custom-call | flops 3623878656 | bytes 9437184 | tf_op jit(solution)/shard_map/late_weight_grads/pallas_call | solution.py:509
  245.9 2.5 add_convert_fusion.2
  251.9 2.1 dynamic-slice_bitcast_fusion.4
  254.9 3.5 %collective-permute-start.14 = (bf16[24,4608]{1,0:T(8,128)(2,1)}, bf16[24,4608]{1,0:T(8,128)(2,1)}, u32[]{:S(2)}, u32[]{:S(2)}) collective-permute-start(bf16[24,4608]{1,0:T(8,128)(2,1)} %get-tuple-element.156), channel_id=1, source_target_pairs={{0,3},{1,2},{2,1},{3,0},{4,7},{5,6},{6,5},{7,4},{8,11},{9,10},{10,... | collective-permute-start | bytes 663560 | tf_op jit(solution)/shard_map/ppermute | solution.py:13
  258.4 3.4 %all-to-all-start.1 = ((f32[32,4,128]{2,1,0:T(4,128)}), f32[32,4,128]{2,1,0:T(4,128)S(1)}, u32[]{:S(2)}, u32[]{:S(2)}) async-start(f32[32,4,128]{2,1,0:T(4,128)} %reshape.116), calls=%async_computation.2 | async-start | bytes 131072 | tf_op jit(solution)/shard_map/all_to_all | solution.py:701
  261.8 9.1 %input_grad.1 = f32[1024,768]{1,0:T(8,128)} custom-call(bf16[768,2432]{1,0:T(8,128)(2,1)} %get-tuple-element.128.w_ref, f32[1024,768]{1,0:T(8,128)} %get-tuple-element.129.fs_ref, bf16[1024,2304]{1,0:T(8,128)(2,1)} %attention_grad.1.mg_ref.refs_0_), custom_call_target="tpu_custom_call" | custom-call | flops 3623878656 | bytes 12582912 | tf_op jit(solution)/shard_map/input_grad/pallas_call | solution.py:530
  272.1 3.4 %collective-permute-done.15 = bf16[2,96,2432]{2,1,0:T(8,128)(2,1)S(1)} collective-permute-done((bf16[2,96,2432]{2,1,0:T(8,128)(2,1)}, bf16[2,96,2432]{2,1,0:T(8,128)(2,1)S(1)}, u32[]{:S(2)}, u32[]{:S(2)}) %collective-permute-start.15) | collective-permute-done | bytes 933920 | tf_op jit(solution)/shard_map/ppermute | solution.py:13
  282.4 9.8 %collective-permute-done.18 = bf16[1,96,2304]{2,1,0:T(8,128)(2,1)S(1)} collective-permute-done((bf16[1,96,2304]{2,1,0:T(8,128)(2,1)S(1)}, bf16[1,96,2304]{2,1,0:T(8,128)(2,1)S(1)}, u32[]{:S(2)}, u32[]{:S(2)}) %collective-permute-start.18) | collective-permute-done | bytes 442400 | tf_op jit(solution)/shard_map/ppermute | solution.py:13
  296.8 2.3 collective-permute-start.20
  305.2 2.6 reshape.124
  309.3 6.9 %collective-permute-done.20 = bf16[24,4736]{1,0:T(8,128)(2,1)} collective-permute-done((bf16[24,4736]{1,0:T(8,128)(2,1)}, bf16[24,4736]{1,0:T(8,128)(2,1)}, u32[]{:S(2)}, u32[]{:S(2)}) %collective-permute-start.20) | collective-permute-done | bytes 227360 | tf_op jit(solution)/shard_map/ppermute | solution.py:13
  (184 shorter events, 39.6 us)
Async XLA Ops:
  7.2 101.1 %all-gather.2.cloned.1.call-start = ((), (), s32[]{:S(2)}) async-start(), calls=%async_computation.3 | async-start | bytes 11151360 | tf_op jit(solution)/shard_map/all_gather | solution.py:610
  11.8 240.0 %reduce-scatter.2.cloned.1.call-start = ((), (), s32[]{:S(2)}) async-start(), calls=%async_computation.4 | async-start | bytes 4423680 | tf_op jit(solution)/shard_map/reduce_scatter | solution.py:665
  12.7 15.3 %collective-permute-start = (bf16[24,2432]{1,0:T(8,128)(2,1)S(1)}, bf16[24,2432]{1,0:T(8,128)(2,1)S(1)}, u32[]{:S(2)}, u32[]{:S(2)}) collective-permute-start(bf16[24,2432]{1,0:T(8,128)(2,1)S(1)} %fusion.1), channel_id=1, source_target_pairs={{0,1},{1,0},{2,3},{3,2},{4,5},{5,4},{6,7},{7,6},{8,9},{9,8},{10,11... | collective-permute-start | bytes 350216 | tf_op jit(solution)/shard_map/ppermute | solution.py:13
  15.7 12.2 %collective-permute-start.1 = (bf16[24,2432]{1,0:T(8,128)(2,1)S(1)}, bf16[24,2432]{1,0:T(8,128)(2,1)S(1)}, u32[]{:S(2)}, u32[]{:S(2)}) collective-permute-start(bf16[24,2432]{1,0:T(8,128)(2,1)S(1)} %fusion.1), channel_id=1, source_target_pairs={{0,2},{1,3},{2,0},{3,1},{4,6},{5,7},{6,4},{7,5},{8,10},{9,11},{10,... | collective-permute-start | bytes 350216 | tf_op jit(solution)/shard_map/ppermute | solution.py:13
  18.4 7.9 %collective-permute-start.2 = (bf16[24,2432]{1,0:T(8,128)(2,1)S(1)}, bf16[24,2432]{1,0:T(8,128)(2,1)S(1)}, u32[]{:S(2)}, u32[]{:S(2)}) collective-permute-start(bf16[24,2432]{1,0:T(8,128)(2,1)S(1)} %fusion.1), channel_id=1, source_target_pairs={{0,3},{1,2},{2,1},{3,0},{4,7},{5,6},{6,5},{7,4},{8,11},{9,10},{10,... | collective-permute-start | bytes 350216 | tf_op jit(solution)/shard_map/ppermute | solution.py:13
  28.0 6.3 %collective-permute-start.6 = (bf16[4,24,1280]{2,1,0:T(8,128)(2,1)S(1)}, bf16[4,24,1280]{2,1,0:T(8,128)(2,1)S(1)}, u32[]{:S(2)}, u32[]{:S(2)}) collective-permute-start(bf16[4,24,1280]{2,1,0:T(8,128)(2,1)S(1)} %pad_maximum_fusion.1), channel_id=1, source_target_pairs={{0,8},{4,12},{8,0},{12,4},{16,24},{20,28},{24,16},{28,20},{1,9},{5... | collective-permute-start | bytes 737288 | tf_op jit(solution)/shard_map/ppermute | solution.py:13
  29.7 8.1 %collective-permute-start.3 = (bf16[4,24,1152]{2,1,0:T(8,128)(2,1)S(1)}, bf16[4,24,1152]{2,1,0:T(8,128)(2,1)S(1)}, u32[]{:S(2)}, u32[]{:S(2)}) collective-permute-start(bf16[4,24,1152]{2,1,0:T(8,128)(2,1)S(1)} %pad_maximum_fusion.6), channel_id=1, source_target_pairs={{0,16},{4,20},{8,24},{12,28},{16,0},{20,4},{24,8},{28,12},{1,17},{... | collective-permute-start | bytes 663560 | tf_op jit(solution)/shard_map/ppermute | solution.py:13
  31.4 20.1 %copy-start.19 = (s32[8,1]{0,1:T(1,128)S(1)}, s32[8,1]{0,1:T(1,128)}, u32[]{:S(2)}) copy-start(s32[8,1]{0,1:T(1,128)} %param.22) | copy-start | bytes 100
  34.3 15.8 %collective-permute-start.7 = (bf16[8,24,1280]{2,1,0:T(8,128)(2,1)S(1)}, bf16[8,24,1280]{2,1,0:T(8,128)(2,1)S(1)}, u32[]{:S(2)}, u32[]{:S(2)}) collective-permute-start(bf16[8,24,1280]{2,1,0:T(8,128)(2,1)S(1)} %get-tuple-element.173), channel_id=1, source_target_pairs={{0,16},{4,20},{8,24},{12,28},{16,0},{20,4},{24,8},{28,12},{1,17},{... | collective-permute-start | bytes 1474568 | tf_op jit(solution)/shard_map/ppermute | solution.py:13
  37.8 12.5 %collective-permute-start.4 = (bf16[8,24,1152]{2,1,0:T(8,128)(2,1)S(1)}, bf16[8,24,1152]{2,1,0:T(8,128)(2,1)S(1)}, u32[]{:S(2)}, u32[]{:S(2)}) collective-permute-start(bf16[8,24,1152]{2,1,0:T(8,128)(2,1)S(1)} %get-tuple-element.175), channel_id=1, source_target_pairs={{0,8},{4,12},{8,0},{12,4},{16,24},{20,28},{24,16},{28,20},{1,9},{5... | collective-permute-start | bytes 1327112 | tf_op jit(solution)/shard_map/ppermute | solution.py:13
  50.2 4.0 %collective-permute-start.8 = (bf16[16,24,1280]{2,1,0:T(8,128)(2,1)S(1)}, bf16[16,24,1280]{2,1,0:T(8,128)(2,1)S(1)}, u32[]{:S(2)}, u32[]{:S(2)}) collective-permute-start(bf16[16,24,1280]{2,1,0:T(8,128)(2,1)S(1)} %constant_dynamic-update-slice_fusion.16.p2), channel_id=1, source_target_pairs={{0,4},{4,0},{8,12},{12,8},{16,20},{20,16},{24,28},{28,24},{1,5},{5... | collective-permute-start | bytes 2949128 | tf_op jit(solution)/shard_map/ppermute | solution.py:13
  50.3 3.9 %collective-permute-start.5 = (bf16[16,24,1152]{2,1,0:T(8,128)(2,1)S(1)}, bf16[16,24,1152]{2,1,0:T(8,128)(2,1)}, u32[]{:S(2)}, u32[]{:S(2)}) collective-permute-start(bf16[16,24,1152]{2,1,0:T(8,128)(2,1)S(1)} %constant_dynamic-update-slice_fusion.5.p0), channel_id=1, source_target_pairs={{0,4},{4,0},{8,12},{12,8},{16,20},{20,16},{24,28},{28,24},{1,5},{5... | collective-permute-start | bytes 2654216 | tf_op jit(solution)/shard_map/ppermute | solution.py:13
  192.1 8.1 %collective-permute-start.9 = (bf16[4,96,4608]{2,1,0:T(8,128)(2,1)}, bf16[4,96,4608]{2,1,0:T(8,128)(2,1)}, u32[]{:S(2)}, u32[]{:S(2)}) collective-permute-start(bf16[4,96,4608]{2,1,0:T(8,128)(2,1)} %get-tuple-element.107), channel_id=1, source_target_pairs={{0,4},{4,0},{8,12},{12,8},{16,20},{20,16},{24,28},{28,24},{1,5},{5... | collective-permute-start | bytes 10616840 | tf_op jit(solution)/shard_map/ppermute | solution.py:13
  206.3 27.2 %collective-permute-start.10 = (bf16[4,96,2304]{2,1,0:T(8,128)(2,1)S(1)}, bf16[4,96,2304]{2,1,0:T(8,128)(2,1)S(1)}, u32[]{:S(2)}, u32[]{:S(2)}) collective-permute-start(bf16[4,96,2304]{2,1,0:T(8,128)(2,1)S(1)} %copy-done.30), channel_id=1, source_target_pairs={{0,4},{4,0},{8,12},{12,8},{16,20},{20,16},{24,28},{28,24},{1,5},{5... | collective-permute-start | bytes 5308424 | tf_op jit(solution)/shard_map/ppermute | solution.py:13
  233.5 9.6 %copy-start.3 = (bf16[4,96,2304]{2,1,0:T(8,128)(2,1)}, bf16[4,96,2304]{2,1,0:T(8,128)(2,1)S(1)}, u32[]{:S(2)}) copy-start(bf16[4,96,2304]{2,1,0:T(8,128)(2,1)S(1)} %collective-permute-done.10) | copy-start | bytes 5308420
  233.5 9.8 %copy-start.14 = (f32[16,768]{1,0:T(8,128)S(1)}, f32[16,768]{1,0:T(8,128)}, u32[]{:S(2)}) copy-start(f32[16,768]{1,0:T(8,128)} %get-tuple-element.97) | copy-start | bytes 147460
  233.5 10.4 %copy-start.12 = (f32[32,1,128]{2,1,0:T(1,128)S(1)}, f32[32,1,128]{2,1,0:T(1,128)}, u32[]{:S(2)}) copy-start(f32[32,1,128]{2,1,0:T(1,128)} %get-tuple-element.193) | copy-start | bytes 49156
  243.2 6.4 %collective-permute-start.11 = (bf16[4,96,2432]{2,1,0:T(8,128)(2,1)}, bf16[4,96,2432]{2,1,0:T(8,128)(2,1)S(1)}, u32[]{:S(2)}, u32[]{:S(2)}) collective-permute-start(bf16[4,96,2432]{2,1,0:T(8,128)(2,1)} %get-tuple-element.120), channel_id=1, source_target_pairs={{0,4},{4,0},{8,12},{12,8},{16,20},{20,16},{24,28},{28,24},{1,5},{5... | collective-permute-start | bytes 5603336 | tf_op jit(solution)/shard_map/ppermute | solution.py:13
  249.5 22.5 %collective-permute-start.16 = (bf16[2,96,2304]{2,1,0:T(8,128)(2,1)}, bf16[2,96,2304]{2,1,0:T(8,128)(2,1)}, u32[]{:S(2)}, u32[]{:S(2)}) collective-permute-start(bf16[2,96,2304]{2,1,0:T(8,128)(2,1)} %get-tuple-element.155), channel_id=1, source_target_pairs={{0,16},{4,20},{8,24},{12,28},{16,0},{20,4},{24,8},{28,12},{1,17},{... | collective-permute-start | bytes 2654216 | tf_op jit(solution)/shard_map/ppermute | solution.py:13
  251.9 23.6 %collective-permute-start.15 = (bf16[2,96,2432]{2,1,0:T(8,128)(2,1)}, bf16[2,96,2432]{2,1,0:T(8,128)(2,1)S(1)}, u32[]{:S(2)}, u32[]{:S(2)}) collective-permute-start(bf16[2,96,2432]{2,1,0:T(8,128)(2,1)} %get-tuple-element.152), channel_id=1, source_target_pairs={{0,8},{4,12},{8,0},{12,4},{16,24},{20,28},{24,16},{28,20},{1,9},{5... | collective-permute-start | bytes 2801672 | tf_op jit(solution)/shard_map/ppermute | solution.py:13
  254.0 21.5 %collective-permute-start.12 = (bf16[24,4608]{1,0:T(8,128)(2,1)}, bf16[24,4608]{1,0:T(8,128)(2,1)S(1)}, u32[]{:S(2)}, u32[]{:S(2)}) collective-permute-start(bf16[24,4608]{1,0:T(8,128)(2,1)} %get-tuple-element.158), channel_id=1, source_target_pairs={{0,1},{1,0},{2,3},{3,2},{4,5},{5,4},{6,7},{7,6},{8,9},{9,8},{10,11... | collective-permute-start | bytes 663560 | tf_op jit(solution)/shard_map/ppermute | solution.py:13
  254.2 21.3 %collective-permute-start.13 = (bf16[24,4608]{1,0:T(8,128)(2,1)}, bf16[24,4608]{1,0:T(8,128)(2,1)S(1)}, u32[]{:S(2)}, u32[]{:S(2)}) collective-permute-start(bf16[24,4608]{1,0:T(8,128)(2,1)} %get-tuple-element.157), channel_id=1, source_target_pairs={{0,2},{1,3},{2,0},{3,1},{4,6},{5,7},{6,4},{7,5},{8,10},{9,11},{10,... | collective-permute-start | bytes 663560 | tf_op jit(solution)/shard_map/ppermute | solution.py:13
  254.9 21.6 %collective-permute-start.14 = (bf16[24,4608]{1,0:T(8,128)(2,1)}, bf16[24,4608]{1,0:T(8,128)(2,1)}, u32[]{:S(2)}, u32[]{:S(2)}) collective-permute-start(bf16[24,4608]{1,0:T(8,128)(2,1)} %get-tuple-element.156), channel_id=1, source_target_pairs={{0,3},{1,2},{2,1},{3,0},{4,7},{5,6},{6,5},{7,4},{8,11},{9,10},{10,... | collective-permute-start | bytes 663560 | tf_op jit(solution)/shard_map/ppermute | solution.py:13
  258.4 24.0 %all-to-all-start.1 = ((f32[32,4,128]{2,1,0:T(4,128)}), f32[32,4,128]{2,1,0:T(4,128)S(1)}, u32[]{:S(2)}, u32[]{:S(2)}) async-start(f32[32,4,128]{2,1,0:T(4,128)} %reshape.116), calls=%async_computation.2 | async-start | bytes 131072 | tf_op jit(solution)/shard_map/all_to_all | solution.py:701
  261.8 9.1 %copy-start.11 = (f32[32,1,128]{2,1,0:T(1,128)S(1)}, f32[32,1,128]{2,1,0:T(1,128)}, u32[]{:S(2)}) copy-start(f32[32,1,128]{2,1,0:T(1,128)} %get-tuple-element.194) | copy-start | bytes 49156
  278.8 13.5 %collective-permute-start.17 = (bf16[1,96,2432]{2,1,0:T(8,128)(2,1)}, bf16[1,96,2432]{2,1,0:T(8,128)(2,1)S(1)}, u32[]{:S(2)}, u32[]{:S(2)}) collective-permute-start(bf16[1,96,2432]{2,1,0:T(8,128)(2,1)} %constant_dynamic-slice_fusion.1), channel_id=1, source_target_pairs={{0,16},{4,20},{8,24},{12,28},{16,0},{20,4},{24,8},{28,12},{1,17},{... | collective-permute-start | bytes 1400840 | tf_op jit(solution)/shard_map/ppermute | solution.py:13
  281.3 11.0 %collective-permute-start.18 = (bf16[1,96,2304]{2,1,0:T(8,128)(2,1)S(1)}, bf16[1,96,2304]{2,1,0:T(8,128)(2,1)S(1)}, u32[]{:S(2)}, u32[]{:S(2)}) collective-permute-start(bf16[1,96,2304]{2,1,0:T(8,128)(2,1)S(1)} %constant_dynamic-slice_fusion), channel_id=1, source_target_pairs={{0,8},{4,12},{8,0},{12,4},{16,24},{20,28},{24,16},{28,20},{1,9},{5... | collective-permute-start | bytes 1327112 | tf_op jit(solution)/shard_map/ppermute | solution.py:13
  292.4 8.5 %copy-start.8 = (bf16[24,4608]{1,0:T(8,128)(2,1)S(1)}, bf16[24,4608]{1,0:T(8,128)(2,1)}, u32[]{:S(2)}) copy-start(bf16[24,4608]{1,0:T(8,128)(2,1)} %copy-done.7) | copy-start | bytes 663556
  292.4 8.5 %copy-start.10 = (bf16[24,4608]{1,0:T(8,128)(2,1)S(1)}, bf16[24,4608]{1,0:T(8,128)(2,1)}, u32[]{:S(2)}) copy-start(bf16[24,4608]{1,0:T(8,128)(2,1)} %copy-done.9) | copy-start | bytes 663556
  295.2 14.1 %collective-permute-start.21 = (bf16[24,4736]{1,0:T(8,128)(2,1)}, bf16[24,4736]{1,0:T(8,128)(2,1)}, u32[]{:S(2)}, u32[]{:S(2)}) collective-permute-start(bf16[24,4736]{1,0:T(8,128)(2,1)} %pad_maximum_fusion.5), channel_id=1, source_target_pairs={{0,3},{1,2},{2,1},{3,0},{4,7},{5,6},{6,5},{7,4},{8,11},{9,10},{10,... | collective-permute-start | bytes 681992 | tf_op jit(solution)/shard_map/ppermute | solution.py:13
  296.8 19.5 %collective-permute-start.20 = (bf16[24,4736]{1,0:T(8,128)(2,1)}, bf16[24,4736]{1,0:T(8,128)(2,1)}, u32[]{:S(2)}, u32[]{:S(2)}) collective-permute-start(bf16[24,4736]{1,0:T(8,128)(2,1)} %pad_maximum_fusion.4), channel_id=1, source_target_pairs={{0,2},{1,3},{2,0},{3,1},{4,6},{5,7},{6,4},{7,5},{8,10},{9,11},{10,... | collective-permute-start | bytes 681992 | tf_op jit(solution)/shard_map/ppermute | solution.py:13
  299.8 16.5 %collective-permute-start.19 = (bf16[24,4736]{1,0:T(8,128)(2,1)}, bf16[24,4736]{1,0:T(8,128)(2,1)}, u32[]{:S(2)}, u32[]{:S(2)}) collective-permute-start(bf16[24,4736]{1,0:T(8,128)(2,1)} %pad_maximum_fusion.3), channel_id=1, source_target_pairs={{0,1},{1,0},{2,3},{3,2},{4,5},{5,4},{6,7},{7,6},{8,9},{9,8},{10,11... | collective-permute-start | bytes 681992 | tf_op jit(solution)/shard_map/ppermute | solution.py:13
  (25 other events, 71.4 us)
Sparse Core Ops, SparseCore 0:
  12.0 96.3 all-gather.1
  205.0 43.7 reduce-scatter.1
where the time goes:
time: 330 us; the launch traced here: 327 us
  Pallas kernels  151 us (46%)
  waiting for transfers between devices  77.6 us (24%)
  local copies, waits for them, and re-layouts  27.9 us (8%)
  starting transfers between devices  26.2 us (8%)
  other arithmetic  18.2 us (6%)
  between operations  15.2 us (5%)
  blocking collectives  10.4 us (3%)
    ppermute x22, waiting for transfers between devices, swap(): return lax.ppermute(block, axis, [(i, i ^ mask) for i in range(size)])  50.1 us
    pallas_call x1, Pallas kernels, feed_forward(): pl.pallas_call(feed_forward_kernel, grid=(rows // TILE,), in_specs=[pl.Bl...  31.5 us
    all_gather x1, waiting for transfers between devices, shards(): rest_full = lax.all_gather(rest, AXES, axis=0, tiled=True)  27.5 us
    pallas_call x1, Pallas kernels, attention_grad(): pl.pallas_call(functools.partial(attention_grad_kernel, pairs), grid=(row...  26.7 us
    pallas_call x1, Pallas kernels, feed_forward_grad(): pl.pallas_call(feed_forward_grad_kernel, grid=(rows // TILE,), in_specs=[...  25.8 us
    pallas_call x1, Pallas kernels, attention(): pl.pallas_call(functools.partial(attention_kernel, orders, fsdp, small),...  25.7 us
    ppermute x22, starting transfers between devices, swap(): return lax.ppermute(block, axis, [(i, i ^ mask) for i in range(size)])  22.2 us
    pallas_call x1, Pallas kernels, early_grads(): pl.pallas_call(functools.partial(early_kernel, reps), grid=(n,), in_specs...  14.8 us
  transfers between devices with their start and end apart: 25, of which 11 were waited for; matrix products, arithmetic and copies ran while one was open for 8% of the time, Pallas kernels for 24%

commit v1 on v0

--- a/solution.py
+++ b/solution.py
@@ -190,13 +190,20 @@
     return vectors, jnp.sum(jnp.where(fits, spread, 0.0), axis=0, keepdims=True)
 
 
-def attention_kernel(orders,fsdp,small,lens_ref,me_ref,tok_ref,p0,p1,p2,p3,w_ref,vec_ref,mix_ref,ctx_ref,lse_ref,acc_ref,sems):
+EPS=1e-6
+
+def normed(h):
+    c=h-jnp.mean(h,axis=1,keepdims=True)
+    f=lax.rsqrt(jnp.mean(c*c,axis=1,keepdims=True)+EPS)
+    return c*f,f
+
+def attention_kernel(orders,fsdp,small,lens_ref,me_ref,tok_ref,p0,p1,p2,p3,w_ref,vec_ref,mix_ref,ctx_ref,inv_ref,wts_ref,n1_ref,r1_ref,low_ref,acc_ref,sems):
     pack=pl.program_id(0)
     width=tok_ref.shape[1]; wide=3*width
     @pl.when(pack==0)
     def _():
         assemble(me_ref,orders,fsdp,(p0,p1,p2,p3),w_ref,sems)
-        vectors,answer=unpack_small(w_ref[:,wide:],*small)
+        vectors,answer=unpack_small(w_ref[:,wide+width:],*small)
         vec_ref[...]=vectors
         vec_ref[15:16,:LANES]=answer
     query_row=vec_ref[6:7,:]; value_row=vec_ref[7:8,:]
@@ -219,14 +226,19 @@
             s=dot_nt(jnp.concatenate([qm,apart],axis=1),kx)
             m=jnp.max(s,axis=1,keepdims=True)
             w=jnp.exp(s-m).astype(BF16)
+            wts_ref[2*p+half]=w
             o=dot_nn(w,vx)
-            total=o[:,LANES:]
-            outs.append(o[:,:LANES]/total)
-            acc_ref[...]=jnp.where(head_lanes(lane,2*p+half),m+jnp.log(total),acc_ref[...])
+            inv=1.0/o[:,LANES:]
+            outs.append(o[:,:LANES]*inv)
+            acc_ref[...]=jnp.where(head_lanes(lane,2*p+half),inv,acc_ref[...])
         ctx_ref[:,at(0)]=jnp.where(lane<HEAD_DIM,outs[0],outs[1]).astype(BF16)
         return carry
     lax.fori_loop(0,HEADS//2,pair,0)
-    lse_ref[...]=acc_ref[...]
+    inv_ref[...]=acc_ref[...]
+    att=dot_nn(ctx_ref[...],w_ref[:,wide:wide+width])+vec_ref[0:1,:]
+    n1,f1=normed(tok.astype(F32)+att)
+    n1_ref[...]=n1; r1_ref[...]=jnp.broadcast_to(f1,r1_ref.shape)
+    low_ref[...]=(n1*vec_ref[1:2,:]+vec_ref[2:3,:]).astype(BF16)
 
 def attention(lens,me,tok,parts,orders,fsdp,small):
     rows,width=tok.shape; share=parts[0].shape[1]; full=parts[0].shape[2]+parts[2].shape[2]
@@ -240,7 +252,8 @@
     cost=pl.CostEstimate(flops=2*rows*width*wide+8*rows*PACK*width,bytes_accessed=rows*wide*4,transcendentals=HEADS*PACK*rows)
     spec=lambda n: pl.BlockSpec((PACK,n),lambda g:(g,0))
     return pl.pallas_call(functools.partial(attention_kernel,orders,fsdp,small),grid=(rows//PACK,),
-        in_specs=[sm,sm,spec(width)]+[hbm]*4,out_specs=fixed+[spec(n) for n,_ in sizes],out_shape=heads+outs,
+        in_specs=[sm,sm,spec(width)]+[hbm]*4,out_specs=fixed+[spec(n) for n,_ in sizes]+[pl.BlockSpec((HEADS,PACK,PACK),lambda g:(g,0,0)),spec(width),spec(LANES),spec(width)],
+        out_shape=heads+outs+[jax.ShapeDtypeStruct((rows//PACK*HEADS,PACK,PACK),BF16),jax.ShapeDtypeStruct((rows,width),F32),jax.ShapeDtypeStruct((rows,LANES),F32),jax.ShapeDtypeStruct((rows,width),BF16)],
         scratch_shapes=[pltpu.VMEM((PACK,LANES),F32),pltpu.SemaphoreType.DMA((4*parts[0].shape[0],))],
         compiler_params=pltpu.CompilerParams(vmem_limit_bytes=VMEM_MOST),name='attention',cost_estimate=cost)(lens,me,tok,*parts)
 
@@ -250,54 +263,49 @@
     mid=rest.astype(BF16).astype(F32)
     return jnp.where(lane<16,hi,jnp.where(lane<32,mid,jnp.where(lane<48,rest-mid,0.0)))
 
-def attention_grad_kernel(pairs,lens_ref,mix_ref,ctx_ref,dctx_ref,lse_ref,out_ref):
-    g=pl.program_id(0)
+def attention_grad_kernel(mix_ref,ctx_ref,dctx_ref,inv_ref,wts_ref,out_ref,de_ref):
+    p=pl.program_id(1)
     width=ctx_ref.shape[1]
-    part=(pairs[1]-pairs[0])*LANES
-    lane,apart,own=segment_tiles(lens_ref,g)
-    prod=dctx_ref[...].astype(F32)*ctx_ref[...].astype(F32)
-    hi=prod.astype(BF16); lo=(prod-hi.astype(F32)).astype(BF16)
-    wr=lax.broadcasted_iota(jnp.int32,(width,LANES),0); wl=lax.broadcasted_iota(jnp.int32,(width,LANES),1)
-    pick=jnp.where(jnp.logical_and(wl<48,wl%16==wr//HEAD_DIM),1.0,0.0).astype(BF16)
-    dots=dot_nn(hi,pick)+dot_nn(lo,pick)
-    qe=(apart-split_three(lse_ref[...],lane)).astype(BF16)
-    de=(-split_three(dots,lane)).astype(BF16)
-    def pair(p,carry):
-        at=lambda base: pl.ds(pl.multiple_of(base+p*LANES,LANES),LANES)
-        q2=mix_ref[:,at(0)]; k2=mix_ref[:,at(width)]; v2=mix_ref[:,at(2*width)]; d2=dctx_ref[:,at(0)]
-        kt=k2.T
-        dk=jnp.zeros((PACK,LANES),F32); dv=jnp.zeros((PACK,LANES),F32); dqs=[]
-        for half in range(2):
-            here=lane//HEAD_DIM==half
-            qm=jnp.where(here,q2,jnp.zeros_like(q2)); dm=jnp.where(here,d2,jnp.zeros_like(d2))
-            mark=jnp.where(head_lanes(lane,2*p+half),1.0,0.0)
-            kx=jnp.concatenate([k2,(own+mark).astype(BF16)],axis=1)
-            vx=jnp.concatenate([v2,mark.astype(BF16)],axis=1)
-            st=dot_nt(kx,jnp.concatenate([qm,qe],axis=1))
-            pt=jnp.exp(st)
-            dpt=dot_nt(vx,jnp.concatenate([dm,de],axis=1))
-            ds=(pt*dpt).astype(BF16)
-            dv=dv+dot_nn(pt.astype(BF16),dm)
-            dk=dk+dot_nn(ds,qm)
-            dqs.append(dot_nn(kt[half*HEAD_DIM:(half+1)*HEAD_DIM],ds))
-        dq=jnp.concatenate(dqs,axis=0).T*(1/math.sqrt(HEAD_DIM))
-        to=lambda base: pl.ds(pl.multiple_of(base+(p-pairs[0])*LANES,LANES),LANES)
-        out_ref[:,to(0)]=dq.astype(BF16)
-        out_ref[:,to(part)]=dk.astype(BF16)
-        out_ref[:,to(2*part)]=dv.astype(BF16)
-        return carry
-    lax.fori_loop(pairs[0],pairs[1],pair,0)
-
-def attention_grad(pairs,lens,mix,ctx,dctx,lse):
-    rows,width=ctx.shape; wide=mix.shape[1]; part=3*(pairs[1]-pairs[0])*LANES
-    b=lambda n: pl.BlockSpec((PACK,n),lambda g:(g,0))
-    share=(pairs[1]-pairs[0])/(HEADS//2)
-    return pl.pallas_call(functools.partial(attention_grad_kernel,pairs),grid=(rows//PACK,),
-        in_specs=[pl.BlockSpec(memory_space=pltpu.SMEM),b(wide),b(width),b(width),b(LANES)],
-        out_specs=b(part),out_shape=jax.ShapeDtypeStruct((rows,part),BF16),
+    lane=lax.broadcasted_iota(jnp.int32,(PACK,LANES),1)
+    @pl.when(p==0)
+    def _():
+        prod=dctx_ref[...].astype(F32)*ctx_ref[...].astype(F32)
+        hi=prod.astype(BF16); lo=(prod-hi.astype(F32)).astype(BF16)
+        wr=lax.broadcasted_iota(jnp.int32,(width,LANES),0); wl=lax.broadcasted_iota(jnp.int32,(width,LANES),1)
+        pick=jnp.where(jnp.logical_and(wl<48,wl%16==wr//HEAD_DIM),1.0,0.0).astype(BF16)
+        dots=(dot_nn(hi,pick)+dot_nn(lo,pick))*inv_ref[...]
+        de_ref[...]=(-split_three(dots,lane)).astype(BF16)
+    at=lambda base: pl.ds(pl.multiple_of(base+p*LANES,LANES),LANES)
+    q2=mix_ref[:,at(0)]; k2=mix_ref[:,at(width)]; v2=mix_ref[:,at(2*width)]; d2=dctx_ref[:,at(0)].astype(F32)
+    invs=[jnp.sum(jnp.where(lane==2*p+half,inv_ref[...],0.0),axis=1,keepdims=True) for half in range(2)]
+    d2=(d2*jnp.where(lane<HEAD_DIM,invs[0],invs[1])).astype(BF16)
+    qt=q2.T; dt=d2.T
+    de=de_ref[...]
+    dq=[]; dks=[]; dvs=[]
+    for half in range(2):
+        here=lane//HEAD_DIM==half
+        dm=jnp.where(here,d2,jnp.zeros_like(d2))
+        mark=jnp.where(head_lanes(lane,2*p+half),1.0,0.0).astype(BF16)
+        w=wts_ref[half]
+        dp=dot_nt(jnp.concatenate([dm,de],axis=1),jnp.concatenate([v2,mark],axis=1))
+        ds=(w.astype(F32)*dp).astype(BF16)
+        rows=slice(half*HEAD_DIM,(half+1)*HEAD_DIM)
+        dq.append(dot_nn(ds,k2))
+        dks.append(dot_nn(qt[rows],ds))
+        dvs.append(dot_nn(dt[rows],w))
+    out_ref[:,at(0)]=(jnp.where(lane<HEAD_DIM,dq[0],dq[1])*(1/math.sqrt(HEAD_DIM))).astype(BF16)
+    out_ref[:,at(width)]=jnp.concatenate(dks,axis=0).T.astype(BF16)
+    out_ref[:,at(2*width)]=jnp.concatenate(dvs,axis=0).T.astype(BF16)
+
+def attention_grad(mix,ctx,dctx,inv,wts):
+    rows,width=ctx.shape; wide=mix.shape[1]; pairs=HEADS//2
+    b=lambda n: pl.BlockSpec((PACK,n),lambda g,p:(g,0))
+    return pl.pallas_call(attention_grad_kernel,grid=(rows//PACK,pairs),
+        in_specs=[b(wide),b(width),b(width),b(LANES),pl.BlockSpec((2,PACK,PACK),lambda g,p:(g*pairs+p,0,0))],
+        out_specs=b(wide),out_shape=jax.ShapeDtypeStruct((rows,wide),BF16),
+        scratch_shapes=[pltpu.VMEM((PACK,LANES),BF16)],
         compiler_params=pltpu.CompilerParams(vmem_limit_bytes=VMEM_MOST),name='attention_grad',
-        cost_estimate=pl.CostEstimate(flops=int(share*20*rows*PACK*width),bytes_accessed=rows*wide*4,transcendentals=int(share*HEADS*rows*PACK)))(lens,mix,ctx,dctx,lse)
-EPS=1e-6
+        cost_estimate=pl.CostEstimate(flops=16*rows*PACK*width,bytes_accessed=rows*wide*8,transcendentals=0))(mix,ctx,dctx,inv,wts)
 TILE=256
 def half_tail(a, e):
     t=1.0/(1.0+0.3275911*a)
@@ -310,11 +318,6 @@
     h=half_tail(z,e)
     phi=jnp.where(x>0,1.0-h,h)
     return x*phi, phi+x*(e*(1/math.sqrt(2*math.pi)))
-
-def normed(h):
-    c=h-jnp.mean(h,axis=1,keepdims=True)
-    f=lax.rsqrt(jnp.mean(c*c,axis=1,keepdims=True)+EPS)
-    return c*f,f
 
 def norm_back(e,n,f):
     return f*(e-jnp.mean(e,axis=1,keepdims=True)-n*jnp.mean(e*n,axis=1,keepdims=True))
@@ -331,17 +334,13 @@
             seg=seg+(row>=end).astype(jnp.int32)
     return seg==lane
 
-def feed_forward_kernel(lens_ref,ctx_ref,tok_ref,w_ref,vec_ref,n1_ref,r1_ref,low_ref,act_ref,dg_ref,n2_ref,r2_ref,res_ref,span_ref,score_ref,doc_ref,all_ref):
+def feed_forward_kernel(lens_ref,n1_ref,low_ref,w_ref,vec_ref,act_ref,dg_ref,n2_ref,r2_ref,res_ref,span_ref,score_ref,doc_ref,all_ref):
     i=pl.program_id(0)
-    width=ctx_ref.shape[1]; rows=ctx_ref.shape[0]; reps=act_ref.shape[1]//width
+    rows,width=n1_ref.shape; reps=act_ref.shape[1]//width
     vec=lambda k: vec_ref[k:k+1,:]
     base=2*reps*width
-    att=dot_nn(ctx_ref[...],w_ref[:,base:base+width])+vec(0)
-    n1,f1=normed(tok_ref[...].astype(F32)+att)
-    n1_ref[...]=n1; r1_ref[...]=jnp.broadcast_to(f1,(rows,LANES))
-    first=n1*vec(1)+vec(2)
-    low=first.astype(BF16); low_ref[...]=low
-    out=first+vec(3)
+    low=low_ref[...]
+    out=n1_ref[...]*vec(1)+vec(2)+vec(3)
     for q in range(reps):
         c=slice(q*width,(q+1)*width)
         x=dot_nn(low,w_ref[:,c])+vec(8+q)
@@ -353,7 +352,7 @@
     n2_ref[...]=n2; r2_ref[...]=jnp.broadcast_to(f2,(rows,LANES))
     res=(n2*vec(4)+vec(5)).astype(BF16)
     res_ref[...]=res
-    span=dot_nn(res,w_ref[:,base+width:base+width+LANES])
+    span=dot_nn(res,w_ref[:,base:base+LANES])
     span_ref[...]=span
     score=jnp.broadcast_to(jnp.sum(span*vec_ref[15:16,:LANES],axis=1,keepdims=True),(rows,LANES))
     score_ref[...]=score
@@ -367,18 +366,18 @@
         real=lax.broadcasted_iota(jnp.int32,(1,LANES),1)<lens_ref.shape[0]*SEGS_PACK
         doc_ref[...]=jnp.where(real,top+jnp.log(jnp.where(real,total,1.0)),MASKED)
 
-def feed_forward(lens,ctx,tok,w,vec,reps):
-    rows,width=ctx.shape; ff=reps*width
+def feed_forward(lens,n1,low,w,vec,reps):
+    rows,width=n1.shape; ff=reps*width
     b=lambda n: pl.BlockSpec((TILE,n),lambda i:(i,0))
     s=lambda n,t: jax.ShapeDtypeStruct((rows,n),t)
     return pl.pallas_call(feed_forward_kernel,grid=(rows//TILE,),
         in_specs=[pl.BlockSpec(memory_space=pltpu.SMEM),b(width),b(width),once(w.shape),once(vec.shape)],
-        out_specs=[b(width),b(LANES),b(width),b(ff),b(ff),b(width),b(LANES),b(width),b(LANES),b(LANES),once((1,LANES))],
-        out_shape=[s(width,F32),s(LANES,F32),s(width,BF16),s(ff,BF16),s(ff,BF16),s(width,F32),s(LANES,F32),s(width,BF16),s(LANES,F32),s(LANES,F32),jax.ShapeDtypeStruct((1,LANES),F32)],
+        out_specs=[b(ff),b(ff),b(width),b(LANES),b(width),b(LANES),b(LANES),once((1,LANES))],
+        out_shape=[s(ff,BF16),s(ff,BF16),s(width,F32),s(LANES,F32),s(width,BF16),s(LANES,F32),s(LANES,F32),jax.ShapeDtypeStruct((1,LANES),F32)],
         scratch_shapes=[pltpu.VMEM((rows,LANES),F32)],
-        compiler_params=pltpu.CompilerParams(vmem_limit_bytes=VMEM_MOST),name='feed_forward')(lens,ctx,tok,w,vec)
-
-def feed_forward_grad_kernel(lens_ref,own_ids_ref,doc_ref,scores_ref,ids_ref,cot_ref,n2_ref,r2_ref,res_ref,span_ref,score_ref,dg_ref,n1_ref,r1_ref,w_ref,vec_ref,
+        compiler_params=pltpu.CompilerParams(vmem_limit_bytes=VMEM_MOST),name='feed_forward')(lens,n1,low,w,vec)
+
+def feed_forward_grad_kernel(lens_ref,own_ids_ref,doc_ref,scores_ref,ids_ref,cot_ref,n2_ref,r2_ref,res_ref,span_ref,score_ref,dg_ref,n1_ref,r1_ref,w_ref,aw_ref,vec_ref,
                    olow_ref,ilow_ref,alow_ref,fsum_ref,dctx_ref,small_ref,spanw_ref,weight_ref,acc_ref):
     i=pl.program_id(0); last=pl.num_programs(0)-1
     rows,width=cot_ref.shape; reps=dg_ref.shape[1]//width
@@ -408,7 +407,7 @@
     @pl.when(i==last)
     def _():
         spanw_ref[...]=acc_ref[...].astype(BF16)
-    rg=cot_ref[...].astype(F32)+dot_nt(sg,w_ref[:,base+width:base+width+LANES])
+    rg=cot_ref[...].astype(F32)+dot_nt(sg,w_ref[:,base:base+LANES])
     n2=n2_ref[...]
     def colsum(k,v):
         small_ref[k:k+1,:]+=jnp.sum(v,axis=0,keepdims=True)
@@ -429,19 +428,19 @@
     fsum_ref[...]=fsum
     alow=fsum.astype(BF16); alow_ref[...]=alow
     colsum(5,alow.astype(F32))
-    dctx_ref[...]=dot_nt(alow,w_ref[:,base:base+width]).astype(BF16)
-
-def feed_forward_grad(lens,own_ids,doc,scores,ids,cot,n2,r2,res,span,score,dg,n1,r1,w,vec):
+    dctx_ref[...]=dot_nt(alow,aw_ref[...]).astype(BF16)
+
+def feed_forward_grad(lens,own_ids,doc,scores,ids,cot,n2,r2,res,span,score,dg,n1,r1,w,mix,vec):
     rows,width=cot.shape; ff=dg.shape[1]
     b=lambda n: pl.BlockSpec((TILE,n),lambda i:(i,0))
     s=lambda n,t: jax.ShapeDtypeStruct((rows,n),t)
     sm=pl.BlockSpec(memory_space=pltpu.SMEM)
     return pl.pallas_call(feed_forward_grad_kernel,grid=(rows//TILE,),
-        in_specs=[sm,sm,once(doc.shape),once(scores.shape),once(ids.shape),b(width),b(width),b(LANES),b(width),b(LANES),b(LANES),b(ff),b(width),b(LANES),once(w.shape),once(vec.shape)],
+        in_specs=[sm,sm,once(doc.shape),once(scores.shape),once(ids.shape),b(width),b(width),b(LANES),b(width),b(LANES),b(LANES),b(ff),b(width),b(LANES),once(w.shape),pl.BlockSpec((width,width),lambda i:(0,3),pipeline_mode=pl.Buffered(1)),once(vec.shape)],
         out_specs=[b(width),b(ff),b(width),b(width),b(width),once(vec.shape),once((width,LANES))],
         out_shape=[s(width,BF16),s(ff,BF16),s(width,BF16),s(width,F32),s(width,BF16),jax.ShapeDtypeStruct(vec.shape,F32),jax.ShapeDtypeStruct((width,LANES),BF16)],
         scratch_shapes=[pltpu.VMEM((1,LANES),F32),pltpu.VMEM((width,LANES),F32)],
-        compiler_params=pltpu.CompilerParams(vmem_limit_bytes=VMEM_MOST),name='feed_forward_grad')(lens,own_ids,doc,scores,ids,cot,n2,r2,res,span,score,dg,n1,r1,w,vec)
+        compiler_params=pltpu.CompilerParams(vmem_limit_bytes=VMEM_MOST),name='feed_forward_grad')(lens,own_ids,doc,scores,ids,cot,n2,r2,res,span,score,dg,n1,r1,w,mix,vec)
 
 def put_blocks(me_ref,keep_ref,give_ref,value,at):
     blocks,rows,_=keep_ref.shape
@@ -456,11 +455,18 @@
         def _():
             keep_ref[t,:,at]=high; give_ref[t,:,at]=low
 
-def early_kernel(reps,me_ref,low_ref,ilow_ref,act_ref,olow_ref,ctx_ref,alow_ref,keep_ref,give_ref):
+def early_kernel(reps,me_ref,low_ref,ilow_ref,act_ref,olow_hbm,ctx_hbm,alow_hbm,keep_ref,give_ref,olow_ref,ctx_ref,alow_ref,sems):
     j=pl.program_id(0); last=pl.num_programs(0)-1
+    moves=[pltpu.make_async_copy(src,dst,sems.at[k]) for k,(src,dst) in enumerate(((olow_hbm,olow_ref),(ctx_hbm,ctx_ref),(alow_hbm,alow_ref)))]
     put=lambda value: put_blocks(me_ref,keep_ref,give_ref,value,slice(None))
+    @pl.when(j==0)
+    def _():
+        for move in moves: move.start()
     @pl.when(j<reps)
     def _(): put(dot_tn(low_ref[...],ilow_ref[...]))
+    @pl.when(j==reps)
+    def _():
+        for move in moves: move.wait()
     @pl.when(jnp.logical_and(j>=reps,j<last))
     def _(): put(dot_tn(act_ref[...],olow_ref[...]))
     @pl.when(j==last)
@@ -475,8 +481,8 @@
     full=once((rows,width)); n=reps+outer_blocks+1
     specs,shapes=split_outs(dp,width,n)
     return pl.pallas_call(functools.partial(early_kernel,reps),grid=(n,),
-        in_specs=[pl.BlockSpec(memory_space=pltpu.SMEM),full,pl.BlockSpec((rows,width),lambda j:(0,jnp.minimum(j,reps-1))),pl.BlockSpec((rows,width),lambda j:(0,jnp.clip(j-reps,0,outer_blocks-1))),full,full,full],
-        out_specs=specs,out_shape=shapes,
+        in_specs=[pl.BlockSpec(memory_space=pltpu.SMEM),full,pl.BlockSpec((rows,width),lambda j:(0,jnp.minimum(j,reps-1))),pl.BlockSpec((rows,width),lambda j:(0,jnp.clip(j-reps,0,outer_blocks-1)))]+[pl.BlockSpec(memory_space=pl.ANY)]*3,
+        out_specs=specs,out_shape=shapes,scratch_shapes=[pltpu.VMEM((rows,width),BF16)]*3+[pltpu.SemaphoreType.DMA((3,))],
         compiler_params=pltpu.CompilerParams(vmem_limit_bytes=VMEM_MOST),name='early_weight_grads',
         cost_estimate=pl.CostEstimate(flops=2*rows*width*width*n,bytes_accessed=rows*width*n*4,transcendentals=0))(me,low,ilow,act,olow,ctx,alow)
 
@@ -528,7 +534,7 @@
     rows,width=fs.shape
     b=lambda n: pl.BlockSpec((TILE,n),lambda i:(i,0))
     return pl.pallas_call(functools.partial(input_kernel,[m.shape[1]//3 for m in mgs]),grid=(rows//TILE,),
-        in_specs=[once(w.shape),b(width)]+[b(m.shape[1]) for m in mgs],out_specs=b(width),out_shape=jax.ShapeDtypeStruct((rows,width),F32),
+        in_specs=[once((width,3*width)),b(width)]+[b(m.shape[1]) for m in mgs],out_specs=b(width),out_shape=jax.ShapeDtypeStruct((rows,width),F32),
         compiler_params=pltpu.CompilerParams(vmem_limit_bytes=VMEM_MOST),name='input_grad',
         cost_estimate=pl.CostEstimate(flops=6*rows*width*width,bytes_accessed=rows*width*16,transcendentals=0))(w,fs,*mgs)
 AXES = ("dp", "fsdp")
@@ -595,10 +601,10 @@
     orders = bit_orders(lax.axis_size("dp"))
     fsdp = lax.axis_size("fsdp")
     me = jnp.stack([lax.axis_index("dp"), lax.axis_index("fsdp")]).astype(jnp.int32)
-    mix = jnp.concatenate([qkv_weight, packed], axis=1)
+    mix = jnp.concatenate([qkv_weight, attn_weight, packed], axis=1)
     mix_near = gather_near(mix)
     near = len(mix_near)
-    mix_walk = Gathering(mix_near, orders, qkv_weight.shape[1] // 2)
+    mix_walk = Gathering(mix_near, orders, 2 * width)
     mix_walk.advance(0)
     mix_walk.send()
     mix_parts = mix_walk.parts()
@@ -606,26 +612,22 @@
         inner_weight.reshape(share, devices, reps, share).transpose(0, 2, 1, 3).reshape(share, ff)
     )
     outer_blocks = [outer_weight[q * share : (q + 1) * share] for q in range(reps)]
-    rest = jnp.concatenate([inner_turned] + outer_blocks + [attn_weight, span_weight], axis=1)
+    rest = jnp.concatenate([inner_turned] + outer_blocks + [span_weight], axis=1)
     rest_full = lax.all_gather(rest, AXES, axis=0, tiled=True)
 
-    mix_full, vectors, mixed, context, logsum = attention(
-        doc_lengths, me, tokens, mix_parts, orders, near, (share, rows_in, answers)
-    )
     (
+        mix_full,
+        vectors,
+        mixed,
+        context,
+        inverse,
+        weights,
         normed_one,
         factor_one,
         first_low,
-        active,
-        gelu_slope,
-        normed_two,
-        factor_two,
-        result,
-        span_rows,
-        token_score,
-        doc_score,
-    ) = feed_forward(
-        doc_lengths, context, tokens, rest_full, vectors, reps
+    ) = attention(doc_lengths, me, tokens, mix_parts, orders, near, (share, rows_in, answers))
+    active, gelu_slope, normed_two, factor_two, result, span_rows, token_score, doc_score = (
+        feed_forward(doc_lengths, normed_one, first_low, rest_full, vectors, reps)
     )
     exchanged = to_all(jnp.concatenate([doc_score, id_row], axis=0), devices)
     scores_all, ids_all = exchanged[:, 0], exchanged[:, 1]
@@ -647,6 +649,7 @@
             normed_one,
             factor_one,
             rest_full,
+            mix_full,
             vectors,
         )
     )
@@ -670,7 +673,7 @@
         tiled=True,
     )
     context_grad, early = tie(context_grad, early)
-    mixed_grad = attention_grad((0, HEADS // 2), doc_lengths, mixed, context, context_grad, logsum)
+    mixed_grad = attention_grad(mixed, context, context_grad, inverse, weights)
     mixed_grad, outer_walk.came = tie(mixed_grad, outer_walk.came)
     *late, bias_sums = late_grads(me, tokens, mixed_grad, span_grad, dp)
     late, outer_walk.came = tie(late, outer_walk.came)

time: 330 us -> 321 us (0.973)
  waiting for transfers between devices: 77.6 us -> 66.9 us
  starting transfers between devices: 26.2 us -> 29.8 us
    all_gather x1, waiting for transfers between devices: 27.5 us -> 11.1 us  [shards(): rest_full = lax.all_gather(rest, AXES, axis=0, tiled=True)]
    ppermute x22, waiting for transfers between devices: 50.1 us -> 55.7 us  [swap(): return lax.ppermute(block, axis, [(i, i ^ mask) for i in range(size)])]
    pallas_call x1, Pallas kernels: 25.7 us -> 30.8 us  [attention(): pl.pallas_call(functools.partial(attention_kernel, orders, fsdp, small),...]
    pallas_call x1, Pallas kernels: 31.5 us -> 27.6 us  [feed_forward(): pl.pallas_call(feed_forward_kernel, grid=(rows // TILE,), in_specs=[pl.Bl...]
  transfers between devices with their start and end apart: 25 -> 25, of which waited for: 11 -> 11; matrix products, arithmetic and copies ran while one was open for 8% -> 8% of each run, Pallas kernels for 24% -> 26%
where the time goes in v1:
time: 321 us; the launch traced here: 316 us
  Pallas kernels  149 us (46%)
  waiting for transfers between devices  66.9 us (21%)
  starting transfers between devices  29.8 us (9%)
  local copies, waits for them, and re-layouts  27.1 us (8%)
  other arithmetic  18.4 us (6%)
  between operations  15.1 us (5%)
  blocking collectives  10.5 us (3%)
    ppermute x22, waiting for transfers between devices, swap(): return lax.ppermute(block, axis, [(i, i ^ mask) for i in range(size)])  55.7 us
    pallas_call x1, Pallas kernels, attention(): pl.pallas_call(functools.partial(attention_kernel, orders, fsdp, small),...  30.8 us
    pallas_call x1, Pallas kernels, feed_forward(): pl.pallas_call(feed_forward_kernel, grid=(rows // TILE,), in_specs=[pl.Bl...  27.6 us
    pallas_call x1, Pallas kernels, feed_forward_grad(): pl.pallas_call(feed_forward_grad_kernel, grid=(rows // TILE,), in_specs=[...  25.8 us
    pallas_call x1, Pallas kernels, attention_grad(): pl.pallas_call(attention_grad_kernel, grid=(rows // PACK, pairs), in_spec...  24.2 us
    ppermute x22, starting transfers between devices, swap(): return lax.ppermute(block, axis, [(i, i ^ mask) for i in range(size)])  24 us
    pallas_call x1, Pallas kernels, early_grads(): pl.pallas_call(functools.partial(early_kernel, reps), grid=(n,), in_specs...  13.7 us
    all_gather x1, waiting for transfers between devices, shards(): rest_full = lax.all_gather(rest, AXES, axis=0, tiled=True)  11.1 us
  transfers between devices with their start and end apart: 25, of which 11 were waited for; matrix products, arithmetic and copies ran while one was open for 8% of the time, Pallas kernels for 26%

profile of v1, /device:TPU:0, one launch (start us, length us, event | category | flops | bytes accessed | tf_op | source)
XLA Modules:
  0.0 316.3 jit_solution(3267881034149464719)
XLA Ops:
  7.2 2.1 reshape.111
  12.1 3.1 collective-permute-start
  15.2 2.6 collective-permute-start.1
  17.9 10.3 %collective-permute-done.2 = bf16[24,3200]{1,0:T(8,128)(2,1)S(1)} collective-permute-done((bf16[24,3200]{1,0:T(8,128)(2,1)S(1)}, bf16[24,3200]{1,0:T(8,128)(2,1)S(1)}, u32[]{:S(2)}, u32[]{:S(2)}) %collective-permute-start.2) | collective-permute-done | bytes 153632 | tf_op jit(solution)/shard_map/ppermute | solution.py:13
  28.2 4.4 %collective-permute-done.1 = bf16[24,3200]{1,0:T(8,128)(2,1)S(1)} collective-permute-done((bf16[24,3200]{1,0:T(8,128)(2,1)S(1)}, bf16[24,3200]{1,0:T(8,128)(2,1)S(1)}, u32[]{:S(2)}, u32[]{:S(2)}) %collective-permute-start.1) | collective-permute-done | bytes 153632 | tf_op jit(solution)/shard_map/ppermute | solution.py:13
  34.3 1.6 collective-permute-start.3
  36.0 5.9 %collective-permute-done.6 = bf16[4,24,1664]{2,1,0:T(8,128)(2,1)S(1)} collective-permute-done((bf16[4,24,1664]{2,1,0:T(8,128)(2,1)S(1)}, bf16[4,24,1664]{2,1,0:T(8,128)(2,1)S(1)}, u32[]{:S(2)}, u32[]{:S(2)}) %collective-permute-start.6) | collective-permute-done | bytes 319520 | tf_op jit(solution)/shard_map/ppermute | solution.py:13
  41.9 1.9 collective-permute-start.7
  44.3 1.8 collective-permute-start.4
  46.2 11.1 %collective-permute-done.7 = bf16[8,24,1664]{2,1,0:T(8,128)(2,1)S(1)} collective-permute-done((bf16[8,24,1664]{2,1,0:T(8,128)(2,1)S(1)}, bf16[8,24,1664]{2,1,0:T(8,128)(2,1)S(1)}, u32[]{:S(2)}, u32[]{:S(2)}) %collective-permute-start.7) | collective-permute-done | bytes 639008 | tf_op jit(solution)/shard_map/ppermute | solution.py:13
  57.5 3.5 %collective-permute-done.4 = bf16[8,24,1536]{2,1,0:T(8,128)(2,1)S(1)} collective-permute-done((bf16[8,24,1536]{2,1,0:T(8,128)(2,1)S(1)}, bf16[8,24,1536]{2,1,0:T(8,128)(2,1)S(1)}, u32[]{:S(2)}, u32[]{:S(2)}) %collective-permute-start.4) | collective-permute-done | bytes 589856 | tf_op jit(solution)/shard_map/ppermute | solution.py:13
  61.8 2.2 collective-permute-done.5.p1
  64.1 30.8 %attention.1 = (bf16[768,3200]{1,0:T(8,128)(2,1)}, f32[16,768]{1,0:T(8,128)}, bf16[1024,2304]{1,0:T(8,128)(2,1)}, bf16[1024,768]{1,0:T(8,128)(2,1)}, f32[1024,12...) custom-call(s32[2,4]{1,0:T(2,128)} %lens_ref.5, ...), custom_call_target="tpu_custom_call" | custom-call | flops 6845104128 | bytes 9437184 | tf_op jit(solution)/shard_map/attention/pallas_call | solution.py:254
  94.9 11.1 %all-gather.2.cloned.1.call-done.w_ref = bf16[768,6272]{1,0:T(8,128)(2,1)} async-done(((bf16[24,6272]{1,0:T(8,128)(2,1)}), bf16[768,6272]{1,0:T(8,128)(2,1)}) %all-gather.2.cloned.1.call-update) | async-done | bytes 9633808 | tf_op jit(solution)/shard_map/all_gather | solution.py:616
  106.0 27.6 %feed_forward.1 = (bf16[1024,3072]{1,0:T(8,128)(2,1)}, bf16[1024,3072]{1,0:T(8,128)(2,1)}, f32[1024,768]{1,0:T(8,128)}, f32[1024,128]{1,0:T(8,128)}, bf16[1024,7...) custom-call(s32[2,4]{1,0:T(2,128)} %lens_ref.5, ...), custom_call_target="tpu_custom_call" | custom-call | tf_op jit(solution)/shard_map/feed_forward/pallas_call | solution.py:373
  134.3 10.5 %all_to_all.10 = f32[32,2,128]{2,1,0:T(2,128)S(1)} all-to-all(f32[32,2,128]{2,1,0:T(2,128)S(1)} %broadcast_in_dim.25), channel_id=1, replica_groups=mesh['dp'=8,'fsdp'=4] {'dp','fsdp'}, dimensions={0} | all-to-all | bytes 65536 | tf_op jit(solution)/shard_map/all_to_all | solution.py:558
  145.4 25.8 %feed_forward_grad.1 = (bf16[1024,768]{1,0:T(8,128)(2,1)}, bf16[1024,3072]{1,0:T(8,128)(2,1)}, bf16[1024,768]{1,0:T(8,128)(2,1)}, f32[1024,768]{1,0:T(8,128)}, b...) custom-call(s32[2,4]{1,0:T(2,128)} %lens_ref.5, s32[8]{0:T(128)} %bitcast.128, ...), custom_call_target="tpu_custom_call" | custom-call | tf_op jit(solution)/shard_map/feed_forward_grad/pallas_call | solution.py:438
  171.3 13.7 %early_weight_grads.1 = (bf16[4,96,4608]{2,1,0:T(8,128)(2,1)}, bf16[4,96,4608]{2,1,0:T(8,128)(2,1)}) custom-call(s32[2]{0:T(128)} %pad_add_fusion.me_ref, bf16[1024,768]{1,0:T(8,128)(2,1)} %get-tuple-element.87.low_ref, bf16[1024,3072]{1,0:T(8,128)(2,1)} %get-tuple-element.104.ilow_ref, bf16[1024,3072]{1,0:T(8,128)(2,1)} %get-tuple-element.105.act_ref, ...), custom_call_target="tpu_custom_call" | custom-call | flops 7247757312 | bytes 18874368 | tf_op jit(solution)/shard_map/early_weight_grads/pallas_call | solution.py:483
  185.1 8.1 %outer_weight_grad.1 = (bf16[4,96,2304]{2,1,0:T(8,128)(2,1)}, bf16[4,96,2304]{2,1,0:T(8,128)(2,1)}) custom-call(s32[2]{0:T(128)} %pad_add_fusion.me_ref, bf16[1024,3072]{1,0:T(8,128)(2,1)} %get-tuple-element.105.act_ref, bf16[1024,768]{1,0:T(8,128)(2,1)} %get-tuple-element.110.olow_hbm.olow_ref), custom_call_target="tpu_custom_call" | custom-call | flops 3623878656 | bytes 9437184 | tf_op jit(solution)/shard_map/outer_weight_grad/pallas_call | solution.py:495
  193.1 4.6 %add_convert_fusion = bf16[4,96,4608]{2,1,0:T(8,128)(2,1)} fusion(bf16[4,96,4608]{2,1,0:T(8,128)(2,1)} %collective-permute-done.9, bf16[4,96,4608]{2,1,0:T(8,128)(2,1)S(1)} %copy-done), kind=kLoop, calls=%fused_computation | loop fusion | flops 7077888 | bytes 10616832 | tf_op jit(solution)/shard_map/convert_element_type | solution.py:65
  199.7 24.2 %attention_grad.1.mg_ref.refs_0_ = bf16[1024,2304]{1,0:T(8,128)(2,1)} custom-call(bf16[1024,2304]{1,0:T(8,128)(2,1)} %get-tuple-element.100.mix_ref, bf16[1024,768]{1,0:T(8,128)(2,1)} %get-tuple-element.101.ctx_hbm.ctx_ref, bf16[1024,768]{1,0:T(8,128)(2,1)} %get-tuple-element.113.dctx_ref, f32[1024,128]{1,0:T(8,128)} %get-tuple-element.114.inv_ref, ...), custom_call_target="tpu_custom_call" | custom-call | flops 6442450944 | bytes 18874368 | tf_op jit(solution)/shard_map/attention_grad/pallas_call | solution.py:303
  224.0 9.5 %late_weight_grads.1 = (bf16[4,96,2432]{2,1,0:T(8,128)(2,1)}, bf16[4,96,2432]{2,1,0:T(8,128)(2,1)}, f32[8,2304]{1,0:T(8,128)}) custom-call(s32[2]{0:T(128)} %pad_add_fusion.me_ref, bf16[1024,768]{1,0:T(8,128)(2,1)} %tok_ref.3, bf16[1024,2304]{1,0:T(8,128)(2,1)} %attention_grad.1.mg_ref.refs_0_, bf16[768,128]{1,0:T(8,128)(2,1)} %get-tuple-element.118.span_ref), custom_call_target="tpu_custom_call" | custom-call | flops 3623878656 | bytes 9437184 | tf_op jit(solution)/shard_map/late_weight_grads/pallas_call | solution.py:515
  236.3 2.5 add_convert_fusion.2
  242.3 2.1 dynamic-slice_bitcast_fusion.4
  245.3 3.5 %collective-permute-start.13 = (bf16[24,4608]{1,0:T(8,128)(2,1)}, bf16[24,4608]{1,0:T(8,128)(2,1)S(1)}, u32[]{:S(2)}, u32[]{:S(2)}) collective-permute-start(bf16[24,4608]{1,0:T(8,128)(2,1)} %get-tuple-element.159), channel_id=1, source_target_pairs={{0,2},{1,3},{2,0},{3,1},{4,6},{5,7},{6,4},{7,5},{8,10},{9,11},{10,... | collective-permute-start | bytes 663560 | tf_op jit(solution)/shard_map/ppermute | solution.py:13
  248.8 8.8 %input_grad.1 = f32[1024,768]{1,0:T(8,128)} custom-call(bf16[768,3200]{1,0:T(8,128)(2,1)} %get-tuple-element.97.aw_ref.w_ref, f32[1024,768]{1,0:T(8,128)} %get-tuple-element.131.fs_ref, bf16[1024,2304]{1,0:T(8,128)(2,1)} %attention_grad.1.mg_ref.refs_0_), custom_call_target="tpu_custom_call" | custom-call | flops 3623878656 | bytes 12582912 | tf_op jit(solution)/shard_map/input_grad/pallas_call | solution.py:536
  257.6 5.8 %all-to-all-start.1 = ((f32[32,4,128]{2,1,0:T(4,128)}), f32[32,4,128]{2,1,0:T(4,128)S(1)}, u32[]{:S(2)}, u32[]{:S(2)}) async-start(f32[32,4,128]{2,1,0:T(4,128)} %reshape.116), calls=%async_computation.2 | async-start | bytes 131072 | tf_op jit(solution)/shard_map/all_to_all | solution.py:704
  263.6 1.7 collective-permute-done.15
  272.6 9.7 %collective-permute-done.18 = bf16[1,96,2304]{2,1,0:T(8,128)(2,1)S(1)} collective-permute-done((bf16[1,96,2304]{2,1,0:T(8,128)(2,1)S(1)}, bf16[1,96,2304]{2,1,0:T(8,128)(2,1)S(1)}, u32[]{:S(2)}, u32[]{:S(2)}) %collective-permute-start.18) | collective-permute-done | bytes 442400 | tf_op jit(solution)/shard_map/ppermute | solution.py:13
  285.2 3.4 %collective-permute-start.21 = (bf16[24,4736]{1,0:T(8,128)(2,1)}, bf16[24,4736]{1,0:T(8,128)(2,1)}, u32[]{:S(2)}, u32[]{:S(2)}) collective-permute-start(bf16[24,4736]{1,0:T(8,128)(2,1)} %pad_maximum_fusion.6), channel_id=1, source_target_pairs={{0,3},{1,2},{2,1},{3,0},{4,7},{5,6},{6,5},{7,4},{8,11},{9,10},{10,... | collective-permute-start | bytes 681992 | tf_op jit(solution)/shard_map/ppermute | solution.py:13
  295.3 2.6 reshape.124
  299.4 6.5 %collective-permute-done.20 = bf16[24,4736]{1,0:T(8,128)(2,1)} collective-permute-done((bf16[24,4736]{1,0:T(8,128)(2,1)}, bf16[24,4736]{1,0:T(8,128)(2,1)}, u32[]{:S(2)}, u32[]{:S(2)}) %collective-permute-start.20) | collective-permute-done | bytes 227360 | tf_op jit(solution)/shard_map/ppermute | solution.py:13
  (181 shorter events, 38.2 us)
Async XLA Ops:
  7.2 98.8 %all-gather.2.cloned.1.call-start = ((), (), s32[]{:S(2)}) async-start(), calls=%async_computation.3 | async-start | bytes 9934848 | tf_op jit(solution)/shard_map/all_gather | solution.py:616
  11.8 230.5 %reduce-scatter.2.cloned.1.call-start = ((), (), s32[]{:S(2)}) async-start(), calls=%async_computation.4 | async-start | bytes 4423680 | tf_op jit(solution)/shard_map/reduce_scatter | solution.py:668
  12.1 20.4 %collective-permute-start = (bf16[24,3200]{1,0:T(8,128)(2,1)S(1)}, bf16[24,3200]{1,0:T(8,128)(2,1)S(1)}, u32[]{:S(2)}, u32[]{:S(2)}) collective-permute-start(bf16[24,3200]{1,0:T(8,128)(2,1)S(1)} %fusion.1), channel_id=1, source_target_pairs={{0,1},{1,0},{2,3},{3,2},{4,5},{5,4},{6,7},{7,6},{8,9},{9,8},{10,11... | collective-permute-start | bytes 460808 | tf_op jit(solution)/shard_map/ppermute | solution.py:13
  15.2 17.3 %collective-permute-start.1 = (bf16[24,3200]{1,0:T(8,128)(2,1)S(1)}, bf16[24,3200]{1,0:T(8,128)(2,1)S(1)}, u32[]{:S(2)}, u32[]{:S(2)}) collective-permute-start(bf16[24,3200]{1,0:T(8,128)(2,1)S(1)} %fusion.1), channel_id=1, source_target_pairs={{0,2},{1,3},{2,0},{3,1},{4,6},{5,7},{6,4},{7,5},{8,10},{9,11},{10,... | collective-permute-start | bytes 460808 | tf_op jit(solution)/shard_map/ppermute | solution.py:13
  17.8 10.4 %collective-permute-start.2 = (bf16[24,3200]{1,0:T(8,128)(2,1)S(1)}, bf16[24,3200]{1,0:T(8,128)(2,1)S(1)}, u32[]{:S(2)}, u32[]{:S(2)}) collective-permute-start(bf16[24,3200]{1,0:T(8,128)(2,1)S(1)} %fusion.1), channel_id=1, source_target_pairs={{0,3},{1,2},{2,1},{3,0},{4,7},{5,6},{6,5},{7,4},{8,11},{9,10},{10,... | collective-permute-start | bytes 460808 | tf_op jit(solution)/shard_map/ppermute | solution.py:13
  32.6 9.2 %collective-permute-start.6 = (bf16[4,24,1664]{2,1,0:T(8,128)(2,1)S(1)}, bf16[4,24,1664]{2,1,0:T(8,128)(2,1)S(1)}, u32[]{:S(2)}, u32[]{:S(2)}) collective-permute-start(bf16[4,24,1664]{2,1,0:T(8,128)(2,1)S(1)} %pad_maximum_fusion), channel_id=1, source_target_pairs={{0,8},{4,12},{8,0},{12,4},{16,24},{20,28},{24,16},{28,20},{1,9},{5... | collective-permute-start | bytes 958472 | tf_op jit(solution)/shard_map/ppermute | solution.py:13
  34.3 10.0 %collective-permute-start.3 = (bf16[4,24,1536]{2,1,0:T(8,128)(2,1)S(1)}, bf16[4,24,1536]{2,1,0:T(8,128)(2,1)S(1)}, u32[]{:S(2)}, u32[]{:S(2)}) collective-permute-start(bf16[4,24,1536]{2,1,0:T(8,128)(2,1)S(1)} %pad_maximum_fusion.1), channel_id=1, source_target_pairs={{0,16},{4,20},{8,24},{12,28},{16,0},{20,4},{24,8},{28,12},{1,17},{... | collective-permute-start | bytes 884744 | tf_op jit(solution)/shard_map/ppermute | solution.py:13
  41.9 15.4 %collective-permute-start.7 = (bf16[8,24,1664]{2,1,0:T(8,128)(2,1)S(1)}, bf16[8,24,1664]{2,1,0:T(8,128)(2,1)S(1)}, u32[]{:S(2)}, u32[]{:S(2)}) collective-permute-start(bf16[8,24,1664]{2,1,0:T(8,128)(2,1)S(1)} %get-tuple-element.175), channel_id=1, source_target_pairs={{0,16},{4,20},{8,24},{12,28},{16,0},{20,4},{24,8},{28,12},{1,17},{... | collective-permute-start | bytes 1916936 | tf_op jit(solution)/shard_map/ppermute | solution.py:13
  43.9 18.0 %copy-start.29 = (s32[8,1]{0,1:T(1,128)S(1)}, s32[8,1]{0,1:T(1,128)}, u32[]{:S(2)}) copy-start(s32[8,1]{0,1:T(1,128)} %param.22) | copy-start | bytes 100
  44.3 16.6 %collective-permute-start.4 = (bf16[8,24,1536]{2,1,0:T(8,128)(2,1)S(1)}, bf16[8,24,1536]{2,1,0:T(8,128)(2,1)S(1)}, u32[]{:S(2)}, u32[]{:S(2)}) collective-permute-start(bf16[8,24,1536]{2,1,0:T(8,128)(2,1)S(1)} %get-tuple-element.177), channel_id=1, source_target_pairs={{0,8},{4,12},{8,0},{12,4},{16,24},{20,28},{24,16},{28,20},{1,9},{5... | collective-permute-start | bytes 1769480 | tf_op jit(solution)/shard_map/ppermute | solution.py:13
  57.4 6.7 %collective-permute-start.8 = (bf16[16,24,1664]{2,1,0:T(8,128)(2,1)S(1)}, bf16[16,24,1664]{2,1,0:T(8,128)(2,1)}, u32[]{:S(2)}, u32[]{:S(2)}) collective-permute-start(bf16[16,24,1664]{2,1,0:T(8,128)(2,1)S(1)} %constant_dynamic-update-slice_fusion.16.p2), channel_id=1, source_target_pairs={{0,4},{4,0},{8,12},{12,8},{16,20},{20,16},{24,28},{28,24},{1,5},{5... | collective-permute-start | bytes 3833864 | tf_op jit(solution)/shard_map/ppermute | solution.py:13
  61.0 3.0 collective-permute-start.5
  185.0 8.2 %collective-permute-start.9 = (bf16[4,96,4608]{2,1,0:T(8,128)(2,1)}, bf16[4,96,4608]{2,1,0:T(8,128)(2,1)}, u32[]{:S(2)}, u32[]{:S(2)}) collective-permute-start(bf16[4,96,4608]{2,1,0:T(8,128)(2,1)} %get-tuple-element.109), channel_id=1, source_target_pairs={{0,4},{4,0},{8,12},{12,8},{16,20},{20,16},{24,28},{28,24},{1,5},{5... | collective-permute-start | bytes 10616840 | tf_op jit(solution)/shard_map/ppermute | solution.py:13
  199.2 24.7 %collective-permute-start.10 = (bf16[4,96,2304]{2,1,0:T(8,128)(2,1)S(1)}, bf16[4,96,2304]{2,1,0:T(8,128)(2,1)S(1)}, u32[]{:S(2)}, u32[]{:S(2)}) collective-permute-start(bf16[4,96,2304]{2,1,0:T(8,128)(2,1)S(1)} %copy-done.30), channel_id=1, source_target_pairs={{0,4},{4,0},{8,12},{12,8},{16,20},{20,16},{24,28},{28,24},{1,5},{5... | collective-permute-start | bytes 5308424 | tf_op jit(solution)/shard_map/ppermute | solution.py:13
  223.9 9.5 %copy-start.3 = (bf16[4,96,2304]{2,1,0:T(8,128)(2,1)}, bf16[4,96,2304]{2,1,0:T(8,128)(2,1)S(1)}, u32[]{:S(2)}) copy-start(bf16[4,96,2304]{2,1,0:T(8,128)(2,1)S(1)} %collective-permute-done.10) | copy-start | bytes 5308420
  223.9 9.7 %copy-start.14 = (f32[16,768]{1,0:T(8,128)S(1)}, f32[16,768]{1,0:T(8,128)}, u32[]{:S(2)}) copy-start(f32[16,768]{1,0:T(8,128)} %get-tuple-element.99) | copy-start | bytes 147460
  223.9 10.3 %copy-start.12 = (f32[32,1,128]{2,1,0:T(1,128)S(1)}, f32[32,1,128]{2,1,0:T(1,128)}, u32[]{:S(2)}) copy-start(f32[32,1,128]{2,1,0:T(1,128)} %get-tuple-element.195) | copy-start | bytes 49156
  233.5 6.4 %collective-permute-start.11 = (bf16[4,96,2432]{2,1,0:T(8,128)(2,1)}, bf16[4,96,2432]{2,1,0:T(8,128)(2,1)S(1)}, u32[]{:S(2)}, u32[]{:S(2)}) collective-permute-start(bf16[4,96,2432]{2,1,0:T(8,128)(2,1)} %get-tuple-element.123), channel_id=1, source_target_pairs={{0,4},{4,0},{8,12},{12,8},{16,20},{20,16},{24,28},{28,24},{1,5},{5... | collective-permute-start | bytes 5603336 | tf_op jit(solution)/shard_map/ppermute | solution.py:13
  239.8 23.8 %collective-permute-start.16 = (bf16[2,96,2304]{2,1,0:T(8,128)(2,1)}, bf16[2,96,2304]{2,1,0:T(8,128)(2,1)}, u32[]{:S(2)}, u32[]{:S(2)}) collective-permute-start(bf16[2,96,2304]{2,1,0:T(8,128)(2,1)} %get-tuple-element.157), channel_id=1, source_target_pairs={{0,16},{4,20},{8,24},{12,28},{16,0},{20,4},{24,8},{28,12},{1,17},{... | collective-permute-start | bytes 2654216 | tf_op jit(solution)/shard_map/ppermute | solution.py:13
  242.3 23.1 %collective-permute-start.15 = (bf16[2,96,2432]{2,1,0:T(8,128)(2,1)}, bf16[2,96,2432]{2,1,0:T(8,128)(2,1)S(1)}, u32[]{:S(2)}, u32[]{:S(2)}) collective-permute-start(bf16[2,96,2432]{2,1,0:T(8,128)(2,1)} %get-tuple-element.154), channel_id=1, source_target_pairs={{0,8},{4,12},{8,0},{12,4},{16,24},{20,28},{24,16},{28,20},{1,9},{5... | collective-permute-start | bytes 2801672 | tf_op jit(solution)/shard_map/ppermute | solution.py:13
  244.4 21.0 %collective-permute-start.12 = (bf16[24,4608]{1,0:T(8,128)(2,1)}, bf16[24,4608]{1,0:T(8,128)(2,1)S(1)}, u32[]{:S(2)}, u32[]{:S(2)}) collective-permute-start(bf16[24,4608]{1,0:T(8,128)(2,1)} %get-tuple-element.160), channel_id=1, source_target_pairs={{0,1},{1,0},{2,3},{3,2},{4,5},{5,4},{6,7},{7,6},{8,9},{9,8},{10,11... | collective-permute-start | bytes 663560 | tf_op jit(solution)/shard_map/ppermute | solution.py:13
  245.3 20.1 %collective-permute-start.13 = (bf16[24,4608]{1,0:T(8,128)(2,1)}, bf16[24,4608]{1,0:T(8,128)(2,1)S(1)}, u32[]{:S(2)}, u32[]{:S(2)}) collective-permute-start(bf16[24,4608]{1,0:T(8,128)(2,1)} %get-tuple-element.159), channel_id=1, source_target_pairs={{0,2},{1,3},{2,0},{3,1},{4,6},{5,7},{6,4},{7,5},{8,10},{9,11},{10,... | collective-permute-start | bytes 663560 | tf_op jit(solution)/shard_map/ppermute | solution.py:13
  248.8 14.6 %copy-start.11 = (f32[32,1,128]{2,1,0:T(1,128)S(1)}, f32[32,1,128]{2,1,0:T(1,128)}, u32[]{:S(2)}) copy-start(f32[32,1,128]{2,1,0:T(1,128)} %get-tuple-element.196) | copy-start | bytes 49156
  248.8 17.5 %collective-permute-start.14 = (bf16[24,4608]{1,0:T(8,128)(2,1)}, bf16[24,4608]{1,0:T(8,128)(2,1)}, u32[]{:S(2)}, u32[]{:S(2)}) collective-permute-start(bf16[24,4608]{1,0:T(8,128)(2,1)} %get-tuple-element.158), channel_id=1, source_target_pairs={{0,3},{1,2},{2,1},{3,0},{4,7},{5,6},{6,5},{7,4},{8,11},{9,10},{10,... | collective-permute-start | bytes 663560 | tf_op jit(solution)/shard_map/ppermute | solution.py:13
  257.6 15.0 %all-to-all-start.1 = ((f32[32,4,128]{2,1,0:T(4,128)}), f32[32,4,128]{2,1,0:T(4,128)S(1)}, u32[]{:S(2)}, u32[]{:S(2)}) async-start(f32[32,4,128]{2,1,0:T(4,128)} %reshape.116), calls=%async_computation.2 | async-start | bytes 131072 | tf_op jit(solution)/shard_map/all_to_all | solution.py:704
  268.7 13.6 %collective-permute-start.17 = (bf16[1,96,2432]{2,1,0:T(8,128)(2,1)}, bf16[1,96,2432]{2,1,0:T(8,128)(2,1)S(1)}, u32[]{:S(2)}, u32[]{:S(2)}) collective-permute-start(bf16[1,96,2432]{2,1,0:T(8,128)(2,1)} %constant_dynamic-slice_fusion.1), channel_id=1, source_target_pairs={{0,16},{4,20},{8,24},{12,28},{16,0},{20,4},{24,8},{28,12},{1,17},{... | collective-permute-start | bytes 1400840 | tf_op jit(solution)/shard_map/ppermute | solution.py:13
  271.1 11.2 %collective-permute-start.18 = (bf16[1,96,2304]{2,1,0:T(8,128)(2,1)S(1)}, bf16[1,96,2304]{2,1,0:T(8,128)(2,1)S(1)}, u32[]{:S(2)}, u32[]{:S(2)}) collective-permute-start(bf16[1,96,2304]{2,1,0:T(8,128)(2,1)S(1)} %constant_dynamic-slice_fusion), channel_id=1, source_target_pairs={{0,8},{4,12},{8,0},{12,4},{16,24},{20,28},{24,16},{28,20},{1,9},{5... | collective-permute-start | bytes 1327112 | tf_op jit(solution)/shard_map/ppermute | solution.py:13
  282.5 8.5 %copy-start.8 = (bf16[24,4608]{1,0:T(8,128)(2,1)S(1)}, bf16[24,4608]{1,0:T(8,128)(2,1)}, u32[]{:S(2)}) copy-start(bf16[24,4608]{1,0:T(8,128)(2,1)} %copy-done.7) | copy-start | bytes 663556
  282.5 8.5 %copy-start.10 = (bf16[24,4608]{1,0:T(8,128)(2,1)S(1)}, bf16[24,4608]{1,0:T(8,128)(2,1)}, u32[]{:S(2)}) copy-start(bf16[24,4608]{1,0:T(8,128)(2,1)} %copy-done.9) | copy-start | bytes 663556
  285.2 14.2 %collective-permute-start.21 = (bf16[24,4736]{1,0:T(8,128)(2,1)}, bf16[24,4736]{1,0:T(8,128)(2,1)}, u32[]{:S(2)}, u32[]{:S(2)}) collective-permute-start(bf16[24,4736]{1,0:T(8,128)(2,1)} %pad_maximum_fusion.6), channel_id=1, source_target_pairs={{0,3},{1,2},{2,1},{3,0},{4,7},{5,6},{6,5},{7,4},{8,11},{9,10},{10,... | collective-permute-start | bytes 681992 | tf_op jit(solution)/shard_map/ppermute | solution.py:13
  289.3 16.6 %collective-permute-start.20 = (bf16[24,4736]{1,0:T(8,128)(2,1)}, bf16[24,4736]{1,0:T(8,128)(2,1)}, u32[]{:S(2)}, u32[]{:S(2)}) collective-permute-start(bf16[24,4736]{1,0:T(8,128)(2,1)} %pad_maximum_fusion.5), channel_id=1, source_target_pairs={{0,2},{1,3},{2,0},{3,1},{4,6},{5,7},{6,4},{7,5},{8,10},{9,11},{10,... | collective-permute-start | bytes 681992 | tf_op jit(solution)/shard_map/ppermute | solution.py:13
  290.0 15.9 %collective-permute-start.19 = (bf16[24,4736]{1,0:T(8,128)(2,1)}, bf16[24,4736]{1,0:T(8,128)(2,1)}, u32[]{:S(2)}, u32[]{:S(2)}) collective-permute-start(bf16[24,4736]{1,0:T(8,128)(2,1)} %pad_maximum_fusion.4), channel_id=1, source_target_pairs={{0,1},{1,0},{2,3},{3,2},{4,5},{5,4},{6,7},{7,6},{8,9},{9,8},{10,11... | collective-permute-start | bytes 681992 | tf_op jit(solution)/shard_map/ppermute | solution.py:13
  (24 other events, 62.8 us)
Sparse Core Ops, SparseCore 0:
  12.0 94.0 all-gather.1
  197.9 43.7 reduce-scatter.1

commit v2 on v1

--- a/solution.py
+++ b/solution.py
@@ -378,7 +378,7 @@
         compiler_params=pltpu.CompilerParams(vmem_limit_bytes=VMEM_MOST),name='feed_forward')(lens,n1,low,w,vec)
 
 def feed_forward_grad_kernel(lens_ref,own_ids_ref,doc_ref,scores_ref,ids_ref,cot_ref,n2_ref,r2_ref,res_ref,span_ref,score_ref,dg_ref,n1_ref,r1_ref,w_ref,aw_ref,vec_ref,
-                   olow_ref,ilow_ref,alow_ref,fsum_ref,dctx_ref,small_ref,spanw_ref,weight_ref,acc_ref):
+                   low_ref,fsum_ref,dctx_ref,small_ref,spanw_ref,weight_ref,acc_ref):
     i=pl.program_id(0); last=pl.num_programs(0)-1
     rows,width=cot_ref.shape; reps=dg_ref.shape[1]//width
     vec=lambda k: vec_ref[k:k+1,:]
@@ -413,20 +413,20 @@
         small_ref[k:k+1,:]+=jnp.sum(v,axis=0,keepdims=True)
     colsum(0,rg*n2); colsum(1,rg)
     ssum=norm_back(rg*vec(4),n2,r2_ref[:,:1])
-    olow=ssum.astype(BF16); olow_ref[...]=olow
+    olow=ssum.astype(BF16); low_ref[:,reps*width:(reps+1)*width]=olow
     colsum(2,olow.astype(F32))
     fg=ssum
     for q in range(reps):
         c=slice(q*width,(q+1)*width)
         il=(dot_nt(olow,w_ref[:,(reps+q)*width:(reps+q+1)*width])*dg_ref[:,c].astype(F32)).astype(BF16)
-        ilow_ref[:,c]=il
+        low_ref[:,c]=il
         colsum(8+q,il.astype(F32))
         fg=fg+dot_nt(il,w_ref[:,c])
     n1=n1_ref[...]
     colsum(3,fg*n1); colsum(4,fg)
     fsum=norm_back(fg*vec(1),n1,r1_ref[:,:1])
     fsum_ref[...]=fsum
-    alow=fsum.astype(BF16); alow_ref[...]=alow
+    alow=fsum.astype(BF16); low_ref[:,(reps+1)*width:]=alow
     colsum(5,alow.astype(F32))
     dctx_ref[...]=dot_nt(alow,aw_ref[...]).astype(BF16)
 
@@ -437,8 +437,8 @@
     sm=pl.BlockSpec(memory_space=pltpu.SMEM)
     return pl.pallas_call(feed_forward_grad_kernel,grid=(rows//TILE,),
         in_specs=[sm,sm,once(doc.shape),once(scores.shape),once(ids.shape),b(width),b(width),b(LANES),b(width),b(LANES),b(LANES),b(ff),b(width),b(LANES),once(w.shape),pl.BlockSpec((width,width),lambda i:(0,3),pipeline_mode=pl.Buffered(1)),once(vec.shape)],
-        out_specs=[b(width),b(ff),b(width),b(width),b(width),once(vec.shape),once((width,LANES))],
-        out_shape=[s(width,BF16),s(ff,BF16),s(width,BF16),s(width,F32),s(width,BF16),jax.ShapeDtypeStruct(vec.shape,F32),jax.ShapeDtypeStruct((width,LANES),BF16)],
+        out_specs=[b(ff+2*width),b(width),b(width),once(vec.shape),once((width,LANES))],
+        out_shape=[s(ff+2*width,BF16),s(width,F32),s(width,BF16),jax.ShapeDtypeStruct(vec.shape,F32),jax.ShapeDtypeStruct((width,LANES),BF16)],
         scratch_shapes=[pltpu.VMEM((1,LANES),F32),pltpu.VMEM((width,LANES),F32)],
         compiler_params=pltpu.CompilerParams(vmem_limit_bytes=VMEM_MOST),name='feed_forward_grad')(lens,own_ids,doc,scores,ids,cot,n2,r2,res,span,score,dg,n1,r1,w,mix,vec)
 
@@ -455,48 +455,45 @@
         def _():
             keep_ref[t,:,at]=high; give_ref[t,:,at]=low
 
-def early_kernel(reps,me_ref,low_ref,ilow_ref,act_ref,olow_hbm,ctx_hbm,alow_hbm,keep_ref,give_ref,olow_ref,ctx_ref,alow_ref,sems):
-    j=pl.program_id(0); last=pl.num_programs(0)-1
-    moves=[pltpu.make_async_copy(src,dst,sems.at[k]) for k,(src,dst) in enumerate(((olow_hbm,olow_ref),(ctx_hbm,ctx_ref),(alow_hbm,alow_ref)))]
-    put=lambda value: put_blocks(me_ref,keep_ref,give_ref,value,slice(None))
+def early_kernel(reps,me_ref,low_hbm,act_hbm,ctx_hbm,right_ref,keep_ref,give_ref,left_ref,sems):
+    j=pl.program_id(0); slots,_,width=left_ref.shape
+    sources=[low_hbm]+[act_hbm.at[:,pl.ds(k*width,width)] for k in range(slots-2)]+[ctx_hbm]
+    moves=[pltpu.make_async_copy(src,left_ref.at[k],sems.at[k]) for k,src in enumerate(sources)]
     @pl.when(j==0)
     def _():
         for move in moves: move.start()
-    @pl.when(j<reps)
-    def _(): put(dot_tn(low_ref[...],ilow_ref[...]))
-    @pl.when(j==reps)
-    def _():
-        for move in moves: move.wait()
-    @pl.when(jnp.logical_and(j>=reps,j<last))
-    def _(): put(dot_tn(act_ref[...],olow_ref[...]))
-    @pl.when(j==last)
-    def _(): put(dot_tn(ctx_ref[...],alow_ref[...]))
+    for k,move in enumerate(moves):
+        @pl.when(j==(0 if k==0 else reps+k-1))
+        def _(): move.wait()
+    put_blocks(me_ref,keep_ref,give_ref,dot_tn(left_ref[jnp.maximum(j-reps+1,0)],right_ref[...]),slice(None))
 
 def split_outs(dp,width,n):
     block=(dp//2,width//dp,width)
     return [pl.BlockSpec(block,lambda j:(0,0,j))]*2,[jax.ShapeDtypeStruct(block[:2]+(n*width,),BF16)]*2
 
-def early_grads(me,low,ilow,act,olow,ctx,alow,outer_blocks,dp):
+def early_grads(me,low,act,ctx,right,outer_blocks,dp):
     rows,width=low.shape; reps=act.shape[1]//width
-    full=once((rows,width)); n=reps+outer_blocks+1
+    n=reps+outer_blocks+1
     specs,shapes=split_outs(dp,width,n)
+    hbm=pl.BlockSpec(memory_space=pl.ANY)
+    column=lambda j: jnp.where(j<reps,j,jnp.where(j<n-1,reps,reps+1))
     return pl.pallas_call(functools.partial(early_kernel,reps),grid=(n,),
-        in_specs=[pl.BlockSpec(memory_space=pltpu.SMEM),full,pl.BlockSpec((rows,width),lambda j:(0,jnp.minimum(j,reps-1))),pl.BlockSpec((rows,width),lambda j:(0,jnp.clip(j-reps,0,outer_blocks-1)))]+[pl.BlockSpec(memory_space=pl.ANY)]*3,
-        out_specs=specs,out_shape=shapes,scratch_shapes=[pltpu.VMEM((rows,width),BF16)]*3+[pltpu.SemaphoreType.DMA((3,))],
+        in_specs=[pl.BlockSpec(memory_space=pltpu.SMEM),hbm,hbm,hbm,pl.BlockSpec((rows,width),lambda j:(0,column(j)))],
+        out_specs=specs,out_shape=shapes,scratch_shapes=[pltpu.VMEM((outer_blocks+2,rows,width),BF16),pltpu.SemaphoreType.DMA((outer_blocks+2,))],
         compiler_params=pltpu.CompilerParams(vmem_limit_bytes=VMEM_MOST),name='early_weight_grads',
-        cost_estimate=pl.CostEstimate(flops=2*rows*width*width*n,bytes_accessed=rows*width*n*4,transcendentals=0))(me,low,ilow,act,olow,ctx,alow)
+        cost_estimate=pl.CostEstimate(flops=2*rows*width*width*n,bytes_accessed=rows*width*n*4,transcendentals=0))(me,low,act,ctx,right)
 
 def outer_kernel(me_ref,act_ref,olow_ref,keep_ref,give_ref):
     put_blocks(me_ref,keep_ref,give_ref,dot_tn(act_ref[...],olow_ref[...]),slice(None))
 
-def outer_grads(me,act,olow,first,dp):
-    rows,width=olow.shape; n=act.shape[1]//width-first
+def outer_grads(me,act,right,first,dp):
+    rows,ff=act.shape; width=right.shape[1]-ff>>1; n=ff//width-first
     specs,shapes=split_outs(dp,width,n)
     return pl.pallas_call(outer_kernel,grid=(n,),
-        in_specs=[pl.BlockSpec(memory_space=pltpu.SMEM),pl.BlockSpec((rows,width),lambda j:(0,j+first)),once((rows,width))],
+        in_specs=[pl.BlockSpec(memory_space=pltpu.SMEM),pl.BlockSpec((rows,width),lambda j:(0,j+first)),pl.BlockSpec((rows,width),lambda j:(0,ff//width),pipeline_mode=pl.Buffered(1))],
         out_specs=specs,out_shape=shapes,
         compiler_params=pltpu.CompilerParams(vmem_limit_bytes=VMEM_MOST),name='outer_weight_grad',
-        cost_estimate=pl.CostEstimate(flops=2*rows*width*width*n,bytes_accessed=rows*width*n*4,transcendentals=0))(me,act,olow)
+        cost_estimate=pl.CostEstimate(flops=2*rows*width*width*n,bytes_accessed=rows*width*n*4,transcendentals=0))(me,act,right)
 
 def late_kernel(me_ref,tok_ref,mg_ref,span_ref,keep_ref,give_ref,sum_ref):
     j=pl.program_id(0)
@@ -632,7 +629,7 @@
     exchanged = to_all(jnp.concatenate([doc_score, id_row], axis=0), devices)
     scores_all, ids_all = exchanged[:, 0], exchanged[:, 1]
 
-    outer_low, inner_low, attended_low, first_sum_grad, context_grad, small_sums, span_grad = (
+    lows, first_sum_grad, context_grad, small_sums, span_grad = (
         feed_forward_grad(
             doc_lengths,
             query_ids.reshape(-1),
@@ -655,12 +652,10 @@
     )
     early_blocks = reps - LATE_BLOCKS
     dp = lax.axis_size("dp")
-    keep, give = early_grads(
-        me, first_low, inner_low, active, outer_low, context, attended_low, early_blocks, dp
-    )
+    keep, give = early_grads(me, first_low, active, context, lows, early_blocks, dp)
     came = swap(give, "dp", orders[0][0])
-    outer_low, keep = tie(outer_low, keep)
-    outer_walk = Reduction(*outer_grads(me, active, outer_low, early_blocks, dp), orders[1])
+    lows, keep = tie(lows, keep)
+    outer_walk = Reduction(*outer_grads(me, active, lows, early_blocks, dp), orders[1])
     came, outer_walk.keep = tie(came, outer_walk.keep)
     outer_walk.send()
     early = add_low(keep, came)

time: 321 us -> 321 us (level)
  no operation moved by 1% of the time
where the time goes in v2:
time: 321 us; the launch traced here: 317 us
  Pallas kernels  149 us (46%)
  waiting for transfers between devices  67.8 us (21%)
  starting transfers between devices  29 us (9%)
  local copies, waits for them, and re-layouts  27.1 us (8%)
  other arithmetic  18.3 us (6%)
  between operations  15.4 us (5%)
  blocking collectives  10.5 us (3%)
    ppermute x22, waiting for transfers between devices, swap(): return lax.ppermute(block, axis, [(i, i ^ mask) for i in range(size)])  56.3 us
    pallas_call x1, Pallas kernels, attention(): pl.pallas_call(functools.partial(attention_kernel, orders, fsdp, small),...  30.4 us
    pallas_call x1, Pallas kernels, feed_forward(): pl.pallas_call(feed_forward_kernel, grid=(rows // TILE,), in_specs=[pl.Bl...  27.6 us
    pallas_call x1, Pallas kernels, feed_forward_grad(): pl.pallas_call(feed_forward_grad_kernel, grid=(rows // TILE,), in_specs=[...  25.8 us
    pallas_call x1, Pallas kernels, attention_grad(): pl.pallas_call(attention_grad_kernel, grid=(rows // PACK, pairs), in_spec...  24 us
    ppermute x22, starting transfers between devices, swap(): return lax.ppermute(block, axis, [(i, i ^ mask) for i in range(size)])  23.5 us
    pallas_call x1, Pallas kernels, early_grads(): pl.pallas_call(functools.partial(early_kernel, reps), grid=(n,), in_specs...  14.3 us
    all_gather x1, waiting for transfers between devices, shards(): rest_full = lax.all_gather(rest, AXES, axis=0, tiled=True)  11.5 us
  transfers between devices with their start and end apart: 25, of which 11 were waited for; matrix products, arithmetic and copies ran while one was open for 8% of the time, Pallas kernels for 26%

profile of v2, /device:TPU:0, one launch (start us, length us, event | category | flops | bytes accessed | tf_op | source)
XLA Modules:
  0.0 316.9 jit_solution(5602863697047155221)
XLA Ops:
  7.2 2.1 reshape.111
  12.1 3.1 collective-permute-start
  15.2 2.6 collective-permute-start.1
  17.9 10.3 %collective-permute-done.2 = bf16[24,3200]{1,0:T(8,128)(2,1)S(1)} collective-permute-done((bf16[24,3200]{1,0:T(8,128)(2,1)S(1)}, bf16[24,3200]{1,0:T(8,128)(2,1)S(1)}, u32[]{:S(2)}, u32[]{:S(2)}) %collective-permute-start.2) | collective-permute-done | bytes 153632 | tf_op jit(solution)/shard_map/ppermute | solution.py:13
  28.2 4.4 %collective-permute-done.1 = bf16[24,3200]{1,0:T(8,128)(2,1)S(1)} collective-permute-done((bf16[24,3200]{1,0:T(8,128)(2,1)S(1)}, bf16[24,3200]{1,0:T(8,128)(2,1)S(1)}, u32[]{:S(2)}, u32[]{:S(2)}) %collective-permute-start.1) | collective-permute-done | bytes 153632 | tf_op jit(solution)/shard_map/ppermute | solution.py:13
  34.3 1.6 collective-permute-start.3
  36.0 5.9 %collective-permute-done.6 = bf16[4,24,1664]{2,1,0:T(8,128)(2,1)S(1)} collective-permute-done((bf16[4,24,1664]{2,1,0:T(8,128)(2,1)S(1)}, bf16[4,24,1664]{2,1,0:T(8,128)(2,1)S(1)}, u32[]{:S(2)}, u32[]{:S(2)}) %collective-permute-start.6) | collective-permute-done | bytes 319520 | tf_op jit(solution)/shard_map/ppermute | solution.py:13
  41.9 1.9 collective-permute-start.7
  44.3 1.8 collective-permute-start.4
  46.2 11.1 %collective-permute-done.7 = bf16[8,24,1664]{2,1,0:T(8,128)(2,1)S(1)} collective-permute-done((bf16[8,24,1664]{2,1,0:T(8,128)(2,1)S(1)}, bf16[8,24,1664]{2,1,0:T(8,128)(2,1)S(1)}, u32[]{:S(2)}, u32[]{:S(2)}) %collective-permute-start.7) | collective-permute-done | bytes 639008 | tf_op jit(solution)/shard_map/ppermute | solution.py:13
  57.5 3.5 %collective-permute-done.4 = bf16[8,24,1536]{2,1,0:T(8,128)(2,1)S(1)} collective-permute-done((bf16[8,24,1536]{2,1,0:T(8,128)(2,1)S(1)}, bf16[8,24,1536]{2,1,0:T(8,128)(2,1)S(1)}, u32[]{:S(2)}, u32[]{:S(2)}) %collective-permute-start.4) | collective-permute-done | bytes 589856 | tf_op jit(solution)/shard_map/ppermute | solution.py:13
  61.8 2.2 collective-permute-done.5.p1
  64.1 30.4 %attention.1 = (bf16[768,3200]{1,0:T(8,128)(2,1)}, f32[16,768]{1,0:T(8,128)}, bf16[1024,2304]{1,0:T(8,128)(2,1)}, bf16[1024,768]{1,0:T(8,128)(2,1)}, f32[1024,12...) custom-call(s32[2,4]{1,0:T(2,128)} %lens_ref.5, ...), custom_call_target="tpu_custom_call" | custom-call | flops 6845104128 | bytes 9437184 | tf_op jit(solution)/shard_map/attention/pallas_call | solution.py:254
  94.5 11.5 %all-gather.2.cloned.1.call-done.w_ref = bf16[768,6272]{1,0:T(8,128)(2,1)} async-done(((bf16[24,6272]{1,0:T(8,128)(2,1)}), bf16[768,6272]{1,0:T(8,128)(2,1)}) %all-gather.2.cloned.1.call-update) | async-done | bytes 9633808 | tf_op jit(solution)/shard_map/all_gather | solution.py:613
  106.0 27.6 %feed_forward.1 = (bf16[1024,3072]{1,0:T(8,128)(2,1)}, bf16[1024,3072]{1,0:T(8,128)(2,1)}, f32[1024,768]{1,0:T(8,128)}, f32[1024,128]{1,0:T(8,128)}, bf16[1024,7...) custom-call(s32[2,4]{1,0:T(2,128)} %lens_ref.5, ...), custom_call_target="tpu_custom_call" | custom-call | tf_op jit(solution)/shard_map/feed_forward/pallas_call | solution.py:373
  134.3 10.5 %all_to_all.10 = f32[32,2,128]{2,1,0:T(2,128)S(1)} all-to-all(f32[32,2,128]{2,1,0:T(2,128)S(1)} %broadcast_in_dim.25), channel_id=1, replica_groups=mesh['dp'=8,'fsdp'=4] {'dp','fsdp'}, dimensions={0} | all-to-all | bytes 65536 | tf_op jit(solution)/shard_map/all_to_all | solution.py:555
  145.5 25.8 %feed_forward_grad.1 = (bf16[1024,4608]{1,0:T(8,128)(2,1)}, f32[1024,768]{1,0:T(8,128)}, bf16[1024,768]{1,0:T(8,128)(2,1)}, f32[16,768]{1,0:T(8,128)}, bf16[768,128]{1,0:T(8,128)(2,1)}) custom-call(s32[2,4]{1,0:T(2,128)} %lens_ref.5, s32[8]{0:T(128)} %bitcast.128, f32[1,128]{1,0:T(1,128)} %get-tuple-element.87.doc_ref, f32[32,128]{1,0:T(8,128)} %bitcast.121, ...), custom_call_target="tpu_custom_call" | custom-call | tf_op jit(solution)/shard_map/feed_forward_grad/pallas_call | solution.py:438
  171.3 14.3 %early_weight_grads.1 = (bf16[4,96,4608]{2,1,0:T(8,128)(2,1)}, bf16[4,96,4608]{2,1,0:T(8,128)(2,1)}) custom-call(s32[2]{0:T(128)} %pad_add_fusion.me_ref, bf16[1024,768]{1,0:T(8,128)(2,1)} %get-tuple-element.85.low_ref.low_hbm, bf16[1024,3072]{1,0:T(8,128)(2,1)} %get-tuple-element.102.act_hbm.act_ref, bf16[1024,768]{1,0:T(8,128)(2,1)} %get-tuple-element.99.ctx_hbm.ctx_ref, ...), custom_call_target="tpu_custom_call" | custom-call | flops 7247757312 | bytes 18874368 | tf_op jit(solution)/shard_map/early_weight_grads/pallas_call | solution.py:480
  185.7 8.1 %outer_weight_grad.1 = (bf16[4,96,2304]{2,1,0:T(8,128)(2,1)}, bf16[4,96,2304]{2,1,0:T(8,128)(2,1)}) custom-call(s32[2]{0:T(128)} %pad_add_fusion.me_ref, bf16[1024,3072]{1,0:T(8,128)(2,1)} %get-tuple-element.102.act_hbm.act_ref, bf16[1024,4608]{1,0:T(8,128)(2,1)} %get-tuple-element.106.right_ref.olow_ref), custom_call_target="tpu_custom_call" | custom-call | flops 3623878656 | bytes 9437184 | tf_op jit(solution)/shard_map/outer_weight_grad/pallas_call | solution.py:492
  193.7 4.6 %add_convert_fusion = bf16[4,96,4608]{2,1,0:T(8,128)(2,1)} fusion(bf16[4,96,4608]{2,1,0:T(8,128)(2,1)} %collective-permute-done.9, bf16[4,96,4608]{2,1,0:T(8,128)(2,1)S(1)} %copy-done), kind=kLoop, calls=%fused_computation | loop fusion | flops 7077888 | bytes 10616832 | tf_op jit(solution)/shard_map/convert_element_type | solution.py:65
  200.2 24.0 %attention_grad.1.mg_ref.refs_0_ = bf16[1024,2304]{1,0:T(8,128)(2,1)} custom-call(bf16[1024,2304]{1,0:T(8,128)(2,1)} %get-tuple-element.98.mix_ref, bf16[1024,768]{1,0:T(8,128)(2,1)} %get-tuple-element.99.ctx_hbm.ctx_ref, bf16[1024,768]{1,0:T(8,128)(2,1)} %get-tuple-element.109.dctx_ref, f32[1024,128]{1,0:T(8,128)} %get-tuple-element.110.inv_ref, ...), custom_call_target="tpu_custom_call" | custom-call | flops 6442450944 | bytes 18874368 | tf_op jit(solution)/shard_map/attention_grad/pallas_call | solution.py:303
  224.3 9.7 %late_weight_grads.1 = (bf16[4,96,2432]{2,1,0:T(8,128)(2,1)}, bf16[4,96,2432]{2,1,0:T(8,128)(2,1)}, f32[8,2304]{1,0:T(8,128)}) custom-call(s32[2]{0:T(128)} %pad_add_fusion.me_ref, bf16[1024,768]{1,0:T(8,128)(2,1)} %tok_ref.3, bf16[1024,2304]{1,0:T(8,128)(2,1)} %attention_grad.1.mg_ref.refs_0_, bf16[768,128]{1,0:T(8,128)(2,1)} %get-tuple-element.114.span_ref), custom_call_target="tpu_custom_call" | custom-call | flops 3623878656 | bytes 9437184 | tf_op jit(solution)/shard_map/late_weight_grads/pallas_call | solution.py:512
  236.8 2.5 add_convert_fusion.2
  242.8 2.1 dynamic-slice_bitcast_fusion.4
  245.9 3.4 %collective-permute-start.13 = (bf16[24,4608]{1,0:T(8,128)(2,1)}, bf16[24,4608]{1,0:T(8,128)(2,1)S(1)}, u32[]{:S(2)}, u32[]{:S(2)}) collective-permute-start(bf16[24,4608]{1,0:T(8,128)(2,1)} %get-tuple-element.155), channel_id=1, source_target_pairs={{0,2},{1,3},{2,0},{3,1},{4,6},{5,7},{6,4},{7,5},{8,10},{9,11},{10,... | collective-permute-start | bytes 663560 | tf_op jit(solution)/shard_map/ppermute | solution.py:13
  249.3 8.8 %input_grad.1 = f32[1024,768]{1,0:T(8,128)} custom-call(bf16[768,3200]{1,0:T(8,128)(2,1)} %get-tuple-element.95.aw_ref.w_ref, f32[1024,768]{1,0:T(8,128)} %get-tuple-element.127.fs_ref, bf16[1024,2304]{1,0:T(8,128)(2,1)} %attention_grad.1.mg_ref.refs_0_), custom_call_target="tpu_custom_call" | custom-call | flops 3623878656 | bytes 12582912 | tf_op jit(solution)/shard_map/input_grad/pallas_call | solution.py:533
  258.2 5.5 %all-to-all-start.1 = ((f32[32,4,128]{2,1,0:T(4,128)}), f32[32,4,128]{2,1,0:T(4,128)S(1)}, u32[]{:S(2)}, u32[]{:S(2)}) async-start(f32[32,4,128]{2,1,0:T(4,128)} %reshape.116), calls=%async_computation.2 | async-start | bytes 131072 | tf_op jit(solution)/shard_map/all_to_all | solution.py:699
  263.9 2.1 collective-permute-done.15
  272.8 9.9 %collective-permute-done.18 = bf16[1,96,2304]{2,1,0:T(8,128)(2,1)S(1)} collective-permute-done((bf16[1,96,2304]{2,1,0:T(8,128)(2,1)S(1)}, bf16[1,96,2304]{2,1,0:T(8,128)(2,1)S(1)}, u32[]{:S(2)}, u32[]{:S(2)}) %collective-permute-start.18) | collective-permute-done | bytes 442400 | tf_op jit(solution)/shard_map/ppermute | solution.py:13
  285.6 3.0 collective-permute-start.21
  295.7 2.6 reshape.124
  299.8 6.5 %collective-permute-done.20 = bf16[24,4736]{1,0:T(8,128)(2,1)} collective-permute-done((bf16[24,4736]{1,0:T(8,128)(2,1)}, bf16[24,4736]{1,0:T(8,128)(2,1)}, u32[]{:S(2)}, u32[]{:S(2)}) %collective-permute-start.20) | collective-permute-done | bytes 227360 | tf_op jit(solution)/shard_map/ppermute | solution.py:13
  (181 shorter events, 38.0 us)
Async XLA Ops:
  7.2 98.8 %all-gather.2.cloned.1.call-start = ((), (), s32[]{:S(2)}) async-start(), calls=%async_computation.3 | async-start | bytes 9934848 | tf_op jit(solution)/shard_map/all_gather | solution.py:613
  11.8 231.0 %reduce-scatter.2.cloned.1.call-start = ((), (), s32[]{:S(2)}) async-start(), calls=%async_computation.4 | async-start | bytes 4423680 | tf_op jit(solution)/shard_map/reduce_scatter | solution.py:663
  12.1 20.4 %collective-permute-start = (bf16[24,3200]{1,0:T(8,128)(2,1)S(1)}, bf16[24,3200]{1,0:T(8,128)(2,1)S(1)}, u32[]{:S(2)}, u32[]{:S(2)}) collective-permute-start(bf16[24,3200]{1,0:T(8,128)(2,1)S(1)} %fusion.1), channel_id=1, source_target_pairs={{0,1},{1,0},{2,3},{3,2},{4,5},{5,4},{6,7},{7,6},{8,9},{9,8},{10,11... | collective-permute-start | bytes 460808 | tf_op jit(solution)/shard_map/ppermute | solution.py:13
  15.2 17.3 %collective-permute-start.1 = (bf16[24,3200]{1,0:T(8,128)(2,1)S(1)}, bf16[24,3200]{1,0:T(8,128)(2,1)S(1)}, u32[]{:S(2)}, u32[]{:S(2)}) collective-permute-start(bf16[24,3200]{1,0:T(8,128)(2,1)S(1)} %fusion.1), channel_id=1, source_target_pairs={{0,2},{1,3},{2,0},{3,1},{4,6},{5,7},{6,4},{7,5},{8,10},{9,11},{10,... | collective-permute-start | bytes 460808 | tf_op jit(solution)/shard_map/ppermute | solution.py:13
  17.8 10.4 %collective-permute-start.2 = (bf16[24,3200]{1,0:T(8,128)(2,1)S(1)}, bf16[24,3200]{1,0:T(8,128)(2,1)S(1)}, u32[]{:S(2)}, u32[]{:S(2)}) collective-permute-start(bf16[24,3200]{1,0:T(8,128)(2,1)S(1)} %fusion.1), channel_id=1, source_target_pairs={{0,3},{1,2},{2,1},{3,0},{4,7},{5,6},{6,5},{7,4},{8,11},{9,10},{10,... | collective-permute-start | bytes 460808 | tf_op jit(solution)/shard_map/ppermute | solution.py:13
  32.6 9.2 %collective-permute-start.6 = (bf16[4,24,1664]{2,1,0:T(8,128)(2,1)S(1)}, bf16[4,24,1664]{2,1,0:T(8,128)(2,1)S(1)}, u32[]{:S(2)}, u32[]{:S(2)}) collective-permute-start(bf16[4,24,1664]{2,1,0:T(8,128)(2,1)S(1)} %pad_maximum_fusion), channel_id=1, source_target_pairs={{0,8},{4,12},{8,0},{12,4},{16,24},{20,28},{24,16},{28,20},{1,9},{5... | collective-permute-start | bytes 958472 | tf_op jit(solution)/shard_map/ppermute | solution.py:13
  34.3 10.0 %collective-permute-start.3 = (bf16[4,24,1536]{2,1,0:T(8,128)(2,1)S(1)}, bf16[4,24,1536]{2,1,0:T(8,128)(2,1)S(1)}, u32[]{:S(2)}, u32[]{:S(2)}) collective-permute-start(bf16[4,24,1536]{2,1,0:T(8,128)(2,1)S(1)} %pad_maximum_fusion.1), channel_id=1, source_target_pairs={{0,16},{4,20},{8,24},{12,28},{16,0},{20,4},{24,8},{28,12},{1,17},{... | collective-permute-start | bytes 884744 | tf_op jit(solution)/shard_map/ppermute | solution.py:13
  41.9 15.4 %collective-permute-start.7 = (bf16[8,24,1664]{2,1,0:T(8,128)(2,1)S(1)}, bf16[8,24,1664]{2,1,0:T(8,128)(2,1)S(1)}, u32[]{:S(2)}, u32[]{:S(2)}) collective-permute-start(bf16[8,24,1664]{2,1,0:T(8,128)(2,1)S(1)} %get-tuple-element.171), channel_id=1, source_target_pairs={{0,16},{4,20},{8,24},{12,28},{16,0},{20,4},{24,8},{28,12},{1,17},{... | collective-permute-start | bytes 1916936 | tf_op jit(solution)/shard_map/ppermute | solution.py:13
  43.9 18.0 %copy-start.29 = (s32[8,1]{0,1:T(1,128)S(1)}, s32[8,1]{0,1:T(1,128)}, u32[]{:S(2)}) copy-start(s32[8,1]{0,1:T(1,128)} %param.22) | copy-start | bytes 100
  44.3 16.6 %collective-permute-start.4 = (bf16[8,24,1536]{2,1,0:T(8,128)(2,1)S(1)}, bf16[8,24,1536]{2,1,0:T(8,128)(2,1)S(1)}, u32[]{:S(2)}, u32[]{:S(2)}) collective-permute-start(bf16[8,24,1536]{2,1,0:T(8,128)(2,1)S(1)} %get-tuple-element.173), channel_id=1, source_target_pairs={{0,8},{4,12},{8,0},{12,4},{16,24},{20,28},{24,16},{28,20},{1,9},{5... | collective-permute-start | bytes 1769480 | tf_op jit(solution)/shard_map/ppermute | solution.py:13
  57.4 6.7 %collective-permute-start.8 = (bf16[16,24,1664]{2,1,0:T(8,128)(2,1)S(1)}, bf16[16,24,1664]{2,1,0:T(8,128)(2,1)}, u32[]{:S(2)}, u32[]{:S(2)}) collective-permute-start(bf16[16,24,1664]{2,1,0:T(8,128)(2,1)S(1)} %constant_dynamic-update-slice_fusion.16.p2), channel_id=1, source_target_pairs={{0,4},{4,0},{8,12},{12,8},{16,20},{20,16},{24,28},{28,24},{1,5},{5... | collective-permute-start | bytes 3833864 | tf_op jit(solution)/shard_map/ppermute | solution.py:13
  61.0 3.0 collective-permute-start.5
  185.6 8.1 %collective-permute-start.9 = (bf16[4,96,4608]{2,1,0:T(8,128)(2,1)}, bf16[4,96,4608]{2,1,0:T(8,128)(2,1)}, u32[]{:S(2)}, u32[]{:S(2)}) collective-permute-start(bf16[4,96,4608]{2,1,0:T(8,128)(2,1)} %get-tuple-element.105), channel_id=1, source_target_pairs={{0,4},{4,0},{8,12},{12,8},{16,20},{20,16},{24,28},{28,24},{1,5},{5... | collective-permute-start | bytes 10616840 | tf_op jit(solution)/shard_map/ppermute | solution.py:13
  199.8 24.5 %collective-permute-start.10 = (bf16[4,96,2304]{2,1,0:T(8,128)(2,1)S(1)}, bf16[4,96,2304]{2,1,0:T(8,128)(2,1)S(1)}, u32[]{:S(2)}, u32[]{:S(2)}) collective-permute-start(bf16[4,96,2304]{2,1,0:T(8,128)(2,1)S(1)} %copy-done.30), channel_id=1, source_target_pairs={{0,4},{4,0},{8,12},{12,8},{16,20},{20,16},{24,28},{28,24},{1,5},{5... | collective-permute-start | bytes 5308424 | tf_op jit(solution)/shard_map/ppermute | solution.py:13
  224.2 9.8 %copy-start.3 = (bf16[4,96,2304]{2,1,0:T(8,128)(2,1)}, bf16[4,96,2304]{2,1,0:T(8,128)(2,1)S(1)}, u32[]{:S(2)}) copy-start(bf16[4,96,2304]{2,1,0:T(8,128)(2,1)S(1)} %collective-permute-done.10) | copy-start | bytes 5308420
  224.2 9.9 %copy-start.14 = (f32[16,768]{1,0:T(8,128)S(1)}, f32[16,768]{1,0:T(8,128)}, u32[]{:S(2)}) copy-start(f32[16,768]{1,0:T(8,128)} %get-tuple-element.97) | copy-start | bytes 147460
  224.2 10.6 %copy-start.12 = (f32[32,1,128]{2,1,0:T(1,128)S(1)}, f32[32,1,128]{2,1,0:T(1,128)}, u32[]{:S(2)}) copy-start(f32[32,1,128]{2,1,0:T(1,128)} %get-tuple-element.191) | copy-start | bytes 49156
  234.0 6.3 %collective-permute-start.11 = (bf16[4,96,2432]{2,1,0:T(8,128)(2,1)}, bf16[4,96,2432]{2,1,0:T(8,128)(2,1)S(1)}, u32[]{:S(2)}, u32[]{:S(2)}) collective-permute-start(bf16[4,96,2432]{2,1,0:T(8,128)(2,1)} %get-tuple-element.119), channel_id=1, source_target_pairs={{0,4},{4,0},{8,12},{12,8},{16,20},{20,16},{24,28},{28,24},{1,5},{5... | collective-permute-start | bytes 5603336 | tf_op jit(solution)/shard_map/ppermute | solution.py:13
  240.4 23.5 %collective-permute-start.16 = (bf16[2,96,2304]{2,1,0:T(8,128)(2,1)}, bf16[2,96,2304]{2,1,0:T(8,128)(2,1)}, u32[]{:S(2)}, u32[]{:S(2)}) collective-permute-start(bf16[2,96,2304]{2,1,0:T(8,128)(2,1)} %get-tuple-element.153), channel_id=1, source_target_pairs={{0,16},{4,20},{8,24},{12,28},{16,0},{20,4},{24,8},{28,12},{1,17},{... | collective-permute-start | bytes 2654216 | tf_op jit(solution)/shard_map/ppermute | solution.py:13
  242.8 23.1 %collective-permute-start.15 = (bf16[2,96,2432]{2,1,0:T(8,128)(2,1)}, bf16[2,96,2432]{2,1,0:T(8,128)(2,1)S(1)}, u32[]{:S(2)}, u32[]{:S(2)}) collective-permute-start(bf16[2,96,2432]{2,1,0:T(8,128)(2,1)} %get-tuple-element.150), channel_id=1, source_target_pairs={{0,8},{4,12},{8,0},{12,4},{16,24},{20,28},{24,16},{28,20},{1,9},{5... | collective-permute-start | bytes 2801672 | tf_op jit(solution)/shard_map/ppermute | solution.py:13
  244.9 21.0 %collective-permute-start.12 = (bf16[24,4608]{1,0:T(8,128)(2,1)}, bf16[24,4608]{1,0:T(8,128)(2,1)S(1)}, u32[]{:S(2)}, u32[]{:S(2)}) collective-permute-start(bf16[24,4608]{1,0:T(8,128)(2,1)} %get-tuple-element.156), channel_id=1, source_target_pairs={{0,1},{1,0},{2,3},{3,2},{4,5},{5,4},{6,7},{7,6},{8,9},{9,8},{10,11... | collective-permute-start | bytes 663560 | tf_op jit(solution)/shard_map/ppermute | solution.py:13
  245.9 20.1 %collective-permute-start.13 = (bf16[24,4608]{1,0:T(8,128)(2,1)}, bf16[24,4608]{1,0:T(8,128)(2,1)S(1)}, u32[]{:S(2)}, u32[]{:S(2)}) collective-permute-start(bf16[24,4608]{1,0:T(8,128)(2,1)} %get-tuple-element.155), channel_id=1, source_target_pairs={{0,2},{1,3},{2,0},{3,1},{4,6},{5,7},{6,4},{7,5},{8,10},{9,11},{10,... | collective-permute-start | bytes 663560 | tf_op jit(solution)/shard_map/ppermute | solution.py:13
  249.3 14.3 %copy-start.11 = (f32[32,1,128]{2,1,0:T(1,128)S(1)}, f32[32,1,128]{2,1,0:T(1,128)}, u32[]{:S(2)}) copy-start(f32[32,1,128]{2,1,0:T(1,128)} %get-tuple-element.192) | copy-start | bytes 49156
  249.3 17.6 %collective-permute-start.14 = (bf16[24,4608]{1,0:T(8,128)(2,1)}, bf16[24,4608]{1,0:T(8,128)(2,1)}, u32[]{:S(2)}, u32[]{:S(2)}) collective-permute-start(bf16[24,4608]{1,0:T(8,128)(2,1)} %get-tuple-element.154), channel_id=1, source_target_pairs={{0,3},{1,2},{2,1},{3,0},{4,7},{5,6},{6,5},{7,4},{8,11},{9,10},{10,... | collective-permute-start | bytes 663560 | tf_op jit(solution)/shard_map/ppermute | solution.py:13
  258.2 14.7 %all-to-all-start.1 = ((f32[32,4,128]{2,1,0:T(4,128)}), f32[32,4,128]{2,1,0:T(4,128)S(1)}, u32[]{:S(2)}, u32[]{:S(2)}) async-start(f32[32,4,128]{2,1,0:T(4,128)} %reshape.116), calls=%async_computation.2 | async-start | bytes 131072 | tf_op jit(solution)/shard_map/all_to_all | solution.py:699
  269.3 13.4 %collective-permute-start.17 = (bf16[1,96,2432]{2,1,0:T(8,128)(2,1)}, bf16[1,96,2432]{2,1,0:T(8,128)(2,1)S(1)}, u32[]{:S(2)}, u32[]{:S(2)}) collective-permute-start(bf16[1,96,2432]{2,1,0:T(8,128)(2,1)} %constant_dynamic-slice_fusion.1), channel_id=1, source_target_pairs={{0,16},{4,20},{8,24},{12,28},{16,0},{20,4},{24,8},{28,12},{1,17},{... | collective-permute-start | bytes 1400840 | tf_op jit(solution)/shard_map/ppermute | solution.py:13
  271.7 11.1 %collective-permute-start.18 = (bf16[1,96,2304]{2,1,0:T(8,128)(2,1)S(1)}, bf16[1,96,2304]{2,1,0:T(8,128)(2,1)S(1)}, u32[]{:S(2)}, u32[]{:S(2)}) collective-permute-start(bf16[1,96,2304]{2,1,0:T(8,128)(2,1)S(1)} %constant_dynamic-slice_fusion), channel_id=1, source_target_pairs={{0,8},{4,12},{8,0},{12,4},{16,24},{20,28},{24,16},{28,20},{1,9},{5... | collective-permute-start | bytes 1327112 | tf_op jit(solution)/shard_map/ppermute | solution.py:13
  282.9 8.5 %copy-start.8 = (bf16[24,4608]{1,0:T(8,128)(2,1)S(1)}, bf16[24,4608]{1,0:T(8,128)(2,1)}, u32[]{:S(2)}) copy-start(bf16[24,4608]{1,0:T(8,128)(2,1)} %copy-done.7) | copy-start | bytes 663556
  282.9 8.5 %copy-start.10 = (bf16[24,4608]{1,0:T(8,128)(2,1)S(1)}, bf16[24,4608]{1,0:T(8,128)(2,1)}, u32[]{:S(2)}) copy-start(bf16[24,4608]{1,0:T(8,128)(2,1)} %copy-done.9) | copy-start | bytes 663556
  285.6 14.1 %collective-permute-start.21 = (bf16[24,4736]{1,0:T(8,128)(2,1)}, bf16[24,4736]{1,0:T(8,128)(2,1)}, u32[]{:S(2)}, u32[]{:S(2)}) collective-permute-start(bf16[24,4736]{1,0:T(8,128)(2,1)} %pad_maximum_fusion.6), channel_id=1, source_target_pairs={{0,3},{1,2},{2,1},{3,0},{4,7},{5,6},{6,5},{7,4},{8,11},{9,10},{10,... | collective-permute-start | bytes 681992 | tf_op jit(solution)/shard_map/ppermute | solution.py:13
  289.4 16.9 %collective-permute-start.20 = (bf16[24,4736]{1,0:T(8,128)(2,1)}, bf16[24,4736]{1,0:T(8,128)(2,1)}, u32[]{:S(2)}, u32[]{:S(2)}) collective-permute-start(bf16[24,4736]{1,0:T(8,128)(2,1)} %pad_maximum_fusion.5), channel_id=1, source_target_pairs={{0,2},{1,3},{2,0},{3,1},{4,6},{5,7},{6,4},{7,5},{8,10},{9,11},{10,... | collective-permute-start | bytes 681992 | tf_op jit(solution)/shard_map/ppermute | solution.py:13
  290.2 16.1 %collective-permute-start.19 = (bf16[24,4736]{1,0:T(8,128)(2,1)}, bf16[24,4736]{1,0:T(8,128)(2,1)}, u32[]{:S(2)}, u32[]{:S(2)}) collective-permute-start(bf16[24,4736]{1,0:T(8,128)(2,1)} %pad_maximum_fusion.4), channel_id=1, source_target_pairs={{0,1},{1,0},{2,3},{3,2},{4,5},{5,4},{6,7},{7,6},{8,9},{9,8},{10,11... | collective-permute-start | bytes 681992 | tf_op jit(solution)/shard_map/ppermute | solution.py:13
  (24 other events, 62.8 us)
Sparse Core Ops, SparseCore 0:
  11.9 94.0 all-gather.1
  198.4 43.7 reduce-scatter.1

commit v3 on v2

--- a/solution.py
+++ b/solution.py
@@ -263,31 +263,27 @@
     mid=rest.astype(BF16).astype(F32)
     return jnp.where(lane<16,hi,jnp.where(lane<32,mid,jnp.where(lane<48,rest-mid,0.0)))
 
-def attention_grad_kernel(mix_ref,ctx_ref,dctx_ref,inv_ref,wts_ref,out_ref,de_ref):
+def attention_grad_kernel(q_ref,k_ref,v_ref,ctx_ref,dctx_ref,inv_ref,wts_ref,out_ref):
     p=pl.program_id(1)
-    width=ctx_ref.shape[1]
+    width=out_ref.shape[1]//3
     lane=lax.broadcasted_iota(jnp.int32,(PACK,LANES),1)
-    @pl.when(p==0)
-    def _():
-        prod=dctx_ref[...].astype(F32)*ctx_ref[...].astype(F32)
-        hi=prod.astype(BF16); lo=(prod-hi.astype(F32)).astype(BF16)
-        wr=lax.broadcasted_iota(jnp.int32,(width,LANES),0); wl=lax.broadcasted_iota(jnp.int32,(width,LANES),1)
-        pick=jnp.where(jnp.logical_and(wl<48,wl%16==wr//HEAD_DIM),1.0,0.0).astype(BF16)
-        dots=(dot_nn(hi,pick)+dot_nn(lo,pick))*inv_ref[...]
-        de_ref[...]=(-split_three(dots,lane)).astype(BF16)
     at=lambda base: pl.ds(pl.multiple_of(base+p*LANES,LANES),LANES)
-    q2=mix_ref[:,at(0)]; k2=mix_ref[:,at(width)]; v2=mix_ref[:,at(2*width)]; d2=dctx_ref[:,at(0)].astype(F32)
+    q2=q_ref[...]; k2=k_ref[...]; v2=v_ref[...]; d2=dctx_ref[...].astype(F32)
     invs=[jnp.sum(jnp.where(lane==2*p+half,inv_ref[...],0.0),axis=1,keepdims=True) for half in range(2)]
-    d2=(d2*jnp.where(lane<HEAD_DIM,invs[0],invs[1])).astype(BF16)
+    d2=d2*jnp.where(lane<HEAD_DIM,invs[0],invs[1])
+    prod=d2*ctx_ref[...].astype(F32)
+    d2=d2.astype(BF16)
     qt=q2.T; dt=d2.T
-    de=de_ref[...]
+    mark=head_lanes(lane,0).astype(BF16)
+    vx=jnp.concatenate([v2,mark],axis=1)
     dq=[]; dks=[]; dvs=[]
     for half in range(2):
         here=lane//HEAD_DIM==half
         dm=jnp.where(here,d2,jnp.zeros_like(d2))
-        mark=jnp.where(head_lanes(lane,2*p+half),1.0,0.0).astype(BF16)
+        dots=jnp.sum(jnp.where(here,prod,0.0),axis=1,keepdims=True)
+        de=(-split_three(jnp.broadcast_to(dots,(PACK,LANES)),lane)).astype(BF16)
         w=wts_ref[half]
-        dp=dot_nt(jnp.concatenate([dm,de],axis=1),jnp.concatenate([v2,mark],axis=1))
+        dp=dot_nt(jnp.concatenate([dm,de],axis=1),vx)
         ds=(w.astype(F32)*dp).astype(BF16)
         rows=slice(half*HEAD_DIM,(half+1)*HEAD_DIM)
         dq.append(dot_nn(ds,k2))
@@ -299,13 +295,12 @@
 
 def attention_grad(mix,ctx,dctx,inv,wts):
     rows,width=ctx.shape; wide=mix.shape[1]; pairs=HEADS//2
-    b=lambda n: pl.BlockSpec((PACK,n),lambda g,p:(g,0))
+    pair=lambda at: pl.BlockSpec((PACK,LANES),lambda g,p:(g,at*pairs+p))
     return pl.pallas_call(attention_grad_kernel,grid=(rows//PACK,pairs),
-        in_specs=[b(wide),b(width),b(width),b(LANES),pl.BlockSpec((2,PACK,PACK),lambda g,p:(g*pairs+p,0,0))],
-        out_specs=b(wide),out_shape=jax.ShapeDtypeStruct((rows,wide),BF16),
-        scratch_shapes=[pltpu.VMEM((PACK,LANES),BF16)],
+        in_specs=[pair(0),pair(1),pair(2),pair(0),pair(0),pl.BlockSpec((PACK,LANES),lambda g,p:(g,0)),pl.BlockSpec((2,PACK,PACK),lambda g,p:(g*pairs+p,0,0))],
+        out_specs=pl.BlockSpec((PACK,wide),lambda g,p:(g,0)),out_shape=jax.ShapeDtypeStruct((rows,wide),BF16),
         compiler_params=pltpu.CompilerParams(vmem_limit_bytes=VMEM_MOST),name='attention_grad',
-        cost_estimate=pl.CostEstimate(flops=16*rows*PACK*width,bytes_accessed=rows*wide*8,transcendentals=0))(mix,ctx,dctx,inv,wts)
+        cost_estimate=pl.CostEstimate(flops=16*rows*PACK*width,bytes_accessed=rows*wide*8,transcendentals=0))(mix,mix,mix,ctx,dctx,inv,wts)
 TILE=256
 def half_tail(a, e):
     t=1.0/(1.0+0.3275911*a)

time: 321 us -> 318 us (level); the launches traced: 317 us -> 317 us
  starting transfers between devices: 29 us -> 33.5 us
    ppermute x22, starting transfers between devices: 23.5 us -> 27.3 us  [swap(): return lax.ppermute(block, axis, [(i, i ^ mask) for i in range(size)])]
  transfers between devices with their start and end apart: 25 -> 25, of which waited for: 11 -> 12; matrix products, arithmetic and copies ran while one was open for 8% -> 8% of each run, Pallas kernels for 26% -> 25%
where the time goes in v3:
time: 318 us; the launch traced here: 317 us
  Pallas kernels  147 us (46%)
  waiting for transfers between devices  67 us (21%)
  starting transfers between devices  33.5 us (11%)
  local copies, waits for them, and re-layouts  26 us (8%)
  other arithmetic  18.2 us (6%)
  between operations  14.9 us (5%)
  blocking collectives  10.3 us (3%)
    ppermute x22, waiting for transfers between devices, swap(): return lax.ppermute(block, axis, [(i, i ^ mask) for i in range(size)])  54.9 us
    pallas_call x1, Pallas kernels, attention(): pl.pallas_call(functools.partial(attention_kernel, orders, fsdp, small),...  30.5 us
    pallas_call x1, Pallas kernels, feed_forward(): pl.pallas_call(feed_forward_kernel, grid=(rows // TILE,), in_specs=[pl.Bl...  27.6 us
    ppermute x22, starting transfers between devices, swap(): return lax.ppermute(block, axis, [(i, i ^ mask) for i in range(size)])  27.3 us
    pallas_call x1, Pallas kernels, feed_forward_grad(): pl.pallas_call(feed_forward_grad_kernel, grid=(rows // TILE,), in_specs=[...  25.8 us
    pallas_call x1, Pallas kernels, attention_grad(): pl.pallas_call(attention_grad_kernel, grid=(rows // PACK, pairs), in_spec...  22.9 us
    pallas_call x1, Pallas kernels, early_grads(): pl.pallas_call(functools.partial(early_kernel, reps), grid=(n,), in_specs...  14.3 us
    all_gather x1, waiting for transfers between devices, shards(): rest_full = lax.all_gather(rest, AXES, axis=0, tiled=True)  11.5 us
  transfers between devices with their start and end apart: 25, of which 12 were waited for; matrix products, arithmetic and copies ran while one was open for 8% of the time, Pallas kernels for 25%

profile of v3, /device:TPU:0, one launch (start us, length us, event | category | flops | bytes accessed | tf_op | source)
XLA Modules:
  0.0 317.3 jit_solution(15341656451845484808)
XLA Ops:
  7.2 2.1 reshape.111
  12.1 3.1 collective-permute-start
  15.2 2.6 collective-permute-start.1
  17.9 10.3 %collective-permute-done.2 = bf16[24,3200]{1,0:T(8,128)(2,1)S(1)} collective-permute-done((bf16[24,3200]{1,0:T(8,128)(2,1)S(1)}, bf16[24,3200]{1,0:T(8,128)(2,1)S(1)}, u32[]{:S(2)}, u32[]{:S(2)}) %collective-permute-start.2) | collective-permute-done | bytes 153632 | tf_op jit(solution)/shard_map/ppermute | solution.py:13
  28.2 4.4 %collective-permute-done.1 = bf16[24,3200]{1,0:T(8,128)(2,1)S(1)} collective-permute-done((bf16[24,3200]{1,0:T(8,128)(2,1)S(1)}, bf16[24,3200]{1,0:T(8,128)(2,1)S(1)}, u32[]{:S(2)}, u32[]{:S(2)}) %collective-permute-start.1) | collective-permute-done | bytes 153632 | tf_op jit(solution)/shard_map/ppermute | solution.py:13
  34.3 1.6 collective-permute-start.3
  36.0 5.9 %collective-permute-done.6 = bf16[4,24,1664]{2,1,0:T(8,128)(2,1)S(1)} collective-permute-done((bf16[4,24,1664]{2,1,0:T(8,128)(2,1)S(1)}, bf16[4,24,1664]{2,1,0:T(8,128)(2,1)S(1)}, u32[]{:S(2)}, u32[]{:S(2)}) %collective-permute-start.6) | collective-permute-done | bytes 319520 | tf_op jit(solution)/shard_map/ppermute | solution.py:13
  41.9 1.9 collective-permute-start.7
  44.3 1.8 collective-permute-start.4
  46.2 11.1 %collective-permute-done.7 = bf16[8,24,1664]{2,1,0:T(8,128)(2,1)S(1)} collective-permute-done((bf16[8,24,1664]{2,1,0:T(8,128)(2,1)S(1)}, bf16[8,24,1664]{2,1,0:T(8,128)(2,1)S(1)}, u32[]{:S(2)}, u32[]{:S(2)}) %collective-permute-start.7) | collective-permute-done | bytes 639008 | tf_op jit(solution)/shard_map/ppermute | solution.py:13
  57.5 3.5 %collective-permute-done.4 = bf16[8,24,1536]{2,1,0:T(8,128)(2,1)S(1)} collective-permute-done((bf16[8,24,1536]{2,1,0:T(8,128)(2,1)S(1)}, bf16[8,24,1536]{2,1,0:T(8,128)(2,1)S(1)}, u32[]{:S(2)}, u32[]{:S(2)}) %collective-permute-start.4) | collective-permute-done | bytes 589856 | tf_op jit(solution)/shard_map/ppermute | solution.py:13
  61.8 2.2 collective-permute-done.5.p1
  64.1 30.5 %attention.1 = (bf16[768,3200]{1,0:T(8,128)(2,1)}, f32[16,768]{1,0:T(8,128)}, bf16[1024,2304]{1,0:T(8,128)(2,1)}, bf16[1024,768]{1,0:T(8,128)(2,1)}, f32[1024,12...) custom-call(s32[2,4]{1,0:T(2,128)} %lens_ref.5, ...), custom_call_target="tpu_custom_call" | custom-call | flops 6845104128 | bytes 9437184 | tf_op jit(solution)/shard_map/attention/pallas_call | solution.py:254
  94.5 11.5 %all-gather.2.cloned.1.call-done.w_ref = bf16[768,6272]{1,0:T(8,128)(2,1)} async-done(((bf16[24,6272]{1,0:T(8,128)(2,1)}), bf16[768,6272]{1,0:T(8,128)(2,1)}) %all-gather.2.cloned.1.call-update) | async-done | bytes 9633808 | tf_op jit(solution)/shard_map/all_gather | solution.py:608
  106.0 27.6 %feed_forward.1 = (bf16[1024,3072]{1,0:T(8,128)(2,1)}, bf16[1024,3072]{1,0:T(8,128)(2,1)}, f32[1024,768]{1,0:T(8,128)}, f32[1024,128]{1,0:T(8,128)}, bf16[1024,7...) custom-call(s32[2,4]{1,0:T(2,128)} %lens_ref.5, ...), custom_call_target="tpu_custom_call" | custom-call | tf_op jit(solution)/shard_map/feed_forward/pallas_call | solution.py:368
  134.3 10.3 %all_to_all.10 = f32[32,2,128]{2,1,0:T(2,128)S(1)} all-to-all(f32[32,2,128]{2,1,0:T(2,128)S(1)} %broadcast_in_dim.25), channel_id=1, replica_groups=mesh['dp'=8,'fsdp'=4] {'dp','fsdp'}, dimensions={0} | all-to-all | bytes 65536 | tf_op jit(solution)/shard_map/all_to_all | solution.py:550
  145.2 25.8 %feed_forward_grad.1 = (bf16[1024,4608]{1,0:T(8,128)(2,1)}, f32[1024,768]{1,0:T(8,128)}, bf16[1024,768]{1,0:T(8,128)(2,1)}, f32[16,768]{1,0:T(8,128)}, bf16[768,128]{1,0:T(8,128)(2,1)}) custom-call(s32[2,4]{1,0:T(2,128)} %lens_ref.5, s32[8]{0:T(128)} %bitcast.128, f32[1,128]{1,0:T(1,128)} %get-tuple-element.87.doc_ref, f32[32,128]{1,0:T(8,128)} %bitcast.121, ...), custom_call_target="tpu_custom_call" | custom-call | tf_op jit(solution)/shard_map/feed_forward_grad/pallas_call | solution.py:433
  171.1 14.3 %early_weight_grads.1 = (bf16[4,96,4608]{2,1,0:T(8,128)(2,1)}, bf16[4,96,4608]{2,1,0:T(8,128)(2,1)}) custom-call(s32[2]{0:T(128)} %pad_add_fusion.me_ref, bf16[1024,768]{1,0:T(8,128)(2,1)} %get-tuple-element.85.low_ref.low_hbm, bf16[1024,3072]{1,0:T(8,128)(2,1)} %get-tuple-element.102.act_hbm.act_ref, bf16[1024,768]{1,0:T(8,128)(2,1)} %get-tuple-element.99.ctx_hbm.ctx_ref, ...), custom_call_target="tpu_custom_call" | custom-call | flops 7247757312 | bytes 18874368 | tf_op jit(solution)/shard_map/early_weight_grads/pallas_call | solution.py:475
  185.4 8.1 %outer_weight_grad.1 = (bf16[4,96,2304]{2,1,0:T(8,128)(2,1)}, bf16[4,96,2304]{2,1,0:T(8,128)(2,1)}) custom-call(s32[2]{0:T(128)} %pad_add_fusion.me_ref, bf16[1024,3072]{1,0:T(8,128)(2,1)} %get-tuple-element.102.act_hbm.act_ref, bf16[1024,4608]{1,0:T(8,128)(2,1)} %get-tuple-element.106.right_ref.olow_ref), custom_call_target="tpu_custom_call" | custom-call | flops 3623878656 | bytes 9437184 | tf_op jit(solution)/shard_map/outer_weight_grad/pallas_call | solution.py:487
  193.5 4.6 %add_convert_fusion = bf16[4,96,4608]{2,1,0:T(8,128)(2,1)} fusion(bf16[4,96,4608]{2,1,0:T(8,128)(2,1)} %collective-permute-done.9, bf16[4,96,4608]{2,1,0:T(8,128)(2,1)S(1)} %copy-done), kind=kLoop, calls=%fused_computation | loop fusion | flops 7077888 | bytes 10616832 | tf_op jit(solution)/shard_map/convert_element_type | solution.py:65
  200.0 22.9 %attention_grad.1.mg_ref.refs_0_ = bf16[1024,2304]{1,0:T(8,128)(2,1)} custom-call(bf16[1024,2304]{1,0:T(8,128)(2,1)} %get-tuple-element.98.q_ref.k_ref.v_ref, bf16[1024,2304]{1,0:T(8,128)(2,1)} %get-tuple-element.98.q_ref.k_ref.v_ref, bf16[1024,2304]{1,0:T(8,128)(2,1)} %get-tuple-element.98.q_ref.k_ref.v_ref, ...), custom_call_target="tpu_custom_call" | custom-call | flops 6442450944 | bytes 18874368 | tf_op jit(solution)/shard_map/attention_grad/pallas_call | solution.py:299
  222.9 9.3 %late_weight_grads.1 = (bf16[4,96,2432]{2,1,0:T(8,128)(2,1)}, bf16[4,96,2432]{2,1,0:T(8,128)(2,1)}, f32[8,2304]{1,0:T(8,128)}) custom-call(s32[2]{0:T(128)} %pad_add_fusion.me_ref, bf16[1024,768]{1,0:T(8,128)(2,1)} %tok_ref.3, bf16[1024,2304]{1,0:T(8,128)(2,1)} %attention_grad.1.mg_ref.refs_0_, bf16[768,128]{1,0:T(8,128)(2,1)} %get-tuple-element.114.span_ref), custom_call_target="tpu_custom_call" | custom-call | flops 3623878656 | bytes 9437184 | tf_op jit(solution)/shard_map/late_weight_grads/pallas_call | solution.py:507
  235.0 2.4 add_convert_fusion.2
  242.0 2.1 dynamic-slice_bitcast_fusion.4
  245.6 4.1 %collective-permute-start.13 = (bf16[24,4608]{1,0:T(8,128)(2,1)}, bf16[24,4608]{1,0:T(8,128)(2,1)S(1)}, u32[]{:S(2)}, u32[]{:S(2)}) collective-permute-start(bf16[24,4608]{1,0:T(8,128)(2,1)} %get-tuple-element.155), channel_id=1, source_target_pairs={{0,2},{1,3},{2,0},{3,1},{4,6},{5,7},{6,4},{7,5},{8,10},{9,11},{10,... | collective-permute-start | bytes 663560 | tf_op jit(solution)/shard_map/ppermute | solution.py:13
  249.6 8.8 %input_grad.1 = f32[1024,768]{1,0:T(8,128)} custom-call(bf16[768,3200]{1,0:T(8,128)(2,1)} %get-tuple-element.95.aw_ref.w_ref, f32[1024,768]{1,0:T(8,128)} %get-tuple-element.127.fs_ref, bf16[1024,2304]{1,0:T(8,128)(2,1)} %attention_grad.1.mg_ref.refs_0_), custom_call_target="tpu_custom_call" | custom-call | flops 3623878656 | bytes 12582912 | tf_op jit(solution)/shard_map/input_grad/pallas_call | solution.py:528
  258.5 6.2 %all-to-all-start.1 = ((f32[32,4,128]{2,1,0:T(4,128)}), f32[32,4,128]{2,1,0:T(4,128)S(1)}, u32[]{:S(2)}, u32[]{:S(2)}) async-start(f32[32,4,128]{2,1,0:T(4,128)} %reshape.116), calls=%async_computation.2 | async-start | bytes 131072 | tf_op jit(solution)/shard_map/all_to_all | solution.py:694
  268.2 1.8 collective-permute-start.17
  273.7 9.7 %collective-permute-done.18 = bf16[1,96,2304]{2,1,0:T(8,128)(2,1)S(1)} collective-permute-done((bf16[1,96,2304]{2,1,0:T(8,128)(2,1)S(1)}, bf16[1,96,2304]{2,1,0:T(8,128)(2,1)S(1)}, u32[]{:S(2)}, u32[]{:S(2)}) %collective-permute-start.18) | collective-permute-done | bytes 442400 | tf_op jit(solution)/shard_map/ppermute | solution.py:13
  286.3 3.4 %collective-permute-start.21 = (bf16[24,4736]{1,0:T(8,128)(2,1)}, bf16[24,4736]{1,0:T(8,128)(2,1)}, u32[]{:S(2)}, u32[]{:S(2)}) collective-permute-start(bf16[24,4736]{1,0:T(8,128)(2,1)} %pad_maximum_fusion.6), channel_id=1, source_target_pairs={{0,3},{1,2},{2,1},{3,0},{4,7},{5,6},{6,5},{7,4},{8,11},{9,10},{10,... | collective-permute-start | bytes 681992 | tf_op jit(solution)/shard_map/ppermute | solution.py:13
  296.4 2.6 reshape.124
  300.5 6.6 %collective-permute-done.20 = bf16[24,4736]{1,0:T(8,128)(2,1)} collective-permute-done((bf16[24,4736]{1,0:T(8,128)(2,1)}, bf16[24,4736]{1,0:T(8,128)(2,1)}, u32[]{:S(2)}, u32[]{:S(2)}) %collective-permute-start.20) | collective-permute-done | bytes 227360 | tf_op jit(solution)/shard_map/ppermute | solution.py:13
  (181 shorter events, 39.5 us)
Async XLA Ops:
  7.2 98.8 %all-gather.2.cloned.1.call-start = ((), (), s32[]{:S(2)}) async-start(), calls=%async_computation.3 | async-start | bytes 9934848 | tf_op jit(solution)/shard_map/all_gather | solution.py:608
  11.8 230.1 %reduce-scatter.2.cloned.1.call-start = ((), (), s32[]{:S(2)}) async-start(), calls=%async_computation.4 | async-start | bytes 4423680 | tf_op jit(solution)/shard_map/reduce_scatter | solution.py:658
  12.1 20.4 %collective-permute-start = (bf16[24,3200]{1,0:T(8,128)(2,1)S(1)}, bf16[24,3200]{1,0:T(8,128)(2,1)S(1)}, u32[]{:S(2)}, u32[]{:S(2)}) collective-permute-start(bf16[24,3200]{1,0:T(8,128)(2,1)S(1)} %fusion.1), channel_id=1, source_target_pairs={{0,1},{1,0},{2,3},{3,2},{4,5},{5,4},{6,7},{7,6},{8,9},{9,8},{10,11... | collective-permute-start | bytes 460808 | tf_op jit(solution)/shard_map/ppermute | solution.py:13
  15.2 17.3 %collective-permute-start.1 = (bf16[24,3200]{1,0:T(8,128)(2,1)S(1)}, bf16[24,3200]{1,0:T(8,128)(2,1)S(1)}, u32[]{:S(2)}, u32[]{:S(2)}) collective-permute-start(bf16[24,3200]{1,0:T(8,128)(2,1)S(1)} %fusion.1), channel_id=1, source_target_pairs={{0,2},{1,3},{2,0},{3,1},{4,6},{5,7},{6,4},{7,5},{8,10},{9,11},{10,... | collective-permute-start | bytes 460808 | tf_op jit(solution)/shard_map/ppermute | solution.py:13
  17.8 10.4 %collective-permute-start.2 = (bf16[24,3200]{1,0:T(8,128)(2,1)S(1)}, bf16[24,3200]{1,0:T(8,128)(2,1)S(1)}, u32[]{:S(2)}, u32[]{:S(2)}) collective-permute-start(bf16[24,3200]{1,0:T(8,128)(2,1)S(1)} %fusion.1), channel_id=1, source_target_pairs={{0,3},{1,2},{2,1},{3,0},{4,7},{5,6},{6,5},{7,4},{8,11},{9,10},{10,... | collective-permute-start | bytes 460808 | tf_op jit(solution)/shard_map/ppermute | solution.py:13
  32.6 9.2 %collective-permute-start.6 = (bf16[4,24,1664]{2,1,0:T(8,128)(2,1)S(1)}, bf16[4,24,1664]{2,1,0:T(8,128)(2,1)S(1)}, u32[]{:S(2)}, u32[]{:S(2)}) collective-permute-start(bf16[4,24,1664]{2,1,0:T(8,128)(2,1)S(1)} %pad_maximum_fusion), channel_id=1, source_target_pairs={{0,8},{4,12},{8,0},{12,4},{16,24},{20,28},{24,16},{28,20},{1,9},{5... | collective-permute-start | bytes 958472 | tf_op jit(solution)/shard_map/ppermute | solution.py:13
  34.3 10.0 %collective-permute-start.3 = (bf16[4,24,1536]{2,1,0:T(8,128)(2,1)S(1)}, bf16[4,24,1536]{2,1,0:T(8,128)(2,1)S(1)}, u32[]{:S(2)}, u32[]{:S(2)}) collective-permute-start(bf16[4,24,1536]{2,1,0:T(8,128)(2,1)S(1)} %pad_maximum_fusion.1), channel_id=1, source_target_pairs={{0,16},{4,20},{8,24},{12,28},{16,0},{20,4},{24,8},{28,12},{1,17},{... | collective-permute-start | bytes 884744 | tf_op jit(solution)/shard_map/ppermute | solution.py:13
  41.9 15.4 %collective-permute-start.7 = (bf16[8,24,1664]{2,1,0:T(8,128)(2,1)S(1)}, bf16[8,24,1664]{2,1,0:T(8,128)(2,1)S(1)}, u32[]{:S(2)}, u32[]{:S(2)}) collective-permute-start(bf16[8,24,1664]{2,1,0:T(8,128)(2,1)S(1)} %get-tuple-element.171), channel_id=1, source_target_pairs={{0,16},{4,20},{8,24},{12,28},{16,0},{20,4},{24,8},{28,12},{1,17},{... | collective-permute-start | bytes 1916936 | tf_op jit(solution)/shard_map/ppermute | solution.py:13
  43.9 18.0 %copy-start.29 = (s32[8,1]{0,1:T(1,128)S(1)}, s32[8,1]{0,1:T(1,128)}, u32[]{:S(2)}) copy-start(s32[8,1]{0,1:T(1,128)} %param.22) | copy-start | bytes 100
  44.3 16.6 %collective-permute-start.4 = (bf16[8,24,1536]{2,1,0:T(8,128)(2,1)S(1)}, bf16[8,24,1536]{2,1,0:T(8,128)(2,1)S(1)}, u32[]{:S(2)}, u32[]{:S(2)}) collective-permute-start(bf16[8,24,1536]{2,1,0:T(8,128)(2,1)S(1)} %get-tuple-element.173), channel_id=1, source_target_pairs={{0,8},{4,12},{8,0},{12,4},{16,24},{20,28},{24,16},{28,20},{1,9},{5... | collective-permute-start | bytes 1769480 | tf_op jit(solution)/shard_map/ppermute | solution.py:13
  57.4 6.7 %collective-permute-start.8 = (bf16[16,24,1664]{2,1,0:T(8,128)(2,1)S(1)}, bf16[16,24,1664]{2,1,0:T(8,128)(2,1)}, u32[]{:S(2)}, u32[]{:S(2)}) collective-permute-start(bf16[16,24,1664]{2,1,0:T(8,128)(2,1)S(1)} %constant_dynamic-update-slice_fusion.16.p2), channel_id=1, source_target_pairs={{0,4},{4,0},{8,12},{12,8},{16,20},{20,16},{24,28},{28,24},{1,5},{5... | collective-permute-start | bytes 3833864 | tf_op jit(solution)/shard_map/ppermute | solution.py:13
  61.0 3.0 collective-permute-start.5
  185.3 8.1 %collective-permute-start.9 = (bf16[4,96,4608]{2,1,0:T(8,128)(2,1)}, bf16[4,96,4608]{2,1,0:T(8,128)(2,1)}, u32[]{:S(2)}, u32[]{:S(2)}) collective-permute-start(bf16[4,96,4608]{2,1,0:T(8,128)(2,1)} %get-tuple-element.105), channel_id=1, source_target_pairs={{0,4},{4,0},{8,12},{12,8},{16,20},{20,16},{24,28},{28,24},{1,5},{5... | collective-permute-start | bytes 10616840 | tf_op jit(solution)/shard_map/ppermute | solution.py:13
  199.5 23.4 %collective-permute-start.10 = (bf16[4,96,2304]{2,1,0:T(8,128)(2,1)S(1)}, bf16[4,96,2304]{2,1,0:T(8,128)(2,1)S(1)}, u32[]{:S(2)}, u32[]{:S(2)}) collective-permute-start(bf16[4,96,2304]{2,1,0:T(8,128)(2,1)S(1)} %copy-done.30), channel_id=1, source_target_pairs={{0,4},{4,0},{8,12},{12,8},{16,20},{20,16},{24,28},{28,24},{1,5},{5... | collective-permute-start | bytes 5308424 | tf_op jit(solution)/shard_map/ppermute | solution.py:13
  222.9 9.3 %copy-start.3 = (bf16[4,96,2304]{2,1,0:T(8,128)(2,1)}, bf16[4,96,2304]{2,1,0:T(8,128)(2,1)S(1)}, u32[]{:S(2)}) copy-start(bf16[4,96,2304]{2,1,0:T(8,128)(2,1)S(1)} %collective-permute-done.10) | copy-start | bytes 5308420
  222.9 9.5 %copy-start.14 = (f32[16,768]{1,0:T(8,128)S(1)}, f32[16,768]{1,0:T(8,128)}, u32[]{:S(2)}) copy-start(f32[16,768]{1,0:T(8,128)} %get-tuple-element.97) | copy-start | bytes 147460
  222.9 10.1 %copy-start.12 = (f32[32,1,128]{2,1,0:T(1,128)S(1)}, f32[32,1,128]{2,1,0:T(1,128)}, u32[]{:S(2)}) copy-start(f32[32,1,128]{2,1,0:T(1,128)} %get-tuple-element.191) | copy-start | bytes 49156
  232.2 6.6 %collective-permute-start.11 = (bf16[4,96,2432]{2,1,0:T(8,128)(2,1)}, bf16[4,96,2432]{2,1,0:T(8,128)(2,1)S(1)}, u32[]{:S(2)}, u32[]{:S(2)}) collective-permute-start(bf16[4,96,2432]{2,1,0:T(8,128)(2,1)} %get-tuple-element.119), channel_id=1, source_target_pairs={{0,4},{4,0},{8,12},{12,8},{16,20},{20,16},{24,28},{28,24},{1,5},{5... | collective-permute-start | bytes 5603336 | tf_op jit(solution)/shard_map/ppermute | solution.py:13
  238.5 26.4 %collective-permute-start.16 = (bf16[2,96,2304]{2,1,0:T(8,128)(2,1)}, bf16[2,96,2304]{2,1,0:T(8,128)(2,1)}, u32[]{:S(2)}, u32[]{:S(2)}) collective-permute-start(bf16[2,96,2304]{2,1,0:T(8,128)(2,1)} %get-tuple-element.153), channel_id=1, source_target_pairs={{0,16},{4,20},{8,24},{12,28},{16,0},{20,4},{24,8},{28,12},{1,17},{... | collective-permute-start | bytes 2654216 | tf_op jit(solution)/shard_map/ppermute | solution.py:13
  240.9 23.9 %collective-permute-start.15 = (bf16[2,96,2432]{2,1,0:T(8,128)(2,1)}, bf16[2,96,2432]{2,1,0:T(8,128)(2,1)S(1)}, u32[]{:S(2)}, u32[]{:S(2)}) collective-permute-start(bf16[2,96,2432]{2,1,0:T(8,128)(2,1)} %get-tuple-element.150), channel_id=1, source_target_pairs={{0,8},{4,12},{8,0},{12,4},{16,24},{20,28},{24,16},{28,20},{1,9},{5... | collective-permute-start | bytes 2801672 | tf_op jit(solution)/shard_map/ppermute | solution.py:13
  244.1 20.8 %collective-permute-start.12 = (bf16[24,4608]{1,0:T(8,128)(2,1)}, bf16[24,4608]{1,0:T(8,128)(2,1)S(1)}, u32[]{:S(2)}, u32[]{:S(2)}) collective-permute-start(bf16[24,4608]{1,0:T(8,128)(2,1)} %get-tuple-element.156), channel_id=1, source_target_pairs={{0,1},{1,0},{2,3},{3,2},{4,5},{5,4},{6,7},{7,6},{8,9},{9,8},{10,11... | collective-permute-start | bytes 663560 | tf_op jit(solution)/shard_map/ppermute | solution.py:13
  245.6 20.1 %collective-permute-start.13 = (bf16[24,4608]{1,0:T(8,128)(2,1)}, bf16[24,4608]{1,0:T(8,128)(2,1)S(1)}, u32[]{:S(2)}, u32[]{:S(2)}) collective-permute-start(bf16[24,4608]{1,0:T(8,128)(2,1)} %get-tuple-element.155), channel_id=1, source_target_pairs={{0,2},{1,3},{2,0},{3,1},{4,6},{5,7},{6,4},{7,5},{8,10},{9,11},{10,... | collective-permute-start | bytes 663560 | tf_op jit(solution)/shard_map/ppermute | solution.py:13
  249.6 15.0 %copy-start.11 = (f32[32,1,128]{2,1,0:T(1,128)S(1)}, f32[32,1,128]{2,1,0:T(1,128)}, u32[]{:S(2)}) copy-start(f32[32,1,128]{2,1,0:T(1,128)} %get-tuple-element.192) | copy-start | bytes 49156
  249.6 16.2 %collective-permute-start.14 = (bf16[24,4608]{1,0:T(8,128)(2,1)}, bf16[24,4608]{1,0:T(8,128)(2,1)}, u32[]{:S(2)}, u32[]{:S(2)}) collective-permute-start(bf16[24,4608]{1,0:T(8,128)(2,1)} %get-tuple-element.154), channel_id=1, source_target_pairs={{0,3},{1,2},{2,1},{3,0},{4,7},{5,6},{6,5},{7,4},{8,11},{9,10},{10,... | collective-permute-start | bytes 663560 | tf_op jit(solution)/shard_map/ppermute | solution.py:13
  258.5 15.3 %all-to-all-start.1 = ((f32[32,4,128]{2,1,0:T(4,128)}), f32[32,4,128]{2,1,0:T(4,128)S(1)}, u32[]{:S(2)}, u32[]{:S(2)}) async-start(f32[32,4,128]{2,1,0:T(4,128)} %reshape.116), calls=%async_computation.2 | async-start | bytes 131072 | tf_op jit(solution)/shard_map/all_to_all | solution.py:694
  268.2 15.2 %collective-permute-start.17 = (bf16[1,96,2432]{2,1,0:T(8,128)(2,1)}, bf16[1,96,2432]{2,1,0:T(8,128)(2,1)S(1)}, u32[]{:S(2)}, u32[]{:S(2)}) collective-permute-start(bf16[1,96,2432]{2,1,0:T(8,128)(2,1)} %constant_dynamic-slice_fusion.1), channel_id=1, source_target_pairs={{0,16},{4,20},{8,24},{12,28},{16,0},{20,4},{24,8},{28,12},{1,17},{... | collective-permute-start | bytes 1400840 | tf_op jit(solution)/shard_map/ppermute | solution.py:13
  271.4 12.0 %collective-permute-start.18 = (bf16[1,96,2304]{2,1,0:T(8,128)(2,1)S(1)}, bf16[1,96,2304]{2,1,0:T(8,128)(2,1)S(1)}, u32[]{:S(2)}, u32[]{:S(2)}) collective-permute-start(bf16[1,96,2304]{2,1,0:T(8,128)(2,1)S(1)} %constant_dynamic-slice_fusion), channel_id=1, source_target_pairs={{0,8},{4,12},{8,0},{12,4},{16,24},{20,28},{24,16},{28,20},{1,9},{5... | collective-permute-start | bytes 1327112 | tf_op jit(solution)/shard_map/ppermute | solution.py:13
  283.6 8.5 %copy-start.8 = (bf16[24,4608]{1,0:T(8,128)(2,1)S(1)}, bf16[24,4608]{1,0:T(8,128)(2,1)}, u32[]{:S(2)}) copy-start(bf16[24,4608]{1,0:T(8,128)(2,1)} %copy-done.7) | copy-start | bytes 663556
  283.6 8.5 %copy-start.10 = (bf16[24,4608]{1,0:T(8,128)(2,1)S(1)}, bf16[24,4608]{1,0:T(8,128)(2,1)}, u32[]{:S(2)}) copy-start(bf16[24,4608]{1,0:T(8,128)(2,1)} %copy-done.9) | copy-start | bytes 663556
  286.3 14.1 %collective-permute-start.21 = (bf16[24,4736]{1,0:T(8,128)(2,1)}, bf16[24,4736]{1,0:T(8,128)(2,1)}, u32[]{:S(2)}, u32[]{:S(2)}) collective-permute-start(bf16[24,4736]{1,0:T(8,128)(2,1)} %pad_maximum_fusion.6), channel_id=1, source_target_pairs={{0,3},{1,2},{2,1},{3,0},{4,7},{5,6},{6,5},{7,4},{8,11},{9,10},{10,... | collective-permute-start | bytes 681992 | tf_op jit(solution)/shard_map/ppermute | solution.py:13
  290.4 16.7 %collective-permute-start.20 = (bf16[24,4736]{1,0:T(8,128)(2,1)}, bf16[24,4736]{1,0:T(8,128)(2,1)}, u32[]{:S(2)}, u32[]{:S(2)}) collective-permute-start(bf16[24,4736]{1,0:T(8,128)(2,1)} %pad_maximum_fusion.5), channel_id=1, source_target_pairs={{0,2},{1,3},{2,0},{3,1},{4,6},{5,7},{6,4},{7,5},{8,10},{9,11},{10,... | collective-permute-start | bytes 681992 | tf_op jit(solution)/shard_map/ppermute | solution.py:13
  291.1 16.0 %collective-permute-start.19 = (bf16[24,4736]{1,0:T(8,128)(2,1)}, bf16[24,4736]{1,0:T(8,128)(2,1)}, u32[]{:S(2)}, u32[]{:S(2)}) collective-permute-start(bf16[24,4736]{1,0:T(8,128)(2,1)} %pad_maximum_fusion.4), channel_id=1, source_target_pairs={{0,1},{1,0},{2,3},{3,2},{4,5},{5,4},{6,7},{7,6},{8,9},{9,8},{10,11... | collective-permute-start | bytes 681992 | tf_op jit(solution)/shard_map/ppermute | solution.py:13
  (24 other events, 62.8 us)
Sparse Core Ops, SparseCore 0:
  11.9 94.0 all-gather.1
  198.2 43.7 reduce-scatter.1

commit v4 on v3

--- a/solution.py
+++ b/solution.py
@@ -710,6 +710,7 @@
     late_sum, takes = start_near([late_walk.keep, outer_walk.keep])
     received, early_takes, late_sum = tie(received, early_takes, late_sum)
     early_sum = add_near(early_sum, early_takes)
+    early_sum, received = tie(early_sum, received)
     mine = jnp.sum(received, axis=0)
     own_rows, own_biases, answer_own = unpack_lanes(
         mine, [n_rows * share, 3 * share, span // devices]

time: 318 us -> 320 us (level)
  transfers between devices with their start and end apart: 25 -> 25, of which waited for: 12 -> 12; matrix products, arithmetic and copies ran while one was open for 8% -> 7% of each run, Pallas kernels for 25% -> 25%
where the time goes in v4:
time: 320 us; the launch traced here: 319 us
  Pallas kernels  147 us (46%)
  waiting for transfers between devices  68.8 us (22%)
  starting transfers between devices  33.5 us (10%)
  local copies, waits for them, and re-layouts  26 us (8%)
  other arithmetic  18.2 us (6%)
  between operations  15 us (5%)
  blocking collectives  10.3 us (3%)
    ppermute x22, waiting for transfers between devices, swap(): return lax.ppermute(block, axis, [(i, i ^ mask) for i in range(size)])  56.7 us
    pallas_call x1, Pallas kernels, attention(): pl.pallas_call(functools.partial(attention_kernel, orders, fsdp, small),...  30.5 us
    pallas_call x1, Pallas kernels, feed_forward(): pl.pallas_call(feed_forward_kernel, grid=(rows // TILE,), in_specs=[pl.Bl...  27.6 us
    ppermute x22, starting transfers between devices, swap(): return lax.ppermute(block, axis, [(i, i ^ mask) for i in range(size)])  27.3 us
    pallas_call x1, Pallas kernels, feed_forward_grad(): pl.pallas_call(feed_forward_grad_kernel, grid=(rows // TILE,), in_specs=[...  25.8 us
    pallas_call x1, Pallas kernels, attention_grad(): pl.pallas_call(attention_grad_kernel, grid=(rows // PACK, pairs), in_spec...  22.9 us
    pallas_call x1, Pallas kernels, early_grads(): pl.pallas_call(functools.partial(early_kernel, reps), grid=(n,), in_specs...  14.3 us
    all_gather x1, waiting for transfers between devices, shards(): rest_full = lax.all_gather(rest, AXES, axis=0, tiled=True)  11.5 us
  transfers between devices with their start and end apart: 25, of which 12 were waited for; matrix products, arithmetic and copies ran while one was open for 7% of the time, Pallas kernels for 25%

profile of v4, /device:TPU:0, one launch (start us, length us, event | category | flops | bytes accessed | tf_op | source)
XLA Modules:
  0.0 319.1 jit_solution(4564710325805299220)
XLA Ops:
  7.2 2.1 reshape.111
  12.1 3.1 collective-permute-start
  15.2 2.6 collective-permute-start.1
  17.9 10.3 %collective-permute-done.2 = bf16[24,3200]{1,0:T(8,128)(2,1)S(1)} collective-permute-done((bf16[24,3200]{1,0:T(8,128)(2,1)S(1)}, bf16[24,3200]{1,0:T(8,128)(2,1)S(1)}, u32[]{:S(2)}, u32[]{:S(2)}) %collective-permute-start.2) | collective-permute-done | bytes 153632 | tf_op jit(solution)/shard_map/ppermute | solution.py:13
  28.2 4.4 %collective-permute-done.1 = bf16[24,3200]{1,0:T(8,128)(2,1)S(1)} collective-permute-done((bf16[24,3200]{1,0:T(8,128)(2,1)S(1)}, bf16[24,3200]{1,0:T(8,128)(2,1)S(1)}, u32[]{:S(2)}, u32[]{:S(2)}) %collective-permute-start.1) | collective-permute-done | bytes 153632 | tf_op jit(solution)/shard_map/ppermute | solution.py:13
  34.3 1.6 collective-permute-start.3
  36.0 5.9 %collective-permute-done.6 = bf16[4,24,1664]{2,1,0:T(8,128)(2,1)S(1)} collective-permute-done((bf16[4,24,1664]{2,1,0:T(8,128)(2,1)S(1)}, bf16[4,24,1664]{2,1,0:T(8,128)(2,1)S(1)}, u32[]{:S(2)}, u32[]{:S(2)}) %collective-permute-start.6) | collective-permute-done | bytes 319520 | tf_op jit(solution)/shard_map/ppermute | solution.py:13
  41.9 1.9 collective-permute-start.7
  44.3 1.8 collective-permute-start.4
  46.2 11.1 %collective-permute-done.7 = bf16[8,24,1664]{2,1,0:T(8,128)(2,1)S(1)} collective-permute-done((bf16[8,24,1664]{2,1,0:T(8,128)(2,1)S(1)}, bf16[8,24,1664]{2,1,0:T(8,128)(2,1)S(1)}, u32[]{:S(2)}, u32[]{:S(2)}) %collective-permute-start.7) | collective-permute-done | bytes 639008 | tf_op jit(solution)/shard_map/ppermute | solution.py:13
  57.5 3.5 %collective-permute-done.4 = bf16[8,24,1536]{2,1,0:T(8,128)(2,1)S(1)} collective-permute-done((bf16[8,24,1536]{2,1,0:T(8,128)(2,1)S(1)}, bf16[8,24,1536]{2,1,0:T(8,128)(2,1)S(1)}, u32[]{:S(2)}, u32[]{:S(2)}) %collective-permute-start.4) | collective-permute-done | bytes 589856 | tf_op jit(solution)/shard_map/ppermute | solution.py:13
  61.8 2.2 collective-permute-done.5.p1
  64.1 30.5 %attention.1 = (bf16[768,3200]{1,0:T(8,128)(2,1)}, f32[16,768]{1,0:T(8,128)}, bf16[1024,2304]{1,0:T(8,128)(2,1)}, bf16[1024,768]{1,0:T(8,128)(2,1)}, f32[1024,12...) custom-call(s32[2,4]{1,0:T(2,128)} %lens_ref.5, ...), custom_call_target="tpu_custom_call" | custom-call | flops 6845104128 | bytes 9437184 | tf_op jit(solution)/shard_map/attention/pallas_call | solution.py:254
  94.5 11.5 %all-gather.2.cloned.1.call-done.w_ref = bf16[768,6272]{1,0:T(8,128)(2,1)} async-done(((bf16[24,6272]{1,0:T(8,128)(2,1)}), bf16[768,6272]{1,0:T(8,128)(2,1)}) %all-gather.2.cloned.1.call-update) | async-done | bytes 9633808 | tf_op jit(solution)/shard_map/all_gather | solution.py:608
  106.0 27.6 %feed_forward.1 = (bf16[1024,3072]{1,0:T(8,128)(2,1)}, bf16[1024,3072]{1,0:T(8,128)(2,1)}, f32[1024,768]{1,0:T(8,128)}, f32[1024,128]{1,0:T(8,128)}, bf16[1024,7...) custom-call(s32[2,4]{1,0:T(2,128)} %lens_ref.5, ...), custom_call_target="tpu_custom_call" | custom-call | tf_op jit(solution)/shard_map/feed_forward/pallas_call | solution.py:368
  134.3 10.3 %all_to_all.10 = f32[32,2,128]{2,1,0:T(2,128)S(1)} all-to-all(f32[32,2,128]{2,1,0:T(2,128)S(1)} %broadcast_in_dim.25), channel_id=1, replica_groups=mesh['dp'=8,'fsdp'=4] {'dp','fsdp'}, dimensions={0} | all-to-all | bytes 65536 | tf_op jit(solution)/shard_map/all_to_all | solution.py:550
  145.2 25.8 %feed_forward_grad.1 = (bf16[1024,4608]{1,0:T(8,128)(2,1)}, f32[1024,768]{1,0:T(8,128)}, bf16[1024,768]{1,0:T(8,128)(2,1)}, f32[16,768]{1,0:T(8,128)}, bf16[768,128]{1,0:T(8,128)(2,1)}) custom-call(s32[2,4]{1,0:T(2,128)} %lens_ref.5, s32[8]{0:T(128)} %bitcast.128, f32[1,128]{1,0:T(1,128)} %get-tuple-element.89.doc_ref, f32[32,128]{1,0:T(8,128)} %bitcast.121, ...), custom_call_target="tpu_custom_call" | custom-call | tf_op jit(solution)/shard_map/feed_forward_grad/pallas_call | solution.py:433
  171.1 14.3 %early_weight_grads.1 = (bf16[4,96,4608]{2,1,0:T(8,128)(2,1)}, bf16[4,96,4608]{2,1,0:T(8,128)(2,1)}) custom-call(s32[2]{0:T(128)} %pad_add_fusion.me_ref, bf16[1024,768]{1,0:T(8,128)(2,1)} %get-tuple-element.87.low_ref.low_hbm, bf16[1024,3072]{1,0:T(8,128)(2,1)} %get-tuple-element.104.act_hbm.act_ref, bf16[1024,768]{1,0:T(8,128)(2,1)} %get-tuple-element.101.ctx_hbm.ctx_ref, ...), custom_call_target="tpu_custom_call" | custom-call | flops 7247757312 | bytes 18874368 | tf_op jit(solution)/shard_map/early_weight_grads/pallas_call | solution.py:475
  185.4 8.1 %outer_weight_grad.1 = (bf16[4,96,2304]{2,1,0:T(8,128)(2,1)}, bf16[4,96,2304]{2,1,0:T(8,128)(2,1)}) custom-call(s32[2]{0:T(128)} %pad_add_fusion.me_ref, bf16[1024,3072]{1,0:T(8,128)(2,1)} %get-tuple-element.104.act_hbm.act_ref, bf16[1024,4608]{1,0:T(8,128)(2,1)} %get-tuple-element.108.right_ref.olow_ref), custom_call_target="tpu_custom_call" | custom-call | flops 3623878656 | bytes 9437184 | tf_op jit(solution)/shard_map/outer_weight_grad/pallas_call | solution.py:487
  193.5 4.6 %add_convert_fusion = bf16[4,96,4608]{2,1,0:T(8,128)(2,1)} fusion(bf16[4,96,4608]{2,1,0:T(8,128)(2,1)} %collective-permute-done.9, bf16[4,96,4608]{2,1,0:T(8,128)(2,1)S(1)} %copy-done), kind=kLoop, calls=%fused_computation | loop fusion | flops 7077888 | bytes 10616832 | tf_op jit(solution)/shard_map/convert_element_type | solution.py:65
  200.0 22.9 %attention_grad.1.mg_ref.refs_0_ = bf16[1024,2304]{1,0:T(8,128)(2,1)} custom-call(bf16[1024,2304]{1,0:T(8,128)(2,1)} %get-tuple-element.100.q_ref.k_ref.v_ref, bf16[1024,2304]{1,0:T(8,128)(2,1)} %get-tuple-element.100.q_ref.k_ref.v_ref, bf16[1024,2304]{1,0:T(8,128)(2,1)} %get-tuple-element.100.q_ref.k_ref.v_ref, ...), custom_call_target="tpu_custom_call" | custom-call | flops 6442450944 | bytes 18874368 | tf_op jit(solution)/shard_map/attention_grad/pallas_call | solution.py:299
  222.9 9.3 %late_weight_grads.1 = (bf16[4,96,2432]{2,1,0:T(8,128)(2,1)}, bf16[4,96,2432]{2,1,0:T(8,128)(2,1)}, f32[8,2304]{1,0:T(8,128)}) custom-call(s32[2]{0:T(128)} %pad_add_fusion.me_ref, bf16[1024,768]{1,0:T(8,128)(2,1)} %tok_ref.3, bf16[1024,2304]{1,0:T(8,128)(2,1)} %attention_grad.1.mg_ref.refs_0_, bf16[768,128]{1,0:T(8,128)(2,1)} %get-tuple-element.116.span_ref), custom_call_target="tpu_custom_call" | custom-call | flops 3623878656 | bytes 9437184 | tf_op jit(solution)/shard_map/late_weight_grads/pallas_call | solution.py:507
  235.0 2.4 add_convert_fusion.2
  242.0 2.1 dynamic-slice_bitcast_fusion.4
  245.6 4.1 %collective-permute-start.13 = (bf16[24,4608]{1,0:T(8,128)(2,1)}, bf16[24,4608]{1,0:T(8,128)(2,1)S(1)}, u32[]{:S(2)}, u32[]{:S(2)}) collective-permute-start(bf16[24,4608]{1,0:T(8,128)(2,1)} %get-tuple-element.159), channel_id=1, source_target_pairs={{0,2},{1,3},{2,0},{3,1},{4,6},{5,7},{6,4},{7,5},{8,10},{9,11},{10,... | collective-permute-start | bytes 663560 | tf_op jit(solution)/shard_map/ppermute | solution.py:13
  249.6 8.8 %input_grad.1 = f32[1024,768]{1,0:T(8,128)} custom-call(bf16[768,3200]{1,0:T(8,128)(2,1)} %get-tuple-element.97.aw_ref.w_ref, f32[1024,768]{1,0:T(8,128)} %get-tuple-element.129.fs_ref, bf16[1024,2304]{1,0:T(8,128)(2,1)} %attention_grad.1.mg_ref.refs_0_), custom_call_target="tpu_custom_call" | custom-call | flops 3623878656 | bytes 12582912 | tf_op jit(solution)/shard_map/input_grad/pallas_call | solution.py:528
  258.5 6.2 %all-to-all-start.1 = ((f32[32,4,128]{2,1,0:T(4,128)}), f32[32,4,128]{2,1,0:T(4,128)S(1)}, u32[]{:S(2)}, u32[]{:S(2)}) async-start(f32[32,4,128]{2,1,0:T(4,128)} %reshape.116), calls=%async_computation.2 | async-start | bytes 131072 | tf_op jit(solution)/shard_map/all_to_all | solution.py:694
  268.2 1.8 collective-permute-start.17
  273.7 9.7 %collective-permute-done.18 = bf16[1,96,2304]{2,1,0:T(8,128)(2,1)S(1)} collective-permute-done((bf16[1,96,2304]{2,1,0:T(8,128)(2,1)S(1)}, bf16[1,96,2304]{2,1,0:T(8,128)(2,1)S(1)}, u32[]{:S(2)}, u32[]{:S(2)}) %collective-permute-start.18) | collective-permute-done | bytes 442400 | tf_op jit(solution)/shard_map/ppermute | solution.py:13
  288.2 3.3 %collective-permute-start.21 = (bf16[24,4736]{1,0:T(8,128)(2,1)}, bf16[24,4736]{1,0:T(8,128)(2,1)}, u32[]{:S(2)}, u32[]{:S(2)}) collective-permute-start(bf16[24,4736]{1,0:T(8,128)(2,1)} %pad_maximum_fusion.6), channel_id=1, source_target_pairs={{0,3},{1,2},{2,1},{3,0},{4,7},{5,6},{6,5},{7,4},{8,11},{9,10},{10,... | collective-permute-start | bytes 681992 | tf_op jit(solution)/shard_map/ppermute | solution.py:13
  296.4 2.6 reshape.124
  300.5 8.4 %collective-permute-done.20 = bf16[24,4736]{1,0:T(8,128)(2,1)} collective-permute-done((bf16[24,4736]{1,0:T(8,128)(2,1)}, bf16[24,4736]{1,0:T(8,128)(2,1)}, u32[]{:S(2)}, u32[]{:S(2)}) %collective-permute-start.20) | collective-permute-done | bytes 227360 | tf_op jit(solution)/shard_map/ppermute | solution.py:13
  (181 shorter events, 39.5 us)
Async XLA Ops:
  7.2 98.8 %all-gather.2.cloned.1.call-start = ((), (), s32[]{:S(2)}) async-start(), calls=%async_computation.3 | async-start | bytes 9934848 | tf_op jit(solution)/shard_map/all_gather | solution.py:608
  11.8 230.1 %reduce-scatter.2.cloned.1.call-start = ((), (), s32[]{:S(2)}) async-start(), calls=%async_computation.4 | async-start | bytes 4423680 | tf_op jit(solution)/shard_map/reduce_scatter | solution.py:658
  12.1 20.4 %collective-permute-start = (bf16[24,3200]{1,0:T(8,128)(2,1)S(1)}, bf16[24,3200]{1,0:T(8,128)(2,1)S(1)}, u32[]{:S(2)}, u32[]{:S(2)}) collective-permute-start(bf16[24,3200]{1,0:T(8,128)(2,1)S(1)} %fusion.1), channel_id=1, source_target_pairs={{0,1},{1,0},{2,3},{3,2},{4,5},{5,4},{6,7},{7,6},{8,9},{9,8},{10,11... | collective-permute-start | bytes 460808 | tf_op jit(solution)/shard_map/ppermute | solution.py:13
  15.2 17.3 %collective-permute-start.1 = (bf16[24,3200]{1,0:T(8,128)(2,1)S(1)}, bf16[24,3200]{1,0:T(8,128)(2,1)S(1)}, u32[]{:S(2)}, u32[]{:S(2)}) collective-permute-start(bf16[24,3200]{1,0:T(8,128)(2,1)S(1)} %fusion.1), channel_id=1, source_target_pairs={{0,2},{1,3},{2,0},{3,1},{4,6},{5,7},{6,4},{7,5},{8,10},{9,11},{10,... | collective-permute-start | bytes 460808 | tf_op jit(solution)/shard_map/ppermute | solution.py:13
  17.8 10.4 %collective-permute-start.2 = (bf16[24,3200]{1,0:T(8,128)(2,1)S(1)}, bf16[24,3200]{1,0:T(8,128)(2,1)S(1)}, u32[]{:S(2)}, u32[]{:S(2)}) collective-permute-start(bf16[24,3200]{1,0:T(8,128)(2,1)S(1)} %fusion.1), channel_id=1, source_target_pairs={{0,3},{1,2},{2,1},{3,0},{4,7},{5,6},{6,5},{7,4},{8,11},{9,10},{10,... | collective-permute-start | bytes 460808 | tf_op jit(solution)/shard_map/ppermute | solution.py:13
  32.6 9.2 %collective-permute-start.6 = (bf16[4,24,1664]{2,1,0:T(8,128)(2,1)S(1)}, bf16[4,24,1664]{2,1,0:T(8,128)(2,1)S(1)}, u32[]{:S(2)}, u32[]{:S(2)}) collective-permute-start(bf16[4,24,1664]{2,1,0:T(8,128)(2,1)S(1)} %pad_maximum_fusion), channel_id=1, source_target_pairs={{0,8},{4,12},{8,0},{12,4},{16,24},{20,28},{24,16},{28,20},{1,9},{5... | collective-permute-start | bytes 958472 | tf_op jit(solution)/shard_map/ppermute | solution.py:13
  34.3 10.0 %collective-permute-start.3 = (bf16[4,24,1536]{2,1,0:T(8,128)(2,1)S(1)}, bf16[4,24,1536]{2,1,0:T(8,128)(2,1)S(1)}, u32[]{:S(2)}, u32[]{:S(2)}) collective-permute-start(bf16[4,24,1536]{2,1,0:T(8,128)(2,1)S(1)} %pad_maximum_fusion.1), channel_id=1, source_target_pairs={{0,16},{4,20},{8,24},{12,28},{16,0},{20,4},{24,8},{28,12},{1,17},{... | collective-permute-start | bytes 884744 | tf_op jit(solution)/shard_map/ppermute | solution.py:13
  41.9 15.4 %collective-permute-start.7 = (bf16[8,24,1664]{2,1,0:T(8,128)(2,1)S(1)}, bf16[8,24,1664]{2,1,0:T(8,128)(2,1)S(1)}, u32[]{:S(2)}, u32[]{:S(2)}) collective-permute-start(bf16[8,24,1664]{2,1,0:T(8,128)(2,1)S(1)} %get-tuple-element.175), channel_id=1, source_target_pairs={{0,16},{4,20},{8,24},{12,28},{16,0},{20,4},{24,8},{28,12},{1,17},{... | collective-permute-start | bytes 1916936 | tf_op jit(solution)/shard_map/ppermute | solution.py:13
  43.9 18.0 %copy-start.29 = (s32[8,1]{0,1:T(1,128)S(1)}, s32[8,1]{0,1:T(1,128)}, u32[]{:S(2)}) copy-start(s32[8,1]{0,1:T(1,128)} %param.22) | copy-start | bytes 100
  44.3 16.6 %collective-permute-start.4 = (bf16[8,24,1536]{2,1,0:T(8,128)(2,1)S(1)}, bf16[8,24,1536]{2,1,0:T(8,128)(2,1)S(1)}, u32[]{:S(2)}, u32[]{:S(2)}) collective-permute-start(bf16[8,24,1536]{2,1,0:T(8,128)(2,1)S(1)} %get-tuple-element.177), channel_id=1, source_target_pairs={{0,8},{4,12},{8,0},{12,4},{16,24},{20,28},{24,16},{28,20},{1,9},{5... | collective-permute-start | bytes 1769480 | tf_op jit(solution)/shard_map/ppermute | solution.py:13
  57.4 6.7 %collective-permute-start.8 = (bf16[16,24,1664]{2,1,0:T(8,128)(2,1)S(1)}, bf16[16,24,1664]{2,1,0:T(8,128)(2,1)}, u32[]{:S(2)}, u32[]{:S(2)}) collective-permute-start(bf16[16,24,1664]{2,1,0:T(8,128)(2,1)S(1)} %constant_dynamic-update-slice_fusion.16.p2), channel_id=1, source_target_pairs={{0,4},{4,0},{8,12},{12,8},{16,20},{20,16},{24,28},{28,24},{1,5},{5... | collective-permute-start | bytes 3833864 | tf_op jit(solution)/shard_map/ppermute | solution.py:13
  61.0 3.0 collective-permute-start.5
  185.3 8.1 %collective-permute-start.9 = (bf16[4,96,4608]{2,1,0:T(8,128)(2,1)}, bf16[4,96,4608]{2,1,0:T(8,128)(2,1)}, u32[]{:S(2)}, u32[]{:S(2)}) collective-permute-start(bf16[4,96,4608]{2,1,0:T(8,128)(2,1)} %get-tuple-element.107), channel_id=1, source_target_pairs={{0,4},{4,0},{8,12},{12,8},{16,20},{20,16},{24,28},{28,24},{1,5},{5... | collective-permute-start | bytes 10616840 | tf_op jit(solution)/shard_map/ppermute | solution.py:13
  185.4 8.1 %copy-start = (bf16[4,96,4608]{2,1,0:T(8,128)(2,1)S(1)}, bf16[4,96,4608]{2,1,0:T(8,128)(2,1)}, u32[]{:S(2)}) copy-start(bf16[4,96,4608]{2,1,0:T(8,128)(2,1)} %get-tuple-element.106) | copy-start | bytes 10616836
  199.5 23.4 %collective-permute-start.10 = (bf16[4,96,2304]{2,1,0:T(8,128)(2,1)S(1)}, bf16[4,96,2304]{2,1,0:T(8,128)(2,1)S(1)}, u32[]{:S(2)}, u32[]{:S(2)}) collective-permute-start(bf16[4,96,2304]{2,1,0:T(8,128)(2,1)S(1)} %copy-done.30), channel_id=1, source_target_pairs={{0,4},{4,0},{8,12},{12,8},{16,20},{20,16},{24,28},{28,24},{1,5},{5... | collective-permute-start | bytes 5308424 | tf_op jit(solution)/shard_map/ppermute | solution.py:13
  222.9 9.3 %copy-start.3 = (bf16[4,96,2304]{2,1,0:T(8,128)(2,1)}, bf16[4,96,2304]{2,1,0:T(8,128)(2,1)S(1)}, u32[]{:S(2)}) copy-start(bf16[4,96,2304]{2,1,0:T(8,128)(2,1)S(1)} %collective-permute-done.10) | copy-start | bytes 5308420
  222.9 9.5 %copy-start.14 = (f32[16,768]{1,0:T(8,128)S(1)}, f32[16,768]{1,0:T(8,128)}, u32[]{:S(2)}) copy-start(f32[16,768]{1,0:T(8,128)} %get-tuple-element.99) | copy-start | bytes 147460
  222.9 10.1 %copy-start.12 = (f32[32,1,128]{2,1,0:T(1,128)S(1)}, f32[32,1,128]{2,1,0:T(1,128)}, u32[]{:S(2)}) copy-start(f32[32,1,128]{2,1,0:T(1,128)} %get-tuple-element.195) | copy-start | bytes 49156
  232.2 6.6 %collective-permute-start.11 = (bf16[4,96,2432]{2,1,0:T(8,128)(2,1)}, bf16[4,96,2432]{2,1,0:T(8,128)(2,1)S(1)}, u32[]{:S(2)}, u32[]{:S(2)}) collective-permute-start(bf16[4,96,2432]{2,1,0:T(8,128)(2,1)} %get-tuple-element.121), channel_id=1, source_target_pairs={{0,4},{4,0},{8,12},{12,8},{16,20},{20,16},{24,28},{28,24},{1,5},{5... | collective-permute-start | bytes 5603336 | tf_op jit(solution)/shard_map/ppermute | solution.py:13
  238.5 26.4 %collective-permute-start.16 = (bf16[2,96,2304]{2,1,0:T(8,128)(2,1)}, bf16[2,96,2304]{2,1,0:T(8,128)(2,1)}, u32[]{:S(2)}, u32[]{:S(2)}) collective-permute-start(bf16[2,96,2304]{2,1,0:T(8,128)(2,1)} %get-tuple-element.157), channel_id=1, source_target_pairs={{0,16},{4,20},{8,24},{12,28},{16,0},{20,4},{24,8},{28,12},{1,17},{... | collective-permute-start | bytes 2654216 | tf_op jit(solution)/shard_map/ppermute | solution.py:13
  240.9 23.9 %collective-permute-start.15 = (bf16[2,96,2432]{2,1,0:T(8,128)(2,1)}, bf16[2,96,2432]{2,1,0:T(8,128)(2,1)S(1)}, u32[]{:S(2)}, u32[]{:S(2)}) collective-permute-start(bf16[2,96,2432]{2,1,0:T(8,128)(2,1)} %get-tuple-element.154), channel_id=1, source_target_pairs={{0,8},{4,12},{8,0},{12,4},{16,24},{20,28},{24,16},{28,20},{1,9},{5... | collective-permute-start | bytes 2801672 | tf_op jit(solution)/shard_map/ppermute | solution.py:13
  244.1 20.8 %collective-permute-start.12 = (bf16[24,4608]{1,0:T(8,128)(2,1)}, bf16[24,4608]{1,0:T(8,128)(2,1)S(1)}, u32[]{:S(2)}, u32[]{:S(2)}) collective-permute-start(bf16[24,4608]{1,0:T(8,128)(2,1)} %get-tuple-element.160), channel_id=1, source_target_pairs={{0,1},{1,0},{2,3},{3,2},{4,5},{5,4},{6,7},{7,6},{8,9},{9,8},{10,11... | collective-permute-start | bytes 663560 | tf_op jit(solution)/shard_map/ppermute | solution.py:13
  245.6 20.1 %collective-permute-start.13 = (bf16[24,4608]{1,0:T(8,128)(2,1)}, bf16[24,4608]{1,0:T(8,128)(2,1)S(1)}, u32[]{:S(2)}, u32[]{:S(2)}) collective-permute-start(bf16[24,4608]{1,0:T(8,128)(2,1)} %get-tuple-element.159), channel_id=1, source_target_pairs={{0,2},{1,3},{2,0},{3,1},{4,6},{5,7},{6,4},{7,5},{8,10},{9,11},{10,... | collective-permute-start | bytes 663560 | tf_op jit(solution)/shard_map/ppermute | solution.py:13
  249.6 15.0 %copy-start.11 = (f32[32,1,128]{2,1,0:T(1,128)S(1)}, f32[32,1,128]{2,1,0:T(1,128)}, u32[]{:S(2)}) copy-start(f32[32,1,128]{2,1,0:T(1,128)} %get-tuple-element.196) | copy-start | bytes 49156
  249.6 16.2 %collective-permute-start.14 = (bf16[24,4608]{1,0:T(8,128)(2,1)}, bf16[24,4608]{1,0:T(8,128)(2,1)}, u32[]{:S(2)}, u32[]{:S(2)}) collective-permute-start(bf16[24,4608]{1,0:T(8,128)(2,1)} %get-tuple-element.158), channel_id=1, source_target_pairs={{0,3},{1,2},{2,1},{3,0},{4,7},{5,6},{6,5},{7,4},{8,11},{9,10},{10,... | collective-permute-start | bytes 663560 | tf_op jit(solution)/shard_map/ppermute | solution.py:13
  258.5 15.3 %all-to-all-start.1 = ((f32[32,4,128]{2,1,0:T(4,128)}), f32[32,4,128]{2,1,0:T(4,128)S(1)}, u32[]{:S(2)}, u32[]{:S(2)}) async-start(f32[32,4,128]{2,1,0:T(4,128)} %reshape.116), calls=%async_computation.2 | async-start | bytes 131072 | tf_op jit(solution)/shard_map/all_to_all | solution.py:694
  268.2 15.2 %collective-permute-start.17 = (bf16[1,96,2432]{2,1,0:T(8,128)(2,1)}, bf16[1,96,2432]{2,1,0:T(8,128)(2,1)S(1)}, u32[]{:S(2)}, u32[]{:S(2)}) collective-permute-start(bf16[1,96,2432]{2,1,0:T(8,128)(2,1)} %constant_dynamic-slice_fusion.1), channel_id=1, source_target_pairs={{0,16},{4,20},{8,24},{12,28},{16,0},{20,4},{24,8},{28,12},{1,17},{... | collective-permute-start | bytes 1400840 | tf_op jit(solution)/shard_map/ppermute | solution.py:13
  271.4 12.0 %collective-permute-start.18 = (bf16[1,96,2304]{2,1,0:T(8,128)(2,1)S(1)}, bf16[1,96,2304]{2,1,0:T(8,128)(2,1)S(1)}, u32[]{:S(2)}, u32[]{:S(2)}) collective-permute-start(bf16[1,96,2304]{2,1,0:T(8,128)(2,1)S(1)} %constant_dynamic-slice_fusion), channel_id=1, source_target_pairs={{0,8},{4,12},{8,0},{12,4},{16,24},{20,28},{24,16},{28,20},{1,9},{5... | collective-permute-start | bytes 1327112 | tf_op jit(solution)/shard_map/ppermute | solution.py:13
  285.6 8.3 %copy-start.2 = (f32[24,4608]{1,0:T(8,128)}, f32[24,4608]{1,0:T(8,128)S(1)}, u32[]{:S(2)}) copy-start(f32[24,4608]{1,0:T(8,128)S(1)} %convert_add_fusion.1) | copy-start | bytes 1327108
  288.2 12.3 %collective-permute-start.21 = (bf16[24,4736]{1,0:T(8,128)(2,1)}, bf16[24,4736]{1,0:T(8,128)(2,1)}, u32[]{:S(2)}, u32[]{:S(2)}) collective-permute-start(bf16[24,4736]{1,0:T(8,128)(2,1)} %pad_maximum_fusion.6), channel_id=1, source_target_pairs={{0,3},{1,2},{2,1},{3,0},{4,7},{5,6},{6,5},{7,4},{8,11},{9,10},{10,... | collective-permute-start | bytes 681992 | tf_op jit(solution)/shard_map/ppermute | solution.py:13
  292.2 16.7 %collective-permute-start.20 = (bf16[24,4736]{1,0:T(8,128)(2,1)}, bf16[24,4736]{1,0:T(8,128)(2,1)}, u32[]{:S(2)}, u32[]{:S(2)}) collective-permute-start(bf16[24,4736]{1,0:T(8,128)(2,1)} %pad_maximum_fusion.5), channel_id=1, source_target_pairs={{0,2},{1,3},{2,0},{3,1},{4,6},{5,7},{6,4},{7,5},{8,10},{9,11},{10,... | collective-permute-start | bytes 681992 | tf_op jit(solution)/shard_map/ppermute | solution.py:13
  292.9 16.0 %collective-permute-start.19 = (bf16[24,4736]{1,0:T(8,128)(2,1)}, bf16[24,4736]{1,0:T(8,128)(2,1)}, u32[]{:S(2)}, u32[]{:S(2)}) collective-permute-start(bf16[24,4736]{1,0:T(8,128)(2,1)} %pad_maximum_fusion.4), channel_id=1, source_target_pairs={{0,1},{1,0},{2,3},{3,2},{4,5},{5,4},{6,7},{7,6},{8,9},{9,8},{10,11... | collective-permute-start | bytes 681992 | tf_op jit(solution)/shard_map/ppermute | solution.py:13
  (24 other events, 55.9 us)
Sparse Core Ops, SparseCore 0:
  11.9 94.0 all-gather.1
  198.2 43.7 reduce-scatter.1
